TPU v7x, 256 devices: a whole 4x4x8 slice. The times are simulated.
256 devices in a mesh: ctx: 64 (over y, z_hi, x, core), fsdp: 4 (over z_lo).
Axes of the slice: x: 4, y: 4, z: 8 (z_hi: 2, z_lo: 4; z = z_hi * 4 + z_lo), core: 2. Of those that a mesh axis runs over, the one named last changes fastest.
Arguments:
- tokens: bfloat16 [4, 16384, 2048], P('fsdp', 'ctx'), may hold values from -6 to 6
- qkv_weight: bfloat16 [3, 2048, 2048], P(None, None, 'fsdp'), may hold values from -0.125 to 0.125
- log_decay: float32 [4, 16, 16384], P('fsdp', None, 'ctx'), may hold values from -3 to 0
- norm_gain: float32 [2048], replicated, may hold values from 0.25 to 1.75
Outputs:
- normed: bfloat16 [4, 16384, 2048], P('fsdp', 'ctx')
All inputs are finite; a program needn't handle non-finite values.
Results may differ from a plain program's by a relative error of at most 0.009.
Values may be sent and summed in bfloat16 or wider, within the bound.
No kernel may reach another device: no remote copies, remote signals or barrier semaphores. Data moves between devices by JAX's collectives and lax.ppermute only.
A program may use at most 192 MiB of HBM per device.

v0:
```python
import jax
import jax.numpy as jnp
from jax import lax
from jax.sharding import PartitionSpec as P


def entering(part, axis, combine, identity):
    place = lax.axis_index(axis)
    gathered = jax.tree.map(lambda a: lax.all_gather(a, axis), part)
    state = jax.tree.map(lambda a, e: jnp.zeros_like(a) + jnp.asarray(e, a.dtype), part, identity)

    def one(turn, state):
        return combine(
            state, jax.tree.map(lambda a: lax.dynamic_index_in_dim(a, turn, 0, False), gathered)
        )

    return lax.fori_loop(0, place, one, state)


def chain_states(decay_total, local):

    def combine(earlier, later):
        return (earlier[0] * later[0], later[0][:, None, None] * earlier[1] + later[1])

    identity_pair = (jnp.ones_like(decay_total), jnp.zeros_like(local))
    return entering((decay_total, local), "ctx", combine, identity_pair)[1]


def segment_memory_matrix(keys, values, cumulative):
    tail = jnp.exp(cumulative[:, -1:] - cumulative)
    weighted_key_vectors = (keys.astype(jnp.float32) * tail.T[:, :, None]).astype(jnp.bfloat16)
    local = jnp.einsum(
        "thd,the->hde", weighted_key_vectors, values, preferred_element_type=jnp.float32
    )
    return (jnp.exp(cumulative[:, -1]), local)


def body(tokens, qkv_weight, log_decay, norm_gain):
    inputs = tokens[0]
    log_rates = log_decay[0]
    head_count = log_rates.shape[0]
    span_len = log_rates.shape[1]
    feat_total = norm_gain.shape[0]
    head_dimension = feat_total // head_count
    cumulative = jnp.cumsum(log_rates, axis=1)
    merged_channel_vectors = jnp.einsum(
        "td,cde->cte",
        inputs,
        lax.all_gather(qkv_weight, "fsdp", axis=2, tiled=True),
        preferred_element_type=jnp.float32,
    )
    queries = (
        jax.nn.silu(merged_channel_vectors[0])
        .astype(jnp.bfloat16)
        .reshape(span_len, head_count, head_dimension)
    )
    keys = (
        jax.nn.silu(merged_channel_vectors[1])
        .astype(jnp.bfloat16)
        .reshape(span_len, head_count, head_dimension)
    )
    values = (
        merged_channel_vectors[2].astype(jnp.bfloat16).reshape(span_len, head_count, head_dimension)
    )
    decay_total, local = segment_memory_matrix(keys, values, cumulative)
    carried = chain_states(decay_total, local)
    log_gaps = cumulative[:, :, None] - cumulative[:, None, :]
    causal = jnp.arange(span_len)[:, None] >= jnp.arange(span_len)[None, :]
    factors = jnp.exp(jnp.where(causal[None], log_gaps, -jnp.inf))
    scores = jnp.einsum("thd,shd->hts", queries, keys, preferred_element_type=jnp.float32)
    weights = (scores * factors).astype(jnp.bfloat16)
    inside = jnp.einsum("hts,shd->thd", weights, values, preferred_element_type=jnp.float32)
    reduced_precision_memory = carried.astype(jnp.bfloat16)
    incoming = jnp.einsum(
        "thd,hde->the", queries, reduced_precision_memory, preferred_element_type=jnp.float32
    )
    incoming = incoming * jnp.exp(cumulative).T[:, :, None]
    attention_output = (inside + incoming).reshape(span_len, feat_total)
    mean_sq = jnp.mean(attention_output * attention_output, axis=-1, keepdims=True)
    normed = (attention_output * lax.rsqrt(mean_sq + 1e-05) * norm_gain).astype(jnp.bfloat16)
    return normed[None]


def solution(mesh):
    placed = (P("fsdp", "ctx", None), P(None, None, "fsdp"), P("fsdp", None, "ctx"), P())
    return jax.shard_map(
        body, mesh=mesh, in_specs=placed, out_specs=P("fsdp", "ctx", None), check_vma=False
    )
```

profile of v0, /device:TPU:159, one launch (start us, length us, event | category | flops | bytes accessed | tf_op | source)
XLA Modules:
  0.0 1003.1 jit_solution(10331427790303788034)
XLA Ops:
  6.5 8.9 copy.41
  17.4 426.3 %all-gather.5.cloned.1.call-done = bf16[3,2048,2048]{1,2,0:T(8,128)(2,1)} async-done(((bf16[3,2048,512]{1,2,0:T(8,128)(2,1)}), bf16[3,2048,2048]{1,2,0:T(8,128)(2,1)}) %all-gather.5.cloned.1.call-update) | async-done | bytes 25165840 | tf_op jit(solution)/shard_map/all_gather | solution.py:49
  443.7 12.0 %convolution_bitcast_fusion = f32[3,256,2048]{1,2,0:T(8,128)S(1)} fusion(bf16[3,2048,2048]{1,2,0:T(8,128)(2,1)} %all-gather.5.cloned.1.call-done, bf16[1,256,2048]{2,1,0:T(8,128)(2,1)S(1)} %copy-done), kind=kOutput, calls=%fused_computation.3 | convolution fusion | flops 6442450944 | bytes 32505856 | tf_op jit(solution)/shard_map/td,cde->cte/dot_general | solution.py:46
  456.8 1.6 fusion.7
  458.4 2.9 copy.45
  461.3 4.2 fusion.2
  467.0 225.2 %all-reduce = f32[1024]{0:T(1024)S(1)} all-reduce(f32[1024]{0:T(1024)S(1)} %dynamic-update-slice), channel_id=2, replica_groups=mesh['ctx'=64,'fsdp'=4] {'ctx'}, use_global_device_ids=true, to_apply=%add | all-reduce | flops 1024 | bytes 8192
  692.3 1.9 copy.43
  694.2 6.2 fusion.1
  700.4 194.0 %all-gather.7.cloned.1.call-done = f32[1024,128,128]{2,1,0:T(8,128)} async-done(((f32[16,128,128]{2,1,0:T(8,128)}), f32[1024,128,128]{2,1,0:T(8,128)}) %all-gather.7.cloned.1.call-update) | async-done | bytes 67108880 | tf_op jit(solution)/shard_map/all_gather | solution.py:9
  894.6 94.1 %while.12 = (s32[]{:T(128)}, f32[16,128,128]{2,1,0:T(8,128)S(1)}, s32[]{:T(128)}, f32[64,16]{1,0:T(8,128)S(1)}, f32[64,16,128,128]{3,2,1,0:T(8,128)}, /*index=5*/s32[]{:T(128)}, s32[]{:T(128)}, s32[]{:T(128)}) while((s32[]{:T(128)}, f32[16,128,128]{2,1,0:T(8,128)S(1)}, s32[]{:T(128)}, f32[64,16]{1,0:T(8,128)S(1)}, ...), condition=%wide.region_3.4_spmd, body=%wide.region_2.3_spmd.sunk | while | flops 524293 | bytes 3146055 | solution.py:17
  894.6 1.4 bitcast_add_fusion.2
  897.6 1.4 bitcast_add_fusion.2
  900.6 1.4 bitcast_add_fusion.2
  903.6 1.4 bitcast_add_fusion.2
  906.6 1.4 bitcast_add_fusion.2
  909.5 1.4 bitcast_add_fusion.2
  912.5 1.4 bitcast_add_fusion.2
  920.0 1.4 bitcast_add_fusion.2
  923.0 1.4 bitcast_add_fusion.2
  926.0 1.4 bitcast_add_fusion.2
  929.0 1.4 bitcast_add_fusion.2
  932.0 1.4 bitcast_add_fusion.2
  934.9 1.4 bitcast_add_fusion.2
  937.9 1.4 bitcast_add_fusion.2
  940.9 1.4 bitcast_add_fusion.2
  948.4 1.4 bitcast_add_fusion.2
  951.4 1.4 bitcast_add_fusion.2
  954.4 1.4 bitcast_add_fusion.2
  957.4 1.4 bitcast_add_fusion.2
  988.7 4.3 multiply_reduce_fusion
  993.1 1.9 copy.51
  (137 shorter events, 69.6 us)
Async XLA Ops:
  6.5 437.2 %copy-start = (bf16[1,256,2048]{2,1,0:T(8,128)(2,1)S(1)}, bf16[1,256,2048]{2,1,0:T(8,128)(2,1)}, u32[]{:S(2)}) copy-start(bf16[1,256,2048]{2,1,0:T(8,128)(2,1)} %param.6) | copy-start | bytes 3145732
  6.5 437.2 %all-gather.5.cloned.1.call-start = ((), (), s32[]{:S(2)}) async-start(), calls=%async_computation | async-start | bytes 31457280 | tf_op jit(solution)/shard_map/all_gather | solution.py:49
  15.5 0.7 copy-start.1
  15.5 878.9 %all-gather.7.cloned.1.call-start = ((), (), s32[]{:S(2)}) async-start(), calls=%async_computation.1 | async-start | bytes 68157440 | tf_op jit(solution)/shard_map/all_gather | solution.py:9
  461.3 4.2 copy-start.3
  993.1 1.9 copy-start.2
Sparse Core Ops, SparseCore 0:
  15.6 428.0 all-gather.4
  465.7 428.7 all-gather.6
where the time goes:
time: 1010 us; the launch traced here: 1000 us
  waiting for transfers between devices  620 us (61%)
  blocking collectives  225 us (22%)
  other arithmetic  93.2 us (9%)
  matrix products  26.8 us (3%)
  local copies, waits for them, and re-layouts  21.2 us (2%)
  between operations  14.1 us (1%)
    all_gather x1, waiting for transfers between devices, body(): lax.all_gather(qkv_weight, 'fsdp', axis=2, tiled=True)  426 us
    unnamed x1, blocking collectives  225 us
    all_gather x1, waiting for transfers between devices, entering(): gathered = jax.tree.map(lambda a: lax.all_gather(a, axis), part)  194 us
    add x63, other arithmetic, combine(): later[0][:, None, None] * earlier[1] + later[1]  91.2 us
  transfers between devices with their start and end apart: 2, of which 2 were waited for; matrix products, arithmetic and copies ran while one was open for 1% of the time, Pallas kernels for 0%

commit v1 on v0

v1 whole, which is shorter than its diff:
```python
import itertools

import jax
import jax.numpy as jnp
from jax import lax
from jax.experimental import pallas as pl
from jax.experimental.pallas import tpu as pltpu
from jax.sharding import PartitionSpec as P


F32 = jnp.float32
BF16 = jnp.bfloat16
BOTH = ("ctx", "fsdp")
VMEM = pl.BlockSpec(memory_space=pltpu.VMEM)


def pairs(move):
    flat = lambda y, z, x, c: (((y * 2 + z // 4) * 4 + x) * 2 + c) * 4 + z % 4
    every = itertools.product(range(4), range(8), range(4), range(2))
    return [(flat(*at), flat(*move(*at))) for at in every]


def send(a, move):
    return lax.ppermute(a, BOTH, pairs(move))


def up(y, z, x, c):
    return y, (z + 1) % 8, x, c


def down(y, z, x, c):
    return y, (z - 1) % 8, x, c


def two(y, z, x, c):
    return y, (z + 2 - 4 * (z % 2)) % 8, x, c


def two_back(y, z, x, c):
    return y, (z - 2 + 4 * (z % 2)) % 8, x, c


def far(y, z, x, c):
    return y, (z + 4) % 8, x, c


def along_y(d):
    return lambda y, z, x, c: (y ^ d, z, x, c)


def along_row(d):
    def move(y, z, x, c):
        p = (x * 2 + c) ^ d
        return y, z, p // 2, p % 2

    return move


def silu(a):
    return a * jax.nn.sigmoid(a)


def dot(a, b, dims):
    return lax.dot_general(a, b, (dims, ((), ())), preferred_element_type=F32)


def call(kernel, outs, *args, flops=0, scratch=(), space=pltpu.VMEM, far=0):
    moved = sum(a.size * a.dtype.itemsize for a in args)
    near = len(args) - far
    held = [pltpu.with_memory_space_constraint(a, pltpu.VMEM) for a in args[:near]] + list(args[near:])
    return pl.pallas_call(
        kernel,
        in_specs=[VMEM] * near + [pl.BlockSpec(memory_space=pltpu.HBM)] * far,
        out_specs=[VMEM] * len(outs),
        out_shape=[space(shape, dtype) for shape, dtype in outs],
        scratch_shapes=[pltpu.VMEM(shape, dtype) for shape, dtype in scratch] + [pltpu.SemaphoreType.DMA(())] * far,
        cost_estimate=pl.CostEstimate(flops=flops, bytes_accessed=moved, transcendentals=0),
        compiler_params=pltpu.CompilerParams(vmem_limit_bytes=24 << 20),
    )(*held)


def place():
    i = lax.axis_index("ctx")
    return lax.rem(i, 8), lax.div(i, 8)


def running(a):
    lane = lax.broadcasted_iota(jnp.int32, a.shape, 1)
    for step in (1, 2, 4, 8, 16, 32, 64, 128):
        a = a + jnp.where(lane >= step, pltpu.roll(a, step, axis=1), 0.0)
    return a


SHIFTS = (0, 1, 3, 2)


def split(a):
    high = a.astype(BF16)
    rest = a - high.astype(F32)
    mid = rest.astype(BF16)
    return high, mid, (rest - mid.astype(F32)).astype(BF16)


def pack(column):
    lane = lax.broadcasted_iota(jnp.int32, (16, 128), 1)
    high, mid, low = (jnp.broadcast_to(a.astype(F32), (16, 128)) for a in split(column))
    return jnp.where(lane == 0, high, jnp.where(lane == 1, mid, jnp.where(lane == 2, low, 0.0))).astype(BF16)


def unpack(tile):
    a = tile.astype(F32)
    return a[:, 0:1] + a[:, 1:2] + a[:, 2:3]


def prepare(rates, tok, r0, r1, r2, r3, entry, total, held, sem):
    f = lax.axis_index("fsdp")
    copy = pltpu.make_async_copy(tok, held, sem)
    copy.start()
    cums = []
    for i, out in enumerate((r0, r1, r2, r3)):
        group = lax.rem(f + SHIFTS[i], 4)
        own = rates[0:4, :]
        for g in range(1, 4):
            own = jnp.where(group == g, rates[4 * g : 4 * g + 4, :], own)
        own = jnp.concatenate([own, jnp.zeros_like(own)], axis=0)
        out[...] = own
        cums.append(running(own)[:4])
    cum = jnp.concatenate(cums, axis=0)
    entry[...] = jnp.concatenate([jnp.exp(cum).T, jnp.zeros((256, 112), F32)], axis=1)
    total[...] = pack(cum[:, 255:256])
    copy.wait()


def load(w, held, sem):
    copy = pltpu.make_async_copy(w, held, sem)
    copy.start()
    copy.wait()


def states(tok, w, rates, *refs):
    k_out, v_out, local = refs[-3:]
    cum = running(rates[...])
    tail = jnp.exp(cum[:, 255:256] - cum).T
    for j in range(2):
        pair = slice(256 * j, 256 * j + 256)
        k = silu(jnp.dot(tok[...], w[1, :, pair], preferred_element_type=F32)).astype(BF16)
        v = jnp.dot(tok[...], w[2, :, pair], preferred_element_type=F32).astype(BF16)
        k_out[:, pair] = k
        v_out[:, pair] = v
        for h in range(2):
            cols = slice(128 * h, 128 * h + 128)
            head = 2 * j + h
            scaled = (k[:, cols].astype(F32) * tail[:, head : head + 1]).astype(BF16)
            local[head] = dot(scaled, v[:, cols], ((0,), (0,))).astype(BF16)


def insides(tok, w, rates, k_ref, v_ref, *refs):
    out = refs[-1]
    cum = running(rates[...])
    col = cum.T
    n = tok.shape[0]
    causal = lax.broadcasted_iota(jnp.int32, (n, n), 0) >= lax.broadcasted_iota(jnp.int32, (n, n), 1)
    for j in range(2):
        pair = slice(256 * j, 256 * j + 256)
        q = silu(jnp.dot(tok[...], w[0, :, pair], preferred_element_type=F32)).astype(BF16)
        out[0, :, pair] = q
        for h in range(2):
            head = 2 * j + h
            cols = slice(128 * head, 128 * head + 128)
            scores = dot(q[:, 128 * h : 128 * h + 128], k_ref[:, cols], ((1,), (1,)))
            gaps = col[:, head : head + 1] - cum[head : head + 1, :]
            weights = (scores * jnp.exp(jnp.where(causal, gaps, -jnp.inf))).astype(BF16)
            out[1, :, cols] = jnp.dot(weights, v_ref[:, cols], preferred_element_type=F32).astype(BF16)


def deal(s0, s1, s2, s3, total, *outs):
    p, _ = place()
    for d in range(8):
        rows = pl.ds(pl.multiple_of(jnp.bitwise_xor(p, d) * 16, 16), 16)
        for i, s in enumerate((s0, s1, s2, s3)):
            outs[d][4 * i : 4 * i + 4] = s[:, rows, :]
        outs[d][16] = total[...]


def row_total(*refs):
    pieces, out, natural, decay = refs[:8], refs[8], refs[9], refs[10]
    p, _ = place()
    for d in range(8):
        natural[jnp.bitwise_xor(p, d)] = pieces[d][...]
    logs = jnp.zeros((16, 1), F32)
    for e in range(8):
        own = unpack(natural[e, 16])
        logs += own
        decay[e] = jnp.broadcast_to(jnp.exp(own), (16, 128))
    for h in range(16):
        run = natural[0, h].astype(F32)
        for e in range(1, 8):
            run = run * decay[e, h : h + 1, :] + natural[e, h].astype(F32)
        out[h] = run.astype(BF16)
    out[16] = pack(logs)


def carry(*refs):
    pieces, totals, outs, natural, rows, decay, row_decay = refs[:8], refs[8:16], refs[16:24], *refs[24:]
    p, r = place()
    for d in range(8):
        natural[jnp.bitwise_xor(p, d)] = pieces[d][...]
        rows[jnp.bitwise_xor(r, d)] = totals[d][...]
    for e in range(8):
        decay[e] = jnp.broadcast_to(jnp.exp(unpack(natural[e, 16])), (16, 128))
        row_decay[e] = jnp.broadcast_to(jnp.exp(jnp.where(e < r, unpack(rows[e, 16]), 0.0)), (16, 128))
    for h in range(16):
        run = jnp.zeros((16, 128), F32)
        for e in range(7):
            run = run * row_decay[e, h : h + 1, :] + jnp.where(e < r, rows[e, h].astype(F32), 0.0)
        for e in range(8):
            piece = natural[e, h].astype(F32)
            natural[e, h] = run.astype(BF16)
            run = run * decay[e, h : h + 1, :] + piece
    for d in range(8):
        outs[d][...] = natural[jnp.bitwise_xor(p, d), 0:16]


def final(entry, gain, *refs):
    parts, pieces, out, memory, attended = refs[:4], refs[4:12], refs[12], refs[13], refs[14]
    p, _ = place()
    f = lax.axis_index("fsdp")
    for d in range(8):
        rows = pl.ds(pl.multiple_of(jnp.bitwise_xor(p, d) * 16, 16), 16)
        memory[:, rows, :] = pieces[d][...]
    squares = jnp.zeros((out.shape[0], 128), F32)
    for i, shift in enumerate(SHIFTS):
        group = lax.rem(f + shift, 4)
        for h in range(4):
            cols = slice(128 * h, 128 * h + 128)
            incoming = jnp.dot(parts[i][0, :, cols], memory[4 * i + h], preferred_element_type=F32)
            value = parts[i][1, :, cols].astype(F32) + incoming * entry[:, 4 * i + h : 4 * i + h + 1]
            squares += value * value
            attended[:, pl.ds(pl.multiple_of(group * 512 + 128 * h, 128), 128)] = value
    scale = lax.rsqrt(jnp.sum(squares, axis=-1, keepdims=True) / out.shape[1] + 1e-05)
    out[...] = (attended[...] * scale * gain[...]).astype(BF16)


def body(tokens, qkv_weight, log_decay, norm_gain):
    tok = tokens[0]
    n, d = tok.shape
    piece = ((17, 16, 128), BF16)
    slots = ((8, 17, 16, 128), BF16)
    factor = ((8, 16, 128), F32)

    back_moves = (down, up, two_back)
    *rates, entry, total, held = call(
        prepare,
        [((8, n), F32)] * 4 + [((n, 128), F32), ((16, 128), BF16), ((n, d), BF16)],
        log_decay[0],
        tok,
        far=1,
    )
    rates = [rates[0]] + [send(a, m) for a, m in zip(rates[1:], (up, down, two))]
    toks = [held, send(tok, up), send(tok, down)]
    toks.append(send(held, two))
    weight = call(load, [(qkv_weight.shape, BF16)], qkv_weight, far=1)[0]

    half = ((n, 512), BF16)
    made = []
    for t, a in zip(toks, rates):
        after = (made[0][2],) if made else ()
        made.append(
            call(states, [half, half, ((4, 128, 128), BF16)], t, weight, a, *after, flops=1 << 30)
        )
    owned = [made[0][2]] + [send(made[s + 1][2], m) for s, m in enumerate(back_moves)]
    pieces = call(deal, [piece] * 8, *owned, total)
    first = pieces[1]
    pieces = [pieces[0]] + [send(pieces[e], along_row(e)) for e in range(1, 8)]
    own_total = call(row_total, [piece], *pieces, scratch=[slots, factor])[0]

    after = ((), (made[3][2],), (first,), (own_total,))
    parts = []
    for i in range(4):
        out = ((2, n, 512), BF16)
        parts += call(insides, [out], toks[i], weight, rates[i], *made[i][:2], *after[i], flops=1 << 30)
    parts = [parts[0]] + [send(parts[i + 1], m) for i, m in enumerate(back_moves)]

    far_total = send(own_total, far)
    near = [send(own_total, along_y(e)) for e in range(1, 4)]
    totals = [own_total, far_total]
    for e in range(1, 4):
        totals += [near[e - 1], send(far_total, along_y(e))]
    carried = call(carry, [((16, 16, 128), BF16)] * 8, *pieces, *totals, scratch=[slots] * 2 + [factor] * 2)
    carried = [carried[0]] + [send(carried[e], along_row(e)) for e in range(1, 8)]
    out = call(
        final,
        [((n, d), BF16)],
        entry,
        norm_gain[None],
        *parts,
        *carried,
        scratch=[((16, 128, 128), BF16), ((n, d), F32)],
        space=jax.ShapeDtypeStruct,
    )[0]
    return out[None]


def solution(mesh):
    placed = (P("fsdp", "ctx", None), P(None, None, "fsdp"), P("fsdp", None, "ctx"), P())
    return jax.shard_map(body, mesh=mesh, in_specs=placed, out_specs=P("fsdp", "ctx", None), check_vma=False)
```

time: 1010 us -> 147 us (0.15)
  the two profiles are of different devices: /device:TPU:159 before, /device:TPU:96 now
where the time goes in v1:
time: 147 us; the launch traced here: 146 us
  waiting for transfers between devices  72.7 us (49%)
  starting transfers between devices  49.1 us (33%)
  Pallas kernels  19.6 us (13%)
  local copies, waits for them, and re-layouts  4.8 us (3%)
    ppermute x33, waiting for transfers between devices, send(): return lax.ppermute(a, BOTH, pairs(move))  72.7 us
    ppermute x33, starting transfers between devices, send(): return lax.ppermute(a, BOTH, pairs(move))  49.1 us
    pallas_call x14, Pallas kernels, call(): pl.pallas_call(kernel, in_specs=[VMEM] * near + [pl.BlockSpec(memory_spac...  19.6 us
    unnamed x8, local copies, waits for them, and re-layouts  4.8 us
  transfers between devices with their start and end apart: 33, of which 13 were waited for; matrix products, arithmetic and copies ran while one was open for 0% of the time, Pallas kernels for 12%

profile of v1, /device:TPU:96, one launch (start us, length us, event | category | flops | bytes accessed | tf_op | source)
XLA Modules:
  0.0 146.4 jit_solution(305792546108046703)
XLA Ops:
  0.0 3.1 %collective-permute-start = (bf16[256,2048]{1,0:T(8,128)(2,1)}, bf16[256,2048]{1,0:T(8,128)(2,1)S(1)}, u32[]{:S(2)}, u32[]{:S(2)}) collective-permute-start(bf16[256,2048]{1,0:T(8,128)(2,1)} %bitcast.4), channel_id=1, source_target_pairs={{0,1},{4,5},{8,9},{12,13},{16,17},{20,21},{24,25},{28,29},{1,2},{5... | collective-permute-start | bytes 3145736 | tf_op jit(solution)/shard_map/ppermute | solution.py:24
  6.0 3.5 %collective-permute-start.1 = (f32[8,256]{1,0:T(8,128)S(1)}, f32[8,256]{1,0:T(8,128)S(1)}, u32[]{:S(2)}, u32[]{:S(2)}) collective-permute-start(f32[8,256]{1,0:T(8,128)S(1)} %get-tuple-element.45), channel_id=1, source_target_pairs={{0,1},{4,5},{8,9},{12,13},{16,17},{20,21},{24,25},{28,29},{1,2},{5... | collective-permute-start | bytes 24584 | tf_op jit(solution)/shard_map/ppermute | solution.py:24
  9.4 2.7 %collective-permute-start.3 = (f32[8,256]{1,0:T(8,128)S(1)}, f32[8,256]{1,0:T(8,128)S(1)}, u32[]{:S(2)}, u32[]{:S(2)}) collective-permute-start(f32[8,256]{1,0:T(8,128)S(1)} %get-tuple-element.49), channel_id=1, source_target_pairs={{0,2},{4,6},{8,10},{12,14},{16,18},{20,22},{24,26},{28,30},{1,35},... | collective-permute-start | bytes 24584 | tf_op jit(solution)/shard_map/ppermute | solution.py:24
  12.1 2.8 %copy-done = bf16[3,2048,512]{2,1,0:T(8,128)(2,1)S(1)} copy-done((bf16[3,2048,512]{2,1,0:T(8,128)(2,1)S(1)}, bf16[3,2048,512]{2,1,0:T(8,128)(2,1)}, u32[]{:S(2)}) %copy-start) | copy-done | bytes 6291480
  15.3 1.8 %shard_map.48 = (bf16[256,512]{1,0:T(8,128)(2,1)S(1)}, bf16[256,512]{1,0:T(8,128)(2,1)S(1)}, bf16[4,128,128]{2,1,0:T(8,128)(2,1)S(1)}) custom-call(bf16[256,2048]{1,0:T(8,128)(2,1)S(1)} %get-tuple-element.41.tok, bf16[3,2048,512]{2,1,0:T(8,128)(2,1)S(1)} %shard_map.47.w, f32[8,256]{1,0:T(8,128)S(1)} %get-tuple-element.42.rates), custom_call_target="tpu_custom_call" | custom-call | flops 1073741824 | bytes 7348224 | tf_op jit(solution)/shard_map/pallas_call | solution.py:71
  17.1 31.5 %collective-permute-done.1.rates = f32[8,256]{1,0:T(8,128)S(1)} collective-permute-done((f32[8,256]{1,0:T(8,128)S(1)}, f32[8,256]{1,0:T(8,128)S(1)}, u32[]{:S(2)}, u32[]{:S(2)}) %collective-permute-start.1) | collective-permute-done | bytes 8224 | tf_op jit(solution)/shard_map/ppermute | solution.py:24
  48.6 1.8 %shard_map.50 = (bf16[256,512]{1,0:T(8,128)(2,1)S(1)}, bf16[256,512]{1,0:T(8,128)(2,1)S(1)}, bf16[4,128,128]{2,1,0:T(8,128)(2,1)S(1)}) custom-call(bf16[256,2048]{1,0:T(8,128)(2,1)S(1)} %collective-permute-done.tok, bf16[3,2048,512]{2,1,0:T(8,128)(2,1)S(1)} %shard_map.47.w, f32[8,256]{1,0:T(8,128)S(1)} %collective-permute-done.1.rates, ...), custom_call_target="tpu_custom_call" | custom-call | flops 1073741824 | bytes 7479296 | tf_op jit(solution)/shard_map/pallas_call | solution.py:71
  50.5 3.4 %collective-permute-done.6.rates = f32[8,256]{1,0:T(8,128)S(1)} collective-permute-done((f32[8,256]{1,0:T(8,128)S(1)}, f32[8,256]{1,0:T(8,128)S(1)}, u32[]{:S(2)}, u32[]{:S(2)}) %collective-permute-start.6) | collective-permute-done | bytes 8224 | tf_op jit(solution)/shard_map/ppermute | solution.py:24
  53.9 1.8 %shard_map.53 = (bf16[256,512]{1,0:T(8,128)(2,1)S(1)}, bf16[256,512]{1,0:T(8,128)(2,1)S(1)}, bf16[4,128,128]{2,1,0:T(8,128)(2,1)S(1)}) custom-call(bf16[256,2048]{1,0:T(8,128)(2,1)S(1)} %collective-permute-done.5.tok, bf16[3,2048,512]{2,1,0:T(8,128)(2,1)S(1)} %shard_map.47.w, f32[8,256]{1,0:T(8,128)S(1)} %collective-permute-done.6.rates, ...), custom_call_target="tpu_custom_call" | custom-call | flops 1073741824 | bytes 7479296 | tf_op jit(solution)/shard_map/pallas_call | solution.py:71
  55.7 2.2 %collective-permute-start.8 = (bf16[4,128,128]{2,1,0:T(8,128)(2,1)S(1)}, bf16[4,128,128]{2,1,0:T(8,128)(2,1)S(1)}, u32[]{:S(2)}, u32[]{:S(2)}) collective-permute-start(bf16[4,128,128]{2,1,0:T(8,128)(2,1)S(1)} %get-tuple-element.55), channel_id=1, source_target_pairs={{0,1},{4,5},{8,9},{12,13},{16,17},{20,21},{24,25},{28,29},{1,2},{5... | collective-permute-start | bytes 393224 | tf_op jit(solution)/shard_map/ppermute | solution.py:24
  57.9 1.8 %shard_map.51 = (bf16[256,512]{1,0:T(8,128)(2,1)S(1)}, bf16[256,512]{1,0:T(8,128)(2,1)S(1)}, bf16[4,128,128]{2,1,0:T(8,128)(2,1)S(1)}) custom-call(bf16[256,2048]{1,0:T(8,128)(2,1)S(1)} %collective-permute-done.2.tok, bf16[3,2048,512]{2,1,0:T(8,128)(2,1)S(1)} %shard_map.47.w, f32[8,256]{1,0:T(8,128)S(1)} %collective-permute-done.3.rates, ...), custom_call_target="tpu_custom_call" | custom-call | flops 1073741824 | bytes 7479296 | tf_op jit(solution)/shard_map/pallas_call | solution.py:71
  59.6 1.9 %collective-permute-start.9 = (bf16[4,128,128]{2,1,0:T(8,128)(2,1)S(1)}, bf16[4,128,128]{2,1,0:T(8,128)(2,1)S(1)}, u32[]{:S(2)}, u32[]{:S(2)}) collective-permute-start(bf16[4,128,128]{2,1,0:T(8,128)(2,1)S(1)} %get-tuple-element.50.refs_0_), channel_id=1, source_target_pairs={{0,34},{4,38},{8,42},{12,46},{16,50},{20,54},{24,58},{28,62},{1,3}... | collective-permute-start | bytes 393224 | tf_op jit(solution)/shard_map/ppermute | solution.py:24
  61.5 4.2 %collective-permute-done.9.s3 = bf16[4,128,128]{2,1,0:T(8,128)(2,1)S(1)} collective-permute-done((bf16[4,128,128]{2,1,0:T(8,128)(2,1)S(1)}, bf16[4,128,128]{2,1,0:T(8,128)(2,1)S(1)}, u32[]{:S(2)}, u32[]{:S(2)}) %collective-permute-start.9) | collective-permute-done | bytes 131104 | tf_op jit(solution)/shard_map/ppermute | solution.py:24
  65.9 1.6 %collective-permute-start.12 = (bf16[17,16,128]{2,1,0:T(8,128)(2,1)S(1)}, bf16[17,16,128]{2,1,0:T(8,128)(2,1)S(1)}, u32[]{:S(2)}, u32[]{:S(2)}) collective-permute-start(bf16[17,16,128]{2,1,0:T(8,128)(2,1)S(1)} %get-tuple-element.61), channel_id=1, source_target_pairs={{0,8},{4,12},{8,0},{12,4},{16,24},{20,28},{24,16},{28,20},{1,9},{5... | collective-permute-start | bytes 208904 | tf_op jit(solution)/shard_map/ppermute | solution.py:24
  67.5 2.1 %shard_map.52 = bf16[2,256,512]{2,1,0:T(8,128)(2,1)S(1)} custom-call(bf16[256,2048]{1,0:T(8,128)(2,1)S(1)} %collective-permute-done.tok, bf16[3,2048,512]{2,1,0:T(8,128)(2,1)S(1)} %shard_map.47.w, f32[8,256]{1,0:T(8,128)S(1)} %collective-permute-done.1.rates, bf16[256,512]{1,0:T(8,128)(2,1)S(1)} %get-tuple-element.47.k_ref, ...), custom_call_target="tpu_custom_call" | custom-call | flops 1073741824 | bytes 8003584 | tf_op jit(solution)/shard_map/pallas_call | solution.py:71
  70.0 3.0 %collective-permute-start.14 = (bf16[17,16,128]{2,1,0:T(8,128)(2,1)S(1)}, bf16[17,16,128]{2,1,0:T(8,128)(2,1)S(1)}, u32[]{:S(2)}, u32[]{:S(2)}) collective-permute-start(bf16[17,16,128]{2,1,0:T(8,128)(2,1)S(1)} %get-tuple-element.63), channel_id=1, source_target_pairs={{0,16},{4,20},{8,24},{12,28},{16,0},{20,4},{24,8},{28,12},{1,17},{... | collective-permute-start | bytes 208904 | tf_op jit(solution)/shard_map/ppermute | solution.py:24
  73.3 2.8 %collective-permute-start.16 = (bf16[17,16,128]{2,1,0:T(8,128)(2,1)S(1)}, bf16[17,16,128]{2,1,0:T(8,128)(2,1)S(1)}, u32[]{:S(2)}, u32[]{:S(2)}) collective-permute-start(bf16[17,16,128]{2,1,0:T(8,128)(2,1)S(1)} %get-tuple-element.65), channel_id=1, source_target_pairs={{0,24},{4,28},{8,16},{12,20},{16,8},{20,12},{24,0},{28,4},{1,25},{... | collective-permute-start | bytes 208904 | tf_op jit(solution)/shard_map/ppermute | solution.py:24
  76.2 2.1 %shard_map.55 = bf16[2,256,512]{2,1,0:T(8,128)(2,1)S(1)} custom-call(bf16[256,2048]{1,0:T(8,128)(2,1)S(1)} %collective-permute-done.5.tok, bf16[3,2048,512]{2,1,0:T(8,128)(2,1)S(1)} %shard_map.47.w, f32[8,256]{1,0:T(8,128)S(1)} %collective-permute-done.6.rates, bf16[256,512]{1,0:T(8,128)(2,1)S(1)} %get-tuple-element.52.k_ref, ...), custom_call_target="tpu_custom_call" | custom-call | flops 1073741824 | bytes 7942144 | tf_op jit(solution)/shard_map/pallas_call | solution.py:71
  79.6 2.1 %collective-permute-start.10 = (bf16[2,256,512]{2,1,0:T(8,128)(2,1)S(1)}, bf16[2,256,512]{2,1,0:T(8,128)(2,1)S(1)}, u32[]{:S(2)}, u32[]{:S(2)}) collective-permute-start(bf16[2,256,512]{2,1,0:T(8,128)(2,1)S(1)} %shard_map.55), channel_id=1, source_target_pairs={{0,1},{4,5},{8,9},{12,13},{16,17},{20,21},{24,25},{28,29},{1,2},{5... | collective-permute-start | bytes 1572872 | tf_op jit(solution)/shard_map/ppermute | solution.py:24
  82.1 1.7 %collective-permute-start.19 = (bf16[17,16,128]{2,1,0:T(8,128)(2,1)S(1)}, bf16[17,16,128]{2,1,0:T(8,128)(2,1)S(1)}, u32[]{:S(2)}, u32[]{:S(2)}) collective-permute-start(bf16[17,16,128]{2,1,0:T(8,128)(2,1)S(1)} %shard_map.56.refs_0_.refs_8_), channel_id=1, source_target_pairs={{0,32},{4,36},{8,40},{12,44},{16,48},{20,52},{24,56},{28,60},{1,33... | collective-permute-start | bytes 208904 | tf_op jit(solution)/shard_map/ppermute | solution.py:24
  83.8 2.1 %shard_map.57 = bf16[2,256,512]{2,1,0:T(8,128)(2,1)S(1)} custom-call(bf16[256,2048]{1,0:T(8,128)(2,1)S(1)} %collective-permute-done.2.tok, bf16[3,2048,512]{2,1,0:T(8,128)(2,1)S(1)} %shard_map.47.w, f32[8,256]{1,0:T(8,128)S(1)} %collective-permute-done.3.rates, bf16[256,512]{1,0:T(8,128)(2,1)S(1)} %get-tuple-element.58.k_ref, ...), custom_call_target="tpu_custom_call" | custom-call | flops 1073741824 | bytes 7942144 | tf_op jit(solution)/shard_map/pallas_call | solution.py:71
  85.9 2.6 %collective-permute-start.18 = (bf16[2,256,512]{2,1,0:T(8,128)(2,1)S(1)}, bf16[2,256,512]{2,1,0:T(8,128)(2,1)S(1)}, u32[]{:S(2)}, u32[]{:S(2)}) collective-permute-start(bf16[2,256,512]{2,1,0:T(8,128)(2,1)S(1)} %shard_map.57), channel_id=1, source_target_pairs={{0,34},{4,38},{8,42},{12,46},{16,50},{20,54},{24,58},{28,62},{1,3}... | collective-permute-start | bytes 1572872 | tf_op jit(solution)/shard_map/ppermute | solution.py:24
  90.1 19.3 %collective-permute-done.19.refs_9_ = bf16[17,16,128]{2,1,0:T(8,128)(2,1)S(1)} collective-permute-done((bf16[17,16,128]{2,1,0:T(8,128)(2,1)S(1)}, bf16[17,16,128]{2,1,0:T(8,128)(2,1)S(1)}, u32[]{:S(2)}, u32[]{:S(2)}) %collective-permute-start.19) | collective-permute-done | bytes 69664 | tf_op jit(solution)/shard_map/ppermute | solution.py:24
  109.4 3.2 %collective-permute-start.22 = (bf16[17,16,128]{2,1,0:T(8,128)(2,1)S(1)}, bf16[17,16,128]{2,1,0:T(8,128)(2,1)S(1)}, u32[]{:S(2)}, u32[]{:S(2)}) collective-permute-start(bf16[17,16,128]{2,1,0:T(8,128)(2,1)S(1)} %shard_map.56.refs_0_.refs_8_), channel_id=1, source_target_pairs={{0,128},{4,132},{8,136},{12,140},{16,144},{20,148},{24,152},{28,15... | collective-permute-start | bytes 208904 | tf_op jit(solution)/shard_map/ppermute | solution.py:24
  119.7 2.8 %collective-permute-start.25 = (bf16[17,16,128]{2,1,0:T(8,128)(2,1)S(1)}, bf16[17,16,128]{2,1,0:T(8,128)(2,1)S(1)}, u32[]{:S(2)}, u32[]{:S(2)}) collective-permute-start(bf16[17,16,128]{2,1,0:T(8,128)(2,1)S(1)} %collective-permute-done.19.refs_9_), channel_id=1, source_target_pairs={{0,192},{4,196},{8,200},{12,204},{16,208},{20,212},{24,216},{28,22... | collective-permute-start | bytes 208904 | tf_op jit(solution)/shard_map/ppermute | solution.py:24
  127.6 2.9 %collective-permute-done.27.refs_6_ = bf16[16,16,128]{2,1,0:T(8,128)(2,1)S(1)} collective-permute-done((bf16[16,16,128]{2,1,0:T(8,128)(2,1)S(1)}, bf16[16,16,128]{2,1,0:T(8,128)(2,1)S(1)}, u32[]{:S(2)}, u32[]{:S(2)}) %collective-permute-start.27) | collective-permute-done | bytes 65568 | tf_op jit(solution)/shard_map/ppermute | solution.py:24
  130.5 2.2 %collective-permute-start.29 = (bf16[16,16,128]{2,1,0:T(8,128)(2,1)S(1)}, bf16[16,16,128]{2,1,0:T(8,128)(2,1)S(1)}, u32[]{:S(2)}, u32[]{:S(2)}) collective-permute-start(bf16[16,16,128]{2,1,0:T(8,128)(2,1)S(1)} %get-tuple-element.71), channel_id=1, source_target_pairs={{0,16},{4,20},{8,24},{12,28},{16,0},{20,4},{24,8},{28,12},{1,17},{... | collective-permute-start | bytes 196616 | tf_op jit(solution)/shard_map/ppermute | solution.py:24
  133.9 2.4 %collective-permute-done.29.refs_8_ = bf16[16,16,128]{2,1,0:T(8,128)(2,1)S(1)} collective-permute-done((bf16[16,16,128]{2,1,0:T(8,128)(2,1)S(1)}, bf16[16,16,128]{2,1,0:T(8,128)(2,1)S(1)}, u32[]{:S(2)}, u32[]{:S(2)}) %collective-permute-start.29) | collective-permute-done | bytes 65568 | tf_op jit(solution)/shard_map/ppermute | solution.py:24
  136.3 3.2 %collective-permute-start.31 = (bf16[16,16,128]{2,1,0:T(8,128)(2,1)S(1)}, bf16[16,16,128]{2,1,0:T(8,128)(2,1)S(1)}, u32[]{:S(2)}, u32[]{:S(2)}) collective-permute-start(bf16[16,16,128]{2,1,0:T(8,128)(2,1)S(1)} %get-tuple-element.73), channel_id=1, source_target_pairs={{0,24},{4,28},{8,16},{12,20},{16,8},{20,12},{24,0},{28,4},{1,25},{... | collective-permute-start | bytes 196616 | tf_op jit(solution)/shard_map/ppermute | solution.py:24
  139.9 2.1 %shard_map.49.refs_0_ = bf16[2,256,512]{2,1,0:T(8,128)(2,1)S(1)} custom-call(bf16[256,2048]{1,0:T(8,128)(2,1)S(1)} %get-tuple-element.41.tok, bf16[3,2048,512]{2,1,0:T(8,128)(2,1)S(1)} %shard_map.47.w, f32[8,256]{1,0:T(8,128)S(1)} %get-tuple-element.42.rates, bf16[256,512]{1,0:T(8,128)(2,1)S(1)} %get-tuple-element.43.k_ref, ...), custom_call_target="tpu_custom_call" | custom-call | flops 1073741824 | bytes 7872512 | tf_op jit(solution)/shard_map/pallas_call | solution.py:71
  142.1 2.3 %collective-permute-done.32.refs_11_ = bf16[16,16,128]{2,1,0:T(8,128)(2,1)S(1)} collective-permute-done((bf16[16,16,128]{2,1,0:T(8,128)(2,1)S(1)}, bf16[16,16,128]{2,1,0:T(8,128)(2,1)S(1)}, u32[]{:S(2)}, u32[]{:S(2)}) %collective-permute-start.32) | collective-permute-done | bytes 65568 | tf_op jit(solution)/shard_map/ppermute | solution.py:24
  144.4 2.0 %shard_map.59 = bf16[256,2048]{1,0:T(8,128)(2,1)} custom-call(f32[256,128]{1,0:T(8,128)S(1)} %get-tuple-element.40.entry, f32[1,2048]{1,0:T(1,128)S(1)} %bitcast.8, bf16[2,256,512]{2,1,0:T(8,128)(2,1)S(1)} %shard_map.49.refs_0_, bf16[2,256,512]{2,1,0:T(8,128)(2,1)S(1)} %collective-permute-done.4.refs_1_, ...), custom_call_target="tpu_custom_call" | custom-call | bytes 2760704 | tf_op jit(solution)/shard_map/pallas_call | solution.py:71
  (56 shorter events, 21.2 us)
Async XLA Ops:
  0.0 48.6 %collective-permute-start = (bf16[256,2048]{1,0:T(8,128)(2,1)}, bf16[256,2048]{1,0:T(8,128)(2,1)S(1)}, u32[]{:S(2)}, u32[]{:S(2)}) collective-permute-start(bf16[256,2048]{1,0:T(8,128)(2,1)} %bitcast.4), channel_id=1, source_target_pairs={{0,1},{4,5},{8,9},{12,13},{16,17},{20,21},{24,25},{28,29},{1,2},{5... | collective-permute-start | bytes 3145736 | tf_op jit(solution)/shard_map/ppermute | solution.py:24
  3.1 50.8 %collective-permute-start.5 = (bf16[256,2048]{1,0:T(8,128)(2,1)}, bf16[256,2048]{1,0:T(8,128)(2,1)S(1)}, u32[]{:S(2)}, u32[]{:S(2)}) collective-permute-start(bf16[256,2048]{1,0:T(8,128)(2,1)} %bitcast.5), channel_id=1, source_target_pairs={{0,35},{4,39},{8,43},{12,47},{16,51},{20,55},{24,59},{28,63},{1,0}... | collective-permute-start | bytes 3145736 | tf_op jit(solution)/shard_map/ppermute | solution.py:24
  5.9 52.0 %collective-permute-start.2 = (bf16[256,2048]{1,0:T(8,128)(2,1)S(1)}, bf16[256,2048]{1,0:T(8,128)(2,1)S(1)}, u32[]{:S(2)}, u32[]{:S(2)}) collective-permute-start(bf16[256,2048]{1,0:T(8,128)(2,1)S(1)} %get-tuple-element.41.tok), channel_id=1, source_target_pairs={{0,2},{4,6},{8,10},{12,14},{16,18},{20,22},{24,26},{28,30},{1,35},... | collective-permute-start | bytes 3145736 | tf_op jit(solution)/shard_map/ppermute | solution.py:24
  6.0 42.6 %collective-permute-start.1 = (f32[8,256]{1,0:T(8,128)S(1)}, f32[8,256]{1,0:T(8,128)S(1)}, u32[]{:S(2)}, u32[]{:S(2)}) collective-permute-start(f32[8,256]{1,0:T(8,128)S(1)} %get-tuple-element.45), channel_id=1, source_target_pairs={{0,1},{4,5},{8,9},{12,13},{16,17},{20,21},{24,25},{28,29},{1,2},{5... | collective-permute-start | bytes 24584 | tf_op jit(solution)/shard_map/ppermute | solution.py:24
  9.4 48.4 %collective-permute-start.3 = (f32[8,256]{1,0:T(8,128)S(1)}, f32[8,256]{1,0:T(8,128)S(1)}, u32[]{:S(2)}, u32[]{:S(2)}) collective-permute-start(f32[8,256]{1,0:T(8,128)S(1)} %get-tuple-element.49), channel_id=1, source_target_pairs={{0,2},{4,6},{8,10},{12,14},{16,18},{20,22},{24,26},{28,30},{1,35},... | collective-permute-start | bytes 24584 | tf_op jit(solution)/shard_map/ppermute | solution.py:24
  48.6 5.3 %collective-permute-start.6 = (f32[8,256]{1,0:T(8,128)S(1)}, f32[8,256]{1,0:T(8,128)S(1)}, u32[]{:S(2)}, u32[]{:S(2)}) collective-permute-start(f32[8,256]{1,0:T(8,128)S(1)} %get-tuple-element.51), channel_id=1, source_target_pairs={{0,35},{4,39},{8,43},{12,47},{16,51},{20,55},{24,59},{28,63},{1,0}... | collective-permute-start | bytes 24584 | tf_op jit(solution)/shard_map/ppermute | solution.py:24
  50.4 11.1 %collective-permute-start.7 = (bf16[4,128,128]{2,1,0:T(8,128)(2,1)S(1)}, bf16[4,128,128]{2,1,0:T(8,128)(2,1)S(1)}, u32[]{:S(2)}, u32[]{:S(2)}) collective-permute-start(bf16[4,128,128]{2,1,0:T(8,128)(2,1)S(1)} %get-tuple-element.54), channel_id=1, source_target_pairs={{0,35},{4,39},{8,43},{12,47},{16,51},{20,55},{24,59},{28,63},{1,0}... | collective-permute-start | bytes 393224 | tf_op jit(solution)/shard_map/ppermute | solution.py:24
  55.7 5.8 %collective-permute-start.8 = (bf16[4,128,128]{2,1,0:T(8,128)(2,1)S(1)}, bf16[4,128,128]{2,1,0:T(8,128)(2,1)S(1)}, u32[]{:S(2)}, u32[]{:S(2)}) collective-permute-start(bf16[4,128,128]{2,1,0:T(8,128)(2,1)S(1)} %get-tuple-element.55), channel_id=1, source_target_pairs={{0,1},{4,5},{8,9},{12,13},{16,17},{20,21},{24,25},{28,29},{1,2},{5... | collective-permute-start | bytes 393224 | tf_op jit(solution)/shard_map/ppermute | solution.py:24
  59.6 6.1 %collective-permute-start.9 = (bf16[4,128,128]{2,1,0:T(8,128)(2,1)S(1)}, bf16[4,128,128]{2,1,0:T(8,128)(2,1)S(1)}, u32[]{:S(2)}, u32[]{:S(2)}) collective-permute-start(bf16[4,128,128]{2,1,0:T(8,128)(2,1)S(1)} %get-tuple-element.50.refs_0_), channel_id=1, source_target_pairs={{0,34},{4,38},{8,42},{12,46},{16,50},{20,54},{24,58},{28,62},{1,3}... | collective-permute-start | bytes 393224 | tf_op jit(solution)/shard_map/ppermute | solution.py:24
  65.8 7.4 %collective-permute-start.11 = (bf16[17,16,128]{2,1,0:T(8,128)(2,1)S(1)}, bf16[17,16,128]{2,1,0:T(8,128)(2,1)S(1)}, u32[]{:S(2)}, u32[]{:S(2)}) collective-permute-start(bf16[17,16,128]{2,1,0:T(8,128)(2,1)S(1)} %get-tuple-element.57.refs_0_), channel_id=1, source_target_pairs={{0,4},{4,0},{8,12},{12,8},{16,20},{20,16},{24,28},{28,24},{1,5},{5... | collective-permute-start | bytes 208904 | tf_op jit(solution)/shard_map/ppermute | solution.py:24
  65.9 10.1 %collective-permute-start.12 = (bf16[17,16,128]{2,1,0:T(8,128)(2,1)S(1)}, bf16[17,16,128]{2,1,0:T(8,128)(2,1)S(1)}, u32[]{:S(2)}, u32[]{:S(2)}) collective-permute-start(bf16[17,16,128]{2,1,0:T(8,128)(2,1)S(1)} %get-tuple-element.61), channel_id=1, source_target_pairs={{0,8},{4,12},{8,0},{12,4},{16,24},{20,28},{24,16},{28,20},{1,9},{5... | collective-permute-start | bytes 208904 | tf_op jit(solution)/shard_map/ppermute | solution.py:24
  69.7 8.7 %collective-permute-start.13 = (bf16[17,16,128]{2,1,0:T(8,128)(2,1)S(1)}, bf16[17,16,128]{2,1,0:T(8,128)(2,1)S(1)}, u32[]{:S(2)}, u32[]{:S(2)}) collective-permute-start(bf16[17,16,128]{2,1,0:T(8,128)(2,1)S(1)} %get-tuple-element.62), channel_id=1, source_target_pairs={{0,12},{4,8},{8,4},{12,0},{16,28},{20,24},{24,20},{28,16},{1,13},{... | collective-permute-start | bytes 208904 | tf_op jit(solution)/shard_map/ppermute | solution.py:24
  70.0 9.6 %collective-permute-start.14 = (bf16[17,16,128]{2,1,0:T(8,128)(2,1)S(1)}, bf16[17,16,128]{2,1,0:T(8,128)(2,1)S(1)}, u32[]{:S(2)}, u32[]{:S(2)}) collective-permute-start(bf16[17,16,128]{2,1,0:T(8,128)(2,1)S(1)} %get-tuple-element.63), channel_id=1, source_target_pairs={{0,16},{4,20},{8,24},{12,28},{16,0},{20,4},{24,8},{28,12},{1,17},{... | collective-permute-start | bytes 208904 | tf_op jit(solution)/shard_map/ppermute | solution.py:24
  73.0 8.7 %collective-permute-start.15 = (bf16[17,16,128]{2,1,0:T(8,128)(2,1)S(1)}, bf16[17,16,128]{2,1,0:T(8,128)(2,1)S(1)}, u32[]{:S(2)}, u32[]{:S(2)}) collective-permute-start(bf16[17,16,128]{2,1,0:T(8,128)(2,1)S(1)} %get-tuple-element.64), channel_id=1, source_target_pairs={{0,20},{4,16},{8,28},{12,24},{16,4},{20,0},{24,12},{28,8},{1,21},{... | collective-permute-start | bytes 208904 | tf_op jit(solution)/shard_map/ppermute | solution.py:24
  73.3 8.5 %collective-permute-start.16 = (bf16[17,16,128]{2,1,0:T(8,128)(2,1)S(1)}, bf16[17,16,128]{2,1,0:T(8,128)(2,1)S(1)}, u32[]{:S(2)}, u32[]{:S(2)}) collective-permute-start(bf16[17,16,128]{2,1,0:T(8,128)(2,1)S(1)} %get-tuple-element.65), channel_id=1, source_target_pairs={{0,24},{4,28},{8,16},{12,20},{16,8},{20,12},{24,0},{28,4},{1,25},{... | collective-permute-start | bytes 208904 | tf_op jit(solution)/shard_map/ppermute | solution.py:24
  76.0 5.8 %collective-permute-start.17 = (bf16[17,16,128]{2,1,0:T(8,128)(2,1)S(1)}, bf16[17,16,128]{2,1,0:T(8,128)(2,1)S(1)}, u32[]{:S(2)}, u32[]{:S(2)}) collective-permute-start(bf16[17,16,128]{2,1,0:T(8,128)(2,1)S(1)} %get-tuple-element.66), channel_id=1, source_target_pairs={{0,28},{4,24},{8,20},{12,16},{16,12},{20,8},{24,4},{28,0},{1,29},{... | collective-permute-start | bytes 208904 | tf_op jit(solution)/shard_map/ppermute | solution.py:24
  78.4 66.0 %collective-permute-start.4 = (bf16[2,256,512]{2,1,0:T(8,128)(2,1)S(1)}, bf16[2,256,512]{2,1,0:T(8,128)(2,1)S(1)}, u32[]{:S(2)}, u32[]{:S(2)}) collective-permute-start(bf16[2,256,512]{2,1,0:T(8,128)(2,1)S(1)} %shard_map.52), channel_id=1, source_target_pairs={{0,35},{4,39},{8,43},{12,47},{16,51},{20,55},{24,59},{28,63},{1,0}... | collective-permute-start | bytes 1572872 | tf_op jit(solution)/shard_map/ppermute | solution.py:24
  79.6 64.8 %collective-permute-start.10 = (bf16[2,256,512]{2,1,0:T(8,128)(2,1)S(1)}, bf16[2,256,512]{2,1,0:T(8,128)(2,1)S(1)}, u32[]{:S(2)}, u32[]{:S(2)}) collective-permute-start(bf16[2,256,512]{2,1,0:T(8,128)(2,1)S(1)} %shard_map.55), channel_id=1, source_target_pairs={{0,1},{4,5},{8,9},{12,13},{16,17},{20,21},{24,25},{28,29},{1,2},{5... | collective-permute-start | bytes 1572872 | tf_op jit(solution)/shard_map/ppermute | solution.py:24
  82.1 27.3 %collective-permute-start.19 = (bf16[17,16,128]{2,1,0:T(8,128)(2,1)S(1)}, bf16[17,16,128]{2,1,0:T(8,128)(2,1)S(1)}, u32[]{:S(2)}, u32[]{:S(2)}) collective-permute-start(bf16[17,16,128]{2,1,0:T(8,128)(2,1)S(1)} %shard_map.56.refs_0_.refs_8_), channel_id=1, source_target_pairs={{0,32},{4,36},{8,40},{12,44},{16,48},{20,52},{24,56},{28,60},{1,33... | collective-permute-start | bytes 208904 | tf_op jit(solution)/shard_map/ppermute | solution.py:24
  85.9 58.5 %collective-permute-start.18 = (bf16[2,256,512]{2,1,0:T(8,128)(2,1)S(1)}, bf16[2,256,512]{2,1,0:T(8,128)(2,1)S(1)}, u32[]{:S(2)}, u32[]{:S(2)}) collective-permute-start(bf16[2,256,512]{2,1,0:T(8,128)(2,1)S(1)} %shard_map.57), channel_id=1, source_target_pairs={{0,34},{4,38},{8,42},{12,46},{16,50},{20,54},{24,58},{28,62},{1,3}... | collective-permute-start | bytes 1572872 | tf_op jit(solution)/shard_map/ppermute | solution.py:24
  88.5 24.1 %collective-permute-start.20 = (bf16[17,16,128]{2,1,0:T(8,128)(2,1)S(1)}, bf16[17,16,128]{2,1,0:T(8,128)(2,1)S(1)}, u32[]{:S(2)}, u32[]{:S(2)}) collective-permute-start(bf16[17,16,128]{2,1,0:T(8,128)(2,1)S(1)} %shard_map.56.refs_0_.refs_8_), channel_id=1, source_target_pairs={{0,64},{4,68},{8,72},{12,76},{16,80},{20,84},{24,88},{28,92},{1,65... | collective-permute-start | bytes 208904 | tf_op jit(solution)/shard_map/ppermute | solution.py:24
  109.4 5.8 %collective-permute-start.22 = (bf16[17,16,128]{2,1,0:T(8,128)(2,1)S(1)}, bf16[17,16,128]{2,1,0:T(8,128)(2,1)S(1)}, u32[]{:S(2)}, u32[]{:S(2)}) collective-permute-start(bf16[17,16,128]{2,1,0:T(8,128)(2,1)S(1)} %shard_map.56.refs_0_.refs_8_), channel_id=1, source_target_pairs={{0,128},{4,132},{8,136},{12,140},{16,144},{20,148},{24,152},{28,15... | collective-permute-start | bytes 208904 | tf_op jit(solution)/shard_map/ppermute | solution.py:24
  112.6 5.5 %collective-permute-start.24 = (bf16[17,16,128]{2,1,0:T(8,128)(2,1)S(1)}, bf16[17,16,128]{2,1,0:T(8,128)(2,1)S(1)}, u32[]{:S(2)}, u32[]{:S(2)}) collective-permute-start(bf16[17,16,128]{2,1,0:T(8,128)(2,1)S(1)} %shard_map.56.refs_0_.refs_8_), channel_id=1, source_target_pairs={{0,192},{4,196},{8,200},{12,204},{16,208},{20,212},{24,216},{28,22... | collective-permute-start | bytes 208904 | tf_op jit(solution)/shard_map/ppermute | solution.py:24
  115.2 4.5 %collective-permute-start.21 = (bf16[17,16,128]{2,1,0:T(8,128)(2,1)S(1)}, bf16[17,16,128]{2,1,0:T(8,128)(2,1)S(1)}, u32[]{:S(2)}, u32[]{:S(2)}) collective-permute-start(bf16[17,16,128]{2,1,0:T(8,128)(2,1)S(1)} %collective-permute-done.19.refs_9_), channel_id=1, source_target_pairs={{0,64},{4,68},{8,72},{12,76},{16,80},{20,84},{24,88},{28,92},{1,65... | collective-permute-start | bytes 208904 | tf_op jit(solution)/shard_map/ppermute | solution.py:24
  118.1 5.8 %collective-permute-start.23 = (bf16[17,16,128]{2,1,0:T(8,128)(2,1)S(1)}, bf16[17,16,128]{2,1,0:T(8,128)(2,1)S(1)}, u32[]{:S(2)}, u32[]{:S(2)}) collective-permute-start(bf16[17,16,128]{2,1,0:T(8,128)(2,1)S(1)} %collective-permute-done.19.refs_9_), channel_id=1, source_target_pairs={{0,128},{4,132},{8,136},{12,140},{16,144},{20,148},{24,152},{28,15... | collective-permute-start | bytes 208904 | tf_op jit(solution)/shard_map/ppermute | solution.py:24
  119.7 5.5 %collective-permute-start.25 = (bf16[17,16,128]{2,1,0:T(8,128)(2,1)S(1)}, bf16[17,16,128]{2,1,0:T(8,128)(2,1)S(1)}, u32[]{:S(2)}, u32[]{:S(2)}) collective-permute-start(bf16[17,16,128]{2,1,0:T(8,128)(2,1)S(1)} %collective-permute-done.19.refs_9_), channel_id=1, source_target_pairs={{0,192},{4,196},{8,200},{12,204},{16,208},{20,212},{24,216},{28,22... | collective-permute-start | bytes 208904 | tf_op jit(solution)/shard_map/ppermute | solution.py:24
  125.8 4.8 %collective-permute-start.27 = (bf16[16,16,128]{2,1,0:T(8,128)(2,1)S(1)}, bf16[16,16,128]{2,1,0:T(8,128)(2,1)S(1)}, u32[]{:S(2)}, u32[]{:S(2)}) collective-permute-start(bf16[16,16,128]{2,1,0:T(8,128)(2,1)S(1)} %get-tuple-element.69), channel_id=1, source_target_pairs={{0,8},{4,12},{8,0},{12,4},{16,24},{20,28},{24,16},{28,20},{1,9},{5... | collective-permute-start | bytes 196616 | tf_op jit(solution)/shard_map/ppermute | solution.py:24
  127.0 5.7 %collective-permute-start.28 = (bf16[16,16,128]{2,1,0:T(8,128)(2,1)S(1)}, bf16[16,16,128]{2,1,0:T(8,128)(2,1)S(1)}, u32[]{:S(2)}, u32[]{:S(2)}) collective-permute-start(bf16[16,16,128]{2,1,0:T(8,128)(2,1)S(1)} %get-tuple-element.70), channel_id=1, source_target_pairs={{0,12},{4,8},{8,4},{12,0},{16,28},{20,24},{24,20},{28,16},{1,13},{... | collective-permute-start | bytes 196616 | tf_op jit(solution)/shard_map/ppermute | solution.py:24
  130.5 5.8 %collective-permute-start.29 = (bf16[16,16,128]{2,1,0:T(8,128)(2,1)S(1)}, bf16[16,16,128]{2,1,0:T(8,128)(2,1)S(1)}, u32[]{:S(2)}, u32[]{:S(2)}) collective-permute-start(bf16[16,16,128]{2,1,0:T(8,128)(2,1)S(1)} %get-tuple-element.71), channel_id=1, source_target_pairs={{0,16},{4,20},{8,24},{12,28},{16,0},{20,4},{24,8},{28,12},{1,17},{... | collective-permute-start | bytes 196616 | tf_op jit(solution)/shard_map/ppermute | solution.py:24
  132.8 6.7 %collective-permute-start.30 = (bf16[16,16,128]{2,1,0:T(8,128)(2,1)S(1)}, bf16[16,16,128]{2,1,0:T(8,128)(2,1)S(1)}, u32[]{:S(2)}, u32[]{:S(2)}) collective-permute-start(bf16[16,16,128]{2,1,0:T(8,128)(2,1)S(1)} %get-tuple-element.72), channel_id=1, source_target_pairs={{0,20},{4,16},{8,28},{12,24},{16,4},{20,0},{24,12},{28,8},{1,21},{... | collective-permute-start | bytes 196616 | tf_op jit(solution)/shard_map/ppermute | solution.py:24
  136.3 5.7 %collective-permute-start.31 = (bf16[16,16,128]{2,1,0:T(8,128)(2,1)S(1)}, bf16[16,16,128]{2,1,0:T(8,128)(2,1)S(1)}, u32[]{:S(2)}, u32[]{:S(2)}) collective-permute-start(bf16[16,16,128]{2,1,0:T(8,128)(2,1)S(1)} %get-tuple-element.73), channel_id=1, source_target_pairs={{0,24},{4,28},{8,16},{12,20},{16,8},{20,12},{24,0},{28,4},{1,25},{... | collective-permute-start | bytes 196616 | tf_op jit(solution)/shard_map/ppermute | solution.py:24
  139.5 4.9 %collective-permute-start.32 = (bf16[16,16,128]{2,1,0:T(8,128)(2,1)S(1)}, bf16[16,16,128]{2,1,0:T(8,128)(2,1)S(1)}, u32[]{:S(2)}, u32[]{:S(2)}) collective-permute-start(bf16[16,16,128]{2,1,0:T(8,128)(2,1)S(1)} %get-tuple-element.74), channel_id=1, source_target_pairs={{0,28},{4,24},{8,20},{12,16},{16,12},{20,8},{24,4},{28,0},{1,29},{... | collective-permute-start | bytes 196616 | tf_op jit(solution)/shard_map/ppermute | solution.py:24
  (5 other events, 64.6 us)

commit v2 on v1

--- a/solution.py
+++ b/solution.py
@@ -67,7 +67,9 @@
 def call(kernel, outs, *args, flops=0, scratch=(), space=pltpu.VMEM, far=0):
     moved = sum(a.size * a.dtype.itemsize for a in args)
     near = len(args) - far
-    held = [pltpu.with_memory_space_constraint(a, pltpu.VMEM) for a in args[:near]] + list(args[near:])
+    held = [pltpu.with_memory_space_constraint(a, pltpu.VMEM) for a in args[:near]] + [
+        pltpu.with_memory_space_constraint(a, pltpu.HBM) for a in args[near:]
+    ]
     return pl.pallas_call(
         kernel,
         in_specs=[VMEM] * near + [pl.BlockSpec(memory_space=pltpu.HBM)] * far,
@@ -258,7 +260,7 @@
     )
     rates = [rates[0]] + [send(a, m) for a, m in zip(rates[1:], (up, down, two))]
     toks = [held, send(tok, up), send(tok, down)]
-    toks.append(send(held, two))
+    toks.append(send(tok, two))
     weight = call(load, [(qkv_weight.shape, BF16)], qkv_weight, far=1)[0]
 
     half = ((n, 512), BF16)
@@ -268,18 +270,20 @@
         made.append(
             call(states, [half, half, ((4, 128, 128), BF16)], t, weight, a, *after, flops=1 << 30)
         )
-    owned = [made[0][2]] + [send(made[s + 1][2], m) for s, m in enumerate(back_moves)]
+    owned = [made[0][2]]
+    for s, m in enumerate(back_moves):
+        owned.append(send(made[s + 1][2], m))
     pieces = call(deal, [piece] * 8, *owned, total)
-    first = pieces[1]
     pieces = [pieces[0]] + [send(pieces[e], along_row(e)) for e in range(1, 8)]
     own_total = call(row_total, [piece], *pieces, scratch=[slots, factor])[0]
 
-    after = ((), (made[3][2],), (first,), (own_total,))
+    after = ((), (made[3][2],), (made[3][2],), (own_total,))
     parts = []
     for i in range(4):
         out = ((2, n, 512), BF16)
         parts += call(insides, [out], toks[i], weight, rates[i], *made[i][:2], *after[i], flops=1 << 30)
-    parts = [parts[0]] + [send(parts[i + 1], m) for i, m in enumerate(back_moves)]
+    for i, m in enumerate(back_moves):
+        parts[i + 1] = send(parts[i + 1], m)
 
     far_total = send(own_total, far)
     near = [send(own_total, along_y(e)) for e in range(1, 4)]

time: 147 us -> 147 us (level)
  local copies, waits for them, and re-layouts: 4.8 us -> 0.72 us
  Pallas kernels: 19.6 us -> 22.5 us
    unnamed x8 -> x4, local copies, waits for them, and re-layouts: 4.8 us -> 0.72 us
    pallas_call x14, Pallas kernels: 19.6 us -> 22.5 us  [call(): pl.pallas_call(kernel, in_specs=[VMEM] * near + [pl.BlockSpec(memory_spac...]
  transfers between devices with their start and end apart: 33 -> 33, of which waited for: 13 -> 13; matrix products, arithmetic and copies ran while one was open for 0% -> 0% of each run, Pallas kernels for 12% -> 14%
where the time goes in v2:
time: 147 us; the launch traced here: 146 us
  waiting for transfers between devices  73.8 us (50%)
  starting transfers between devices  49.2 us (33%)
  Pallas kernels  22.5 us (15%)
    ppermute x33, waiting for transfers between devices, send(): return lax.ppermute(a, BOTH, pairs(move))  73.8 us
    ppermute x33, starting transfers between devices, send(): return lax.ppermute(a, BOTH, pairs(move))  49.2 us
    pallas_call x14, Pallas kernels, call(): pl.pallas_call(kernel, in_specs=[VMEM] * near + [pl.BlockSpec(memory_spac...  22.5 us
  transfers between devices with their start and end apart: 33, of which 13 were waited for; matrix products, arithmetic and copies ran while one was open for 0% of the time, Pallas kernels for 14%

profile of v2, /device:TPU:96, one launch (start us, length us, event | category | flops | bytes accessed | tf_op | source)
XLA Modules:
  0.0 146.4 jit_solution(18077265310694738283)
XLA Ops:
  0.0 3.1 %collective-permute-start = (bf16[256,2048]{1,0:T(8,128)(2,1)}, bf16[256,2048]{1,0:T(8,128)(2,1)S(1)}, u32[]{:S(2)}, u32[]{:S(2)}) collective-permute-start(bf16[256,2048]{1,0:T(8,128)(2,1)} %bitcast.6), channel_id=1, source_target_pairs={{0,1},{4,5},{8,9},{12,13},{16,17},{20,21},{24,25},{28,29},{1,2},{5... | collective-permute-start | bytes 3145736 | tf_op jit(solution)/shard_map/ppermute | solution.py:24
  5.1 3.6 %collective-permute-start.1 = (f32[8,256]{1,0:T(8,128)S(1)}, f32[8,256]{1,0:T(8,128)S(1)}, u32[]{:S(2)}, u32[]{:S(2)}) collective-permute-start(f32[8,256]{1,0:T(8,128)S(1)} %get-tuple-element.45), channel_id=1, source_target_pairs={{0,1},{4,5},{8,9},{12,13},{16,17},{20,21},{24,25},{28,29},{1,2},{5... | collective-permute-start | bytes 24584 | tf_op jit(solution)/shard_map/ppermute | solution.py:24
  8.7 2.7 %collective-permute-start.3 = (f32[8,256]{1,0:T(8,128)S(1)}, f32[8,256]{1,0:T(8,128)S(1)}, u32[]{:S(2)}, u32[]{:S(2)}) collective-permute-start(f32[8,256]{1,0:T(8,128)S(1)} %get-tuple-element.49), channel_id=1, source_target_pairs={{0,2},{4,6},{8,10},{12,14},{16,18},{20,22},{24,26},{28,30},{1,35},... | collective-permute-start | bytes 24584 | tf_op jit(solution)/shard_map/ppermute | solution.py:24
  11.3 2.8 %shard_map.47.w = bf16[3,2048,512]{2,1,0:T(8,128)(2,1)S(1)} custom-call(bf16[3,2048,512]{2,1,0:T(8,128)(2,1)} %w.1), custom_call_target="tpu_custom_call" | custom-call | bytes 6291456 | tf_op jit(solution)/shard_map/pallas_call | solution.py:73
  14.1 1.8 %shard_map.48 = (bf16[256,512]{1,0:T(8,128)(2,1)S(1)}, bf16[256,512]{1,0:T(8,128)(2,1)S(1)}, bf16[4,128,128]{2,1,0:T(8,128)(2,1)S(1)}) custom-call(bf16[256,2048]{1,0:T(8,128)(2,1)S(1)} %get-tuple-element.41.tok, bf16[3,2048,512]{2,1,0:T(8,128)(2,1)S(1)} %shard_map.47.w, f32[8,256]{1,0:T(8,128)S(1)} %get-tuple-element.42.rates), custom_call_target="tpu_custom_call" | custom-call | flops 1073741824 | bytes 7348224 | tf_op jit(solution)/shard_map/pallas_call | solution.py:73
  15.9 32.7 %collective-permute-done.1.rates = f32[8,256]{1,0:T(8,128)S(1)} collective-permute-done((f32[8,256]{1,0:T(8,128)S(1)}, f32[8,256]{1,0:T(8,128)S(1)}, u32[]{:S(2)}, u32[]{:S(2)}) %collective-permute-start.1) | collective-permute-done | bytes 8224 | tf_op jit(solution)/shard_map/ppermute | solution.py:24
  48.6 1.8 %shard_map.50 = (bf16[256,512]{1,0:T(8,128)(2,1)S(1)}, bf16[256,512]{1,0:T(8,128)(2,1)S(1)}, bf16[4,128,128]{2,1,0:T(8,128)(2,1)S(1)}) custom-call(bf16[256,2048]{1,0:T(8,128)(2,1)S(1)} %collective-permute-done.tok, bf16[3,2048,512]{2,1,0:T(8,128)(2,1)S(1)} %shard_map.47.w, f32[8,256]{1,0:T(8,128)S(1)} %collective-permute-done.1.rates, ...), custom_call_target="tpu_custom_call" | custom-call | flops 1073741824 | bytes 7479296 | tf_op jit(solution)/shard_map/pallas_call | solution.py:73
  50.5 3.4 %collective-permute-done.6.rates = f32[8,256]{1,0:T(8,128)S(1)} collective-permute-done((f32[8,256]{1,0:T(8,128)S(1)}, f32[8,256]{1,0:T(8,128)S(1)}, u32[]{:S(2)}, u32[]{:S(2)}) %collective-permute-start.6) | collective-permute-done | bytes 8224 | tf_op jit(solution)/shard_map/ppermute | solution.py:24
  53.9 1.8 %shard_map.53 = (bf16[256,512]{1,0:T(8,128)(2,1)S(1)}, bf16[256,512]{1,0:T(8,128)(2,1)S(1)}, bf16[4,128,128]{2,1,0:T(8,128)(2,1)S(1)}) custom-call(bf16[256,2048]{1,0:T(8,128)(2,1)S(1)} %collective-permute-done.5.tok, bf16[3,2048,512]{2,1,0:T(8,128)(2,1)S(1)} %shard_map.47.w, f32[8,256]{1,0:T(8,128)S(1)} %collective-permute-done.6.rates, ...), custom_call_target="tpu_custom_call" | custom-call | flops 1073741824 | bytes 7479296 | tf_op jit(solution)/shard_map/pallas_call | solution.py:73
  55.7 2.2 %collective-permute-start.9 = (bf16[4,128,128]{2,1,0:T(8,128)(2,1)S(1)}, bf16[4,128,128]{2,1,0:T(8,128)(2,1)S(1)}, u32[]{:S(2)}, u32[]{:S(2)}) collective-permute-start(bf16[4,128,128]{2,1,0:T(8,128)(2,1)S(1)} %get-tuple-element.57), channel_id=1, source_target_pairs={{0,1},{4,5},{8,9},{12,13},{16,17},{20,21},{24,25},{28,29},{1,2},{5... | collective-permute-start | bytes 393224 | tf_op jit(solution)/shard_map/ppermute | solution.py:24
  57.9 1.8 %shard_map.51 = (bf16[256,512]{1,0:T(8,128)(2,1)S(1)}, bf16[256,512]{1,0:T(8,128)(2,1)S(1)}, bf16[4,128,128]{2,1,0:T(8,128)(2,1)S(1)}) custom-call(bf16[256,2048]{1,0:T(8,128)(2,1)S(1)} %collective-permute-done.2.tok, bf16[3,2048,512]{2,1,0:T(8,128)(2,1)S(1)} %shard_map.47.w, f32[8,256]{1,0:T(8,128)S(1)} %collective-permute-done.3.rates, ...), custom_call_target="tpu_custom_call" | custom-call | flops 1073741824 | bytes 7479296 | tf_op jit(solution)/shard_map/pallas_call | solution.py:73
  59.6 1.9 %collective-permute-start.10 = (bf16[4,128,128]{2,1,0:T(8,128)(2,1)S(1)}, bf16[4,128,128]{2,1,0:T(8,128)(2,1)S(1)}, u32[]{:S(2)}, u32[]{:S(2)}) collective-permute-start(bf16[4,128,128]{2,1,0:T(8,128)(2,1)S(1)} %get-tuple-element.50.refs_0_), channel_id=1, source_target_pairs={{0,34},{4,38},{8,42},{12,46},{16,50},{20,54},{24,58},{28,62},{1,3}... | collective-permute-start | bytes 393224 | tf_op jit(solution)/shard_map/ppermute | solution.py:24
  61.5 4.2 %collective-permute-done.10.s3 = bf16[4,128,128]{2,1,0:T(8,128)(2,1)S(1)} collective-permute-done((bf16[4,128,128]{2,1,0:T(8,128)(2,1)S(1)}, bf16[4,128,128]{2,1,0:T(8,128)(2,1)S(1)}, u32[]{:S(2)}, u32[]{:S(2)}) %collective-permute-start.10) | collective-permute-done | bytes 131104 | tf_op jit(solution)/shard_map/ppermute | solution.py:24
  67.5 2.1 %shard_map.52 = bf16[2,256,512]{2,1,0:T(8,128)(2,1)S(1)} custom-call(bf16[256,2048]{1,0:T(8,128)(2,1)S(1)} %collective-permute-done.tok, bf16[3,2048,512]{2,1,0:T(8,128)(2,1)S(1)} %shard_map.47.w, f32[8,256]{1,0:T(8,128)S(1)} %collective-permute-done.1.rates, bf16[256,512]{1,0:T(8,128)(2,1)S(1)} %get-tuple-element.47.k_ref, ...), custom_call_target="tpu_custom_call" | custom-call | flops 1073741824 | bytes 8003584 | tf_op jit(solution)/shard_map/pallas_call | solution.py:73
  70.0 3.0 %collective-permute-start.14 = (bf16[17,16,128]{2,1,0:T(8,128)(2,1)S(1)}, bf16[17,16,128]{2,1,0:T(8,128)(2,1)S(1)}, u32[]{:S(2)}, u32[]{:S(2)}) collective-permute-start(bf16[17,16,128]{2,1,0:T(8,128)(2,1)S(1)} %get-tuple-element.63), channel_id=1, source_target_pairs={{0,16},{4,20},{8,24},{12,28},{16,0},{20,4},{24,8},{28,12},{1,17},{... | collective-permute-start | bytes 208904 | tf_op jit(solution)/shard_map/ppermute | solution.py:24
  73.3 2.8 %collective-permute-start.16 = (bf16[17,16,128]{2,1,0:T(8,128)(2,1)S(1)}, bf16[17,16,128]{2,1,0:T(8,128)(2,1)S(1)}, u32[]{:S(2)}, u32[]{:S(2)}) collective-permute-start(bf16[17,16,128]{2,1,0:T(8,128)(2,1)S(1)} %get-tuple-element.65), channel_id=1, source_target_pairs={{0,24},{4,28},{8,16},{12,20},{16,8},{20,12},{24,0},{28,4},{1,25},{... | collective-permute-start | bytes 208904 | tf_op jit(solution)/shard_map/ppermute | solution.py:24
  76.2 2.1 %shard_map.54 = bf16[2,256,512]{2,1,0:T(8,128)(2,1)S(1)} custom-call(bf16[256,2048]{1,0:T(8,128)(2,1)S(1)} %collective-permute-done.5.tok, bf16[3,2048,512]{2,1,0:T(8,128)(2,1)S(1)} %shard_map.47.w, f32[8,256]{1,0:T(8,128)S(1)} %collective-permute-done.6.rates, bf16[256,512]{1,0:T(8,128)(2,1)S(1)} %get-tuple-element.52.k_ref, ...), custom_call_target="tpu_custom_call" | custom-call | flops 1073741824 | bytes 8003584 | tf_op jit(solution)/shard_map/pallas_call | solution.py:73
  79.6 2.1 %collective-permute-start.7 = (bf16[2,256,512]{2,1,0:T(8,128)(2,1)S(1)}, bf16[2,256,512]{2,1,0:T(8,128)(2,1)S(1)}, u32[]{:S(2)}, u32[]{:S(2)}) collective-permute-start(bf16[2,256,512]{2,1,0:T(8,128)(2,1)S(1)} %shard_map.54), channel_id=1, source_target_pairs={{0,1},{4,5},{8,9},{12,13},{16,17},{20,21},{24,25},{28,29},{1,2},{5... | collective-permute-start | bytes 1572872 | tf_op jit(solution)/shard_map/ppermute | solution.py:24
  82.1 1.7 %collective-permute-start.19 = (bf16[17,16,128]{2,1,0:T(8,128)(2,1)S(1)}, bf16[17,16,128]{2,1,0:T(8,128)(2,1)S(1)}, u32[]{:S(2)}, u32[]{:S(2)}) collective-permute-start(bf16[17,16,128]{2,1,0:T(8,128)(2,1)S(1)} %shard_map.56.refs_0_.refs_8_), channel_id=1, source_target_pairs={{0,32},{4,36},{8,40},{12,44},{16,48},{20,52},{24,56},{28,60},{1,33... | collective-permute-start | bytes 208904 | tf_op jit(solution)/shard_map/ppermute | solution.py:24
  83.8 2.1 %shard_map.57 = bf16[2,256,512]{2,1,0:T(8,128)(2,1)S(1)} custom-call(bf16[256,2048]{1,0:T(8,128)(2,1)S(1)} %collective-permute-done.2.tok, bf16[3,2048,512]{2,1,0:T(8,128)(2,1)S(1)} %shard_map.47.w, f32[8,256]{1,0:T(8,128)S(1)} %collective-permute-done.3.rates, bf16[256,512]{1,0:T(8,128)(2,1)S(1)} %get-tuple-element.54.k_ref, ...), custom_call_target="tpu_custom_call" | custom-call | flops 1073741824 | bytes 7942144 | tf_op jit(solution)/shard_map/pallas_call | solution.py:73
  85.9 2.6 %collective-permute-start.18 = (bf16[2,256,512]{2,1,0:T(8,128)(2,1)S(1)}, bf16[2,256,512]{2,1,0:T(8,128)(2,1)S(1)}, u32[]{:S(2)}, u32[]{:S(2)}) collective-permute-start(bf16[2,256,512]{2,1,0:T(8,128)(2,1)S(1)} %shard_map.57), channel_id=1, source_target_pairs={{0,34},{4,38},{8,42},{12,46},{16,50},{20,54},{24,58},{28,62},{1,3}... | collective-permute-start | bytes 1572872 | tf_op jit(solution)/shard_map/ppermute | solution.py:24
  88.5 1.6 %collective-permute-start.20 = (bf16[17,16,128]{2,1,0:T(8,128)(2,1)S(1)}, bf16[17,16,128]{2,1,0:T(8,128)(2,1)S(1)}, u32[]{:S(2)}, u32[]{:S(2)}) collective-permute-start(bf16[17,16,128]{2,1,0:T(8,128)(2,1)S(1)} %shard_map.56.refs_0_.refs_8_), channel_id=1, source_target_pairs={{0,64},{4,68},{8,72},{12,76},{16,80},{20,84},{24,88},{28,92},{1,65... | collective-permute-start | bytes 208904 | tf_op jit(solution)/shard_map/ppermute | solution.py:24
  90.1 19.3 %collective-permute-done.19.refs_9_ = bf16[17,16,128]{2,1,0:T(8,128)(2,1)S(1)} collective-permute-done((bf16[17,16,128]{2,1,0:T(8,128)(2,1)S(1)}, bf16[17,16,128]{2,1,0:T(8,128)(2,1)S(1)}, u32[]{:S(2)}, u32[]{:S(2)}) %collective-permute-start.19) | collective-permute-done | bytes 69664 | tf_op jit(solution)/shard_map/ppermute | solution.py:24
  109.4 3.2 %collective-permute-start.22 = (bf16[17,16,128]{2,1,0:T(8,128)(2,1)S(1)}, bf16[17,16,128]{2,1,0:T(8,128)(2,1)S(1)}, u32[]{:S(2)}, u32[]{:S(2)}) collective-permute-start(bf16[17,16,128]{2,1,0:T(8,128)(2,1)S(1)} %shard_map.56.refs_0_.refs_8_), channel_id=1, source_target_pairs={{0,128},{4,132},{8,136},{12,140},{16,144},{20,148},{24,152},{28,15... | collective-permute-start | bytes 208904 | tf_op jit(solution)/shard_map/ppermute | solution.py:24
  119.7 2.8 %collective-permute-start.25 = (bf16[17,16,128]{2,1,0:T(8,128)(2,1)S(1)}, bf16[17,16,128]{2,1,0:T(8,128)(2,1)S(1)}, u32[]{:S(2)}, u32[]{:S(2)}) collective-permute-start(bf16[17,16,128]{2,1,0:T(8,128)(2,1)S(1)} %collective-permute-done.19.refs_9_), channel_id=1, source_target_pairs={{0,192},{4,196},{8,200},{12,204},{16,208},{20,212},{24,216},{28,22... | collective-permute-start | bytes 208904 | tf_op jit(solution)/shard_map/ppermute | solution.py:24
  127.6 2.9 %collective-permute-done.27.refs_6_ = bf16[16,16,128]{2,1,0:T(8,128)(2,1)S(1)} collective-permute-done((bf16[16,16,128]{2,1,0:T(8,128)(2,1)S(1)}, bf16[16,16,128]{2,1,0:T(8,128)(2,1)S(1)}, u32[]{:S(2)}, u32[]{:S(2)}) %collective-permute-start.27) | collective-permute-done | bytes 65568 | tf_op jit(solution)/shard_map/ppermute | solution.py:24
  130.5 2.2 %collective-permute-start.29 = (bf16[16,16,128]{2,1,0:T(8,128)(2,1)S(1)}, bf16[16,16,128]{2,1,0:T(8,128)(2,1)S(1)}, u32[]{:S(2)}, u32[]{:S(2)}) collective-permute-start(bf16[16,16,128]{2,1,0:T(8,128)(2,1)S(1)} %get-tuple-element.71), channel_id=1, source_target_pairs={{0,16},{4,20},{8,24},{12,28},{16,0},{20,4},{24,8},{28,12},{1,17},{... | collective-permute-start | bytes 196616 | tf_op jit(solution)/shard_map/ppermute | solution.py:24
  133.9 2.4 %collective-permute-done.29.refs_8_ = bf16[16,16,128]{2,1,0:T(8,128)(2,1)S(1)} collective-permute-done((bf16[16,16,128]{2,1,0:T(8,128)(2,1)S(1)}, bf16[16,16,128]{2,1,0:T(8,128)(2,1)S(1)}, u32[]{:S(2)}, u32[]{:S(2)}) %collective-permute-start.29) | collective-permute-done | bytes 65568 | tf_op jit(solution)/shard_map/ppermute | solution.py:24
  136.3 3.2 %collective-permute-start.31 = (bf16[16,16,128]{2,1,0:T(8,128)(2,1)S(1)}, bf16[16,16,128]{2,1,0:T(8,128)(2,1)S(1)}, u32[]{:S(2)}, u32[]{:S(2)}) collective-permute-start(bf16[16,16,128]{2,1,0:T(8,128)(2,1)S(1)} %get-tuple-element.73), channel_id=1, source_target_pairs={{0,24},{4,28},{8,16},{12,20},{16,8},{20,12},{24,0},{28,4},{1,25},{... | collective-permute-start | bytes 196616 | tf_op jit(solution)/shard_map/ppermute | solution.py:24
  139.9 2.1 %shard_map.49.refs_0_ = bf16[2,256,512]{2,1,0:T(8,128)(2,1)S(1)} custom-call(bf16[256,2048]{1,0:T(8,128)(2,1)S(1)} %get-tuple-element.41.tok, bf16[3,2048,512]{2,1,0:T(8,128)(2,1)S(1)} %shard_map.47.w, f32[8,256]{1,0:T(8,128)S(1)} %get-tuple-element.42.rates, bf16[256,512]{1,0:T(8,128)(2,1)S(1)} %get-tuple-element.43.k_ref, ...), custom_call_target="tpu_custom_call" | custom-call | flops 1073741824 | bytes 7872512 | tf_op jit(solution)/shard_map/pallas_call | solution.py:73
  142.0 2.3 %collective-permute-done.32.refs_11_ = bf16[16,16,128]{2,1,0:T(8,128)(2,1)S(1)} collective-permute-done((bf16[16,16,128]{2,1,0:T(8,128)(2,1)S(1)}, bf16[16,16,128]{2,1,0:T(8,128)(2,1)S(1)}, u32[]{:S(2)}, u32[]{:S(2)}) %collective-permute-start.32) | collective-permute-done | bytes 65568 | tf_op jit(solution)/shard_map/ppermute | solution.py:24
  144.4 2.0 %shard_map.59 = bf16[256,2048]{1,0:T(8,128)(2,1)} custom-call(f32[256,128]{1,0:T(8,128)S(1)} %get-tuple-element.40.entry, f32[1,2048]{1,0:T(1,128)S(1)} %bitcast.5, bf16[2,256,512]{2,1,0:T(8,128)(2,1)S(1)} %shard_map.49.refs_0_, bf16[2,256,512]{2,1,0:T(8,128)(2,1)S(1)} %collective-permute-done.4.refs_1_, ...), custom_call_target="tpu_custom_call" | custom-call | bytes 2760704 | tf_op jit(solution)/shard_map/pallas_call | solution.py:73
  (52 shorter events, 19.9 us)
Async XLA Ops:
  0.0 48.6 %collective-permute-start = (bf16[256,2048]{1,0:T(8,128)(2,1)}, bf16[256,2048]{1,0:T(8,128)(2,1)S(1)}, u32[]{:S(2)}, u32[]{:S(2)}) collective-permute-start(bf16[256,2048]{1,0:T(8,128)(2,1)} %bitcast.6), channel_id=1, source_target_pairs={{0,1},{4,5},{8,9},{12,13},{16,17},{20,21},{24,25},{28,29},{1,2},{5... | collective-permute-start | bytes 3145736 | tf_op jit(solution)/shard_map/ppermute | solution.py:24
  3.1 50.8 %collective-permute-start.5 = (bf16[256,2048]{1,0:T(8,128)(2,1)}, bf16[256,2048]{1,0:T(8,128)(2,1)S(1)}, u32[]{:S(2)}, u32[]{:S(2)}) collective-permute-start(bf16[256,2048]{1,0:T(8,128)(2,1)} %bitcast.7), channel_id=1, source_target_pairs={{0,35},{4,39},{8,43},{12,47},{16,51},{20,55},{24,59},{28,63},{1,0}... | collective-permute-start | bytes 3145736 | tf_op jit(solution)/shard_map/ppermute | solution.py:24
  3.1 54.7 %collective-permute-start.2 = (bf16[256,2048]{1,0:T(8,128)(2,1)}, bf16[256,2048]{1,0:T(8,128)(2,1)S(1)}, u32[]{:S(2)}, u32[]{:S(2)}) collective-permute-start(bf16[256,2048]{1,0:T(8,128)(2,1)} %bitcast.8), channel_id=1, source_target_pairs={{0,2},{4,6},{8,10},{12,14},{16,18},{20,22},{24,26},{28,30},{1,35},... | collective-permute-start | bytes 3145736 | tf_op jit(solution)/shard_map/ppermute | solution.py:24
  5.1 43.5 %collective-permute-start.1 = (f32[8,256]{1,0:T(8,128)S(1)}, f32[8,256]{1,0:T(8,128)S(1)}, u32[]{:S(2)}, u32[]{:S(2)}) collective-permute-start(f32[8,256]{1,0:T(8,128)S(1)} %get-tuple-element.45), channel_id=1, source_target_pairs={{0,1},{4,5},{8,9},{12,13},{16,17},{20,21},{24,25},{28,29},{1,2},{5... | collective-permute-start | bytes 24584 | tf_op jit(solution)/shard_map/ppermute | solution.py:24
  8.7 49.2 %collective-permute-start.3 = (f32[8,256]{1,0:T(8,128)S(1)}, f32[8,256]{1,0:T(8,128)S(1)}, u32[]{:S(2)}, u32[]{:S(2)}) collective-permute-start(f32[8,256]{1,0:T(8,128)S(1)} %get-tuple-element.49), channel_id=1, source_target_pairs={{0,2},{4,6},{8,10},{12,14},{16,18},{20,22},{24,26},{28,30},{1,35},... | collective-permute-start | bytes 24584 | tf_op jit(solution)/shard_map/ppermute | solution.py:24
  48.6 5.3 %collective-permute-start.6 = (f32[8,256]{1,0:T(8,128)S(1)}, f32[8,256]{1,0:T(8,128)S(1)}, u32[]{:S(2)}, u32[]{:S(2)}) collective-permute-start(f32[8,256]{1,0:T(8,128)S(1)} %get-tuple-element.51), channel_id=1, source_target_pairs={{0,35},{4,39},{8,43},{12,47},{16,51},{20,55},{24,59},{28,63},{1,0}... | collective-permute-start | bytes 24584 | tf_op jit(solution)/shard_map/ppermute | solution.py:24
  50.4 11.1 %collective-permute-start.8 = (bf16[4,128,128]{2,1,0:T(8,128)(2,1)S(1)}, bf16[4,128,128]{2,1,0:T(8,128)(2,1)S(1)}, u32[]{:S(2)}, u32[]{:S(2)}) collective-permute-start(bf16[4,128,128]{2,1,0:T(8,128)(2,1)S(1)} %get-tuple-element.56), channel_id=1, source_target_pairs={{0,35},{4,39},{8,43},{12,47},{16,51},{20,55},{24,59},{28,63},{1,0}... | collective-permute-start | bytes 393224 | tf_op jit(solution)/shard_map/ppermute | solution.py:24
  55.7 5.8 %collective-permute-start.9 = (bf16[4,128,128]{2,1,0:T(8,128)(2,1)S(1)}, bf16[4,128,128]{2,1,0:T(8,128)(2,1)S(1)}, u32[]{:S(2)}, u32[]{:S(2)}) collective-permute-start(bf16[4,128,128]{2,1,0:T(8,128)(2,1)S(1)} %get-tuple-element.57), channel_id=1, source_target_pairs={{0,1},{4,5},{8,9},{12,13},{16,17},{20,21},{24,25},{28,29},{1,2},{5... | collective-permute-start | bytes 393224 | tf_op jit(solution)/shard_map/ppermute | solution.py:24
  59.6 6.1 %collective-permute-start.10 = (bf16[4,128,128]{2,1,0:T(8,128)(2,1)S(1)}, bf16[4,128,128]{2,1,0:T(8,128)(2,1)S(1)}, u32[]{:S(2)}, u32[]{:S(2)}) collective-permute-start(bf16[4,128,128]{2,1,0:T(8,128)(2,1)S(1)} %get-tuple-element.50.refs_0_), channel_id=1, source_target_pairs={{0,34},{4,38},{8,42},{12,46},{16,50},{20,54},{24,58},{28,62},{1,3}... | collective-permute-start | bytes 393224 | tf_op jit(solution)/shard_map/ppermute | solution.py:24
  65.8 7.4 %collective-permute-start.11 = (bf16[17,16,128]{2,1,0:T(8,128)(2,1)S(1)}, bf16[17,16,128]{2,1,0:T(8,128)(2,1)S(1)}, u32[]{:S(2)}, u32[]{:S(2)}) collective-permute-start(bf16[17,16,128]{2,1,0:T(8,128)(2,1)S(1)} %get-tuple-element.60), channel_id=1, source_target_pairs={{0,4},{4,0},{8,12},{12,8},{16,20},{20,16},{24,28},{28,24},{1,5},{5... | collective-permute-start | bytes 208904 | tf_op jit(solution)/shard_map/ppermute | solution.py:24
  65.9 10.1 %collective-permute-start.12 = (bf16[17,16,128]{2,1,0:T(8,128)(2,1)S(1)}, bf16[17,16,128]{2,1,0:T(8,128)(2,1)S(1)}, u32[]{:S(2)}, u32[]{:S(2)}) collective-permute-start(bf16[17,16,128]{2,1,0:T(8,128)(2,1)S(1)} %get-tuple-element.61), channel_id=1, source_target_pairs={{0,8},{4,12},{8,0},{12,4},{16,24},{20,28},{24,16},{28,20},{1,9},{5... | collective-permute-start | bytes 208904 | tf_op jit(solution)/shard_map/ppermute | solution.py:24
  69.7 8.7 %collective-permute-start.13 = (bf16[17,16,128]{2,1,0:T(8,128)(2,1)S(1)}, bf16[17,16,128]{2,1,0:T(8,128)(2,1)S(1)}, u32[]{:S(2)}, u32[]{:S(2)}) collective-permute-start(bf16[17,16,128]{2,1,0:T(8,128)(2,1)S(1)} %get-tuple-element.62), channel_id=1, source_target_pairs={{0,12},{4,8},{8,4},{12,0},{16,28},{20,24},{24,20},{28,16},{1,13},{... | collective-permute-start | bytes 208904 | tf_op jit(solution)/shard_map/ppermute | solution.py:24
  70.0 9.6 %collective-permute-start.14 = (bf16[17,16,128]{2,1,0:T(8,128)(2,1)S(1)}, bf16[17,16,128]{2,1,0:T(8,128)(2,1)S(1)}, u32[]{:S(2)}, u32[]{:S(2)}) collective-permute-start(bf16[17,16,128]{2,1,0:T(8,128)(2,1)S(1)} %get-tuple-element.63), channel_id=1, source_target_pairs={{0,16},{4,20},{8,24},{12,28},{16,0},{20,4},{24,8},{28,12},{1,17},{... | collective-permute-start | bytes 208904 | tf_op jit(solution)/shard_map/ppermute | solution.py:24
  73.0 8.7 %collective-permute-start.15 = (bf16[17,16,128]{2,1,0:T(8,128)(2,1)S(1)}, bf16[17,16,128]{2,1,0:T(8,128)(2,1)S(1)}, u32[]{:S(2)}, u32[]{:S(2)}) collective-permute-start(bf16[17,16,128]{2,1,0:T(8,128)(2,1)S(1)} %get-tuple-element.64), channel_id=1, source_target_pairs={{0,20},{4,16},{8,28},{12,24},{16,4},{20,0},{24,12},{28,8},{1,21},{... | collective-permute-start | bytes 208904 | tf_op jit(solution)/shard_map/ppermute | solution.py:24
  73.3 8.5 %collective-permute-start.16 = (bf16[17,16,128]{2,1,0:T(8,128)(2,1)S(1)}, bf16[17,16,128]{2,1,0:T(8,128)(2,1)S(1)}, u32[]{:S(2)}, u32[]{:S(2)}) collective-permute-start(bf16[17,16,128]{2,1,0:T(8,128)(2,1)S(1)} %get-tuple-element.65), channel_id=1, source_target_pairs={{0,24},{4,28},{8,16},{12,20},{16,8},{20,12},{24,0},{28,4},{1,25},{... | collective-permute-start | bytes 208904 | tf_op jit(solution)/shard_map/ppermute | solution.py:24
  76.0 5.8 %collective-permute-start.17 = (bf16[17,16,128]{2,1,0:T(8,128)(2,1)S(1)}, bf16[17,16,128]{2,1,0:T(8,128)(2,1)S(1)}, u32[]{:S(2)}, u32[]{:S(2)}) collective-permute-start(bf16[17,16,128]{2,1,0:T(8,128)(2,1)S(1)} %get-tuple-element.66), channel_id=1, source_target_pairs={{0,28},{4,24},{8,20},{12,16},{16,12},{20,8},{24,4},{28,0},{1,29},{... | collective-permute-start | bytes 208904 | tf_op jit(solution)/shard_map/ppermute | solution.py:24
  78.4 66.0 %collective-permute-start.4 = (bf16[2,256,512]{2,1,0:T(8,128)(2,1)S(1)}, bf16[2,256,512]{2,1,0:T(8,128)(2,1)S(1)}, u32[]{:S(2)}, u32[]{:S(2)}) collective-permute-start(bf16[2,256,512]{2,1,0:T(8,128)(2,1)S(1)} %shard_map.52), channel_id=1, source_target_pairs={{0,35},{4,39},{8,43},{12,47},{16,51},{20,55},{24,59},{28,63},{1,0}... | collective-permute-start | bytes 1572872 | tf_op jit(solution)/shard_map/ppermute | solution.py:24
  79.6 64.8 %collective-permute-start.7 = (bf16[2,256,512]{2,1,0:T(8,128)(2,1)S(1)}, bf16[2,256,512]{2,1,0:T(8,128)(2,1)S(1)}, u32[]{:S(2)}, u32[]{:S(2)}) collective-permute-start(bf16[2,256,512]{2,1,0:T(8,128)(2,1)S(1)} %shard_map.54), channel_id=1, source_target_pairs={{0,1},{4,5},{8,9},{12,13},{16,17},{20,21},{24,25},{28,29},{1,2},{5... | collective-permute-start | bytes 1572872 | tf_op jit(solution)/shard_map/ppermute | solution.py:24
  82.1 27.3 %collective-permute-start.19 = (bf16[17,16,128]{2,1,0:T(8,128)(2,1)S(1)}, bf16[17,16,128]{2,1,0:T(8,128)(2,1)S(1)}, u32[]{:S(2)}, u32[]{:S(2)}) collective-permute-start(bf16[17,16,128]{2,1,0:T(8,128)(2,1)S(1)} %shard_map.56.refs_0_.refs_8_), channel_id=1, source_target_pairs={{0,32},{4,36},{8,40},{12,44},{16,48},{20,52},{24,56},{28,60},{1,33... | collective-permute-start | bytes 208904 | tf_op jit(solution)/shard_map/ppermute | solution.py:24
  85.9 58.5 %collective-permute-start.18 = (bf16[2,256,512]{2,1,0:T(8,128)(2,1)S(1)}, bf16[2,256,512]{2,1,0:T(8,128)(2,1)S(1)}, u32[]{:S(2)}, u32[]{:S(2)}) collective-permute-start(bf16[2,256,512]{2,1,0:T(8,128)(2,1)S(1)} %shard_map.57), channel_id=1, source_target_pairs={{0,34},{4,38},{8,42},{12,46},{16,50},{20,54},{24,58},{28,62},{1,3}... | collective-permute-start | bytes 1572872 | tf_op jit(solution)/shard_map/ppermute | solution.py:24
  88.5 24.1 %collective-permute-start.20 = (bf16[17,16,128]{2,1,0:T(8,128)(2,1)S(1)}, bf16[17,16,128]{2,1,0:T(8,128)(2,1)S(1)}, u32[]{:S(2)}, u32[]{:S(2)}) collective-permute-start(bf16[17,16,128]{2,1,0:T(8,128)(2,1)S(1)} %shard_map.56.refs_0_.refs_8_), channel_id=1, source_target_pairs={{0,64},{4,68},{8,72},{12,76},{16,80},{20,84},{24,88},{28,92},{1,65... | collective-permute-start | bytes 208904 | tf_op jit(solution)/shard_map/ppermute | solution.py:24
  109.4 5.8 %collective-permute-start.22 = (bf16[17,16,128]{2,1,0:T(8,128)(2,1)S(1)}, bf16[17,16,128]{2,1,0:T(8,128)(2,1)S(1)}, u32[]{:S(2)}, u32[]{:S(2)}) collective-permute-start(bf16[17,16,128]{2,1,0:T(8,128)(2,1)S(1)} %shard_map.56.refs_0_.refs_8_), channel_id=1, source_target_pairs={{0,128},{4,132},{8,136},{12,140},{16,144},{20,148},{24,152},{28,15... | collective-permute-start | bytes 208904 | tf_op jit(solution)/shard_map/ppermute | solution.py:24
  112.6 5.5 %collective-permute-start.24 = (bf16[17,16,128]{2,1,0:T(8,128)(2,1)S(1)}, bf16[17,16,128]{2,1,0:T(8,128)(2,1)S(1)}, u32[]{:S(2)}, u32[]{:S(2)}) collective-permute-start(bf16[17,16,128]{2,1,0:T(8,128)(2,1)S(1)} %shard_map.56.refs_0_.refs_8_), channel_id=1, source_target_pairs={{0,192},{4,196},{8,200},{12,204},{16,208},{20,212},{24,216},{28,22... | collective-permute-start | bytes 208904 | tf_op jit(solution)/shard_map/ppermute | solution.py:24
  115.2 4.5 %collective-permute-start.21 = (bf16[17,16,128]{2,1,0:T(8,128)(2,1)S(1)}, bf16[17,16,128]{2,1,0:T(8,128)(2,1)S(1)}, u32[]{:S(2)}, u32[]{:S(2)}) collective-permute-start(bf16[17,16,128]{2,1,0:T(8,128)(2,1)S(1)} %collective-permute-done.19.refs_9_), channel_id=1, source_target_pairs={{0,64},{4,68},{8,72},{12,76},{16,80},{20,84},{24,88},{28,92},{1,65... | collective-permute-start | bytes 208904 | tf_op jit(solution)/shard_map/ppermute | solution.py:24
  118.1 5.8 %collective-permute-start.23 = (bf16[17,16,128]{2,1,0:T(8,128)(2,1)S(1)}, bf16[17,16,128]{2,1,0:T(8,128)(2,1)S(1)}, u32[]{:S(2)}, u32[]{:S(2)}) collective-permute-start(bf16[17,16,128]{2,1,0:T(8,128)(2,1)S(1)} %collective-permute-done.19.refs_9_), channel_id=1, source_target_pairs={{0,128},{4,132},{8,136},{12,140},{16,144},{20,148},{24,152},{28,15... | collective-permute-start | bytes 208904 | tf_op jit(solution)/shard_map/ppermute | solution.py:24
  119.7 5.5 %collective-permute-start.25 = (bf16[17,16,128]{2,1,0:T(8,128)(2,1)S(1)}, bf16[17,16,128]{2,1,0:T(8,128)(2,1)S(1)}, u32[]{:S(2)}, u32[]{:S(2)}) collective-permute-start(bf16[17,16,128]{2,1,0:T(8,128)(2,1)S(1)} %collective-permute-done.19.refs_9_), channel_id=1, source_target_pairs={{0,192},{4,196},{8,200},{12,204},{16,208},{20,212},{24,216},{28,22... | collective-permute-start | bytes 208904 | tf_op jit(solution)/shard_map/ppermute | solution.py:24
  125.8 4.8 %collective-permute-start.27 = (bf16[16,16,128]{2,1,0:T(8,128)(2,1)S(1)}, bf16[16,16,128]{2,1,0:T(8,128)(2,1)S(1)}, u32[]{:S(2)}, u32[]{:S(2)}) collective-permute-start(bf16[16,16,128]{2,1,0:T(8,128)(2,1)S(1)} %get-tuple-element.69), channel_id=1, source_target_pairs={{0,8},{4,12},{8,0},{12,4},{16,24},{20,28},{24,16},{28,20},{1,9},{5... | collective-permute-start | bytes 196616 | tf_op jit(solution)/shard_map/ppermute | solution.py:24
  127.0 5.7 %collective-permute-start.28 = (bf16[16,16,128]{2,1,0:T(8,128)(2,1)S(1)}, bf16[16,16,128]{2,1,0:T(8,128)(2,1)S(1)}, u32[]{:S(2)}, u32[]{:S(2)}) collective-permute-start(bf16[16,16,128]{2,1,0:T(8,128)(2,1)S(1)} %get-tuple-element.70), channel_id=1, source_target_pairs={{0,12},{4,8},{8,4},{12,0},{16,28},{20,24},{24,20},{28,16},{1,13},{... | collective-permute-start | bytes 196616 | tf_op jit(solution)/shard_map/ppermute | solution.py:24
  130.5 5.8 %collective-permute-start.29 = (bf16[16,16,128]{2,1,0:T(8,128)(2,1)S(1)}, bf16[16,16,128]{2,1,0:T(8,128)(2,1)S(1)}, u32[]{:S(2)}, u32[]{:S(2)}) collective-permute-start(bf16[16,16,128]{2,1,0:T(8,128)(2,1)S(1)} %get-tuple-element.71), channel_id=1, source_target_pairs={{0,16},{4,20},{8,24},{12,28},{16,0},{20,4},{24,8},{28,12},{1,17},{... | collective-permute-start | bytes 196616 | tf_op jit(solution)/shard_map/ppermute | solution.py:24
  132.8 6.7 %collective-permute-start.30 = (bf16[16,16,128]{2,1,0:T(8,128)(2,1)S(1)}, bf16[16,16,128]{2,1,0:T(8,128)(2,1)S(1)}, u32[]{:S(2)}, u32[]{:S(2)}) collective-permute-start(bf16[16,16,128]{2,1,0:T(8,128)(2,1)S(1)} %get-tuple-element.72), channel_id=1, source_target_pairs={{0,20},{4,16},{8,28},{12,24},{16,4},{20,0},{24,12},{28,8},{1,21},{... | collective-permute-start | bytes 196616 | tf_op jit(solution)/shard_map/ppermute | solution.py:24
  136.3 5.7 %collective-permute-start.31 = (bf16[16,16,128]{2,1,0:T(8,128)(2,1)S(1)}, bf16[16,16,128]{2,1,0:T(8,128)(2,1)S(1)}, u32[]{:S(2)}, u32[]{:S(2)}) collective-permute-start(bf16[16,16,128]{2,1,0:T(8,128)(2,1)S(1)} %get-tuple-element.73), channel_id=1, source_target_pairs={{0,24},{4,28},{8,16},{12,20},{16,8},{20,12},{24,0},{28,4},{1,25},{... | collective-permute-start | bytes 196616 | tf_op jit(solution)/shard_map/ppermute | solution.py:24
  139.5 4.9 %collective-permute-start.32 = (bf16[16,16,128]{2,1,0:T(8,128)(2,1)S(1)}, bf16[16,16,128]{2,1,0:T(8,128)(2,1)S(1)}, u32[]{:S(2)}, u32[]{:S(2)}) collective-permute-start(bf16[16,16,128]{2,1,0:T(8,128)(2,1)S(1)} %get-tuple-element.74), channel_id=1, source_target_pairs={{0,28},{4,24},{8,20},{12,16},{16,12},{20,8},{24,4},{28,0},{1,29},{... | collective-permute-start | bytes 196616 | tf_op jit(solution)/shard_map/ppermute | solution.py:24
  (3 other events, 60.5 us)

commit v3 on v2

--- a/solution.py
+++ b/solution.py
@@ -40,12 +40,29 @@
     return y, (z - 2 + 4 * (z % 2)) % 8, x, c
 
 
+def other(y, z, x, c):
+    return y, z, x, 1 - c
+
+
+def crossed(move):
+    return lambda *at: other(*move(*at))
+
+
+def along_x(d):
+    return lambda y, z, x, c: (y, z, x ^ d, c)
+
+
 def far(y, z, x, c):
     return y, (z + 4) % 8, x, c
 
 
 def along_y(d):
     return lambda y, z, x, c: (y ^ d, z, x, c)
+
+
+def exchange(parts, order, move):
+    got = {d: send(parts[d], move(d)) for d in order}
+    return [parts[0]] + [got[d] for d in range(1, len(parts))]
 
 
 def along_row(d):
@@ -140,7 +157,7 @@
 
 
 def states(tok, w, rates, *refs):
-    k_out, v_out, local = refs[-3:]
+    k_out, v_out, same, cross, local = refs[-5:]
     cum = running(rates[...])
     tail = jnp.exp(cum[:, 255:256] - cum).T
     for j in range(2):
@@ -154,6 +171,9 @@
             head = 2 * j + h
             scaled = (k[:, cols].astype(F32) * tail[:, head : head + 1]).astype(BF16)
             local[head] = dot(scaled, v[:, cols], ((0,), (0,))).astype(BF16)
+    core = lax.rem(place()[0], 2)
+    same[...] = local[:, pl.ds(pl.multiple_of(core * 64, 64), 64), :]
+    cross[...] = local[:, pl.ds(pl.multiple_of((1 - core) * 64, 64), 64), :]
 
 
 def insides(tok, w, rates, k_ref, v_ref, *refs):
@@ -175,20 +195,29 @@
             out[1, :, cols] = jnp.dot(weights, v_ref[:, cols], preferred_element_type=F32).astype(BF16)
 
 
-def deal(s0, s1, s2, s3, total, *outs):
+def deal(*refs):
+    own, partner, (total, partner_total), outs = refs[:4], refs[4:8], refs[8:10], refs[10:]
     p, _ = place()
-    for d in range(8):
-        rows = pl.ds(pl.multiple_of(jnp.bitwise_xor(p, d) * 16, 16), 16)
-        for i, s in enumerate((s0, s1, s2, s3)):
-            outs[d][4 * i : 4 * i + 4] = s[:, rows, :]
-        outs[d][16] = total[...]
+    x, core = lax.div(p, 2), lax.rem(p, 2)
+    for d in range(4):
+        rows = pl.ds(pl.multiple_of(jnp.bitwise_xor(x, d) * 16, 16), 16)
+        for block, parts, log in ((core, own, total), (1 - core, partner, partner_total)):
+            for i, s in enumerate(parts):
+                outs[d][block, 4 * i : 4 * i + 4] = s[:, rows, :]
+            outs[d][block, 16] = log[...]
+
+
+def arrange(natural, pieces):
+    x = lax.div(place()[0], 2)
+    for d in range(4):
+        at = jnp.bitwise_xor(x, d) * 2
+        for core in range(2):
+            natural[at + core] = pieces[d][core]
 
 
 def row_total(*refs):
-    pieces, out, natural, decay = refs[:8], refs[8], refs[9], refs[10]
-    p, _ = place()
-    for d in range(8):
-        natural[jnp.bitwise_xor(p, d)] = pieces[d][...]
+    pieces, out, natural, decay = refs[:4], refs[4], refs[5], refs[6]
+    arrange(natural, pieces)
     logs = jnp.zeros((16, 1), F32)
     for e in range(8):
         own = unpack(natural[e, 16])
@@ -202,11 +231,15 @@
     out[16] = pack(logs)
 
 
-def carry(*refs):
-    pieces, totals, outs, natural, rows, decay, row_decay = refs[:8], refs[8:16], refs[16:24], *refs[24:]
+def mark(total, out):
+    out[...] = total[16]
+
+
+def carry(_, *refs):
+    pieces, totals, outs, natural, rows, decay, row_decay = refs[:4], refs[4:12], refs[12:20], *refs[20:]
     p, r = place()
+    arrange(natural, pieces)
     for d in range(8):
-        natural[jnp.bitwise_xor(p, d)] = pieces[d][...]
         rows[jnp.bitwise_xor(r, d)] = totals[d][...]
     for e in range(8):
         decay[e] = jnp.broadcast_to(jnp.exp(unpack(natural[e, 16])), (16, 128))
@@ -228,8 +261,9 @@
     p, _ = place()
     f = lax.axis_index("fsdp")
     for d in range(8):
-        rows = pl.ds(pl.multiple_of(jnp.bitwise_xor(p, d) * 16, 16), 16)
-        memory[:, rows, :] = pieces[d][...]
+        sender = jnp.bitwise_xor(p, d)
+        piece = lax.rem(sender, 2) * 4 + lax.div(sender, 2)
+        memory[:, pl.ds(pl.multiple_of(piece * 16, 16), 16), :] = pieces[d][...]
     squares = jnp.zeros((out.shape[0], 128), F32)
     for i, shift in enumerate(SHIFTS):
         group = lax.rem(f + shift, 4)
@@ -247,6 +281,7 @@
     tok = tokens[0]
     n, d = tok.shape
     piece = ((17, 16, 128), BF16)
+    pair = ((2, 17, 16, 128), BF16)
     slots = ((8, 17, 16, 128), BF16)
     factor = ((8, 16, 128), F32)
 
@@ -264,34 +299,46 @@
     weight = call(load, [(qkv_weight.shape, BF16)], qkv_weight, far=1)[0]
 
     half = ((n, 512), BF16)
+    quarter = ((4, 64, 128), BF16)
     made = []
     for t, a in zip(toks, rates):
         after = (made[0][2],) if made else ()
         made.append(
-            call(states, [half, half, ((4, 128, 128), BF16)], t, weight, a, *after, flops=1 << 30)
+            call(
+                states,
+                [half, half, quarter, quarter],
+                t,
+                weight,
+                a,
+                *after,
+                flops=1 << 30,
+                scratch=[((4, 128, 128), BF16)],
+            )
         )
-    owned = [made[0][2]]
-    for s, m in enumerate(back_moves):
-        owned.append(send(made[s + 1][2], m))
-    pieces = call(deal, [piece] * 8, *owned, total)
-    pieces = [pieces[0]] + [send(pieces[e], along_row(e)) for e in range(1, 8)]
+    own, partner = [made[0][2]], [send(made[0][3], other)]
+    partner_total = send(total, other)
+    for i, m in enumerate(back_moves):
+        own.append(send(made[i + 1][2], m))
+        partner.append(send(made[i + 1][3], crossed(m)))
+    pieces = call(deal, [pair] * 4, *own, *partner, total, partner_total)
+    pieces = exchange(pieces, (2, 1, 3), along_x)
     own_total = call(row_total, [piece], *pieces, scratch=[slots, factor])[0]
 
-    after = ((), (made[3][2],), (made[3][2],), (own_total,))
     parts = []
     for i in range(4):
         out = ((2, n, 512), BF16)
-        parts += call(insides, [out], toks[i], weight, rates[i], *made[i][:2], *after[i], flops=1 << 30)
+        parts += call(insides, [out], toks[i], weight, rates[i], *made[i][:2], flops=1 << 30)
     for i, m in enumerate(back_moves):
         parts[i + 1] = send(parts[i + 1], m)
 
+    marked = call(mark, [((16, 128), BF16)], own_total)[0]
     far_total = send(own_total, far)
     near = [send(own_total, along_y(e)) for e in range(1, 4)]
     totals = [own_total, far_total]
     for e in range(1, 4):
         totals += [near[e - 1], send(far_total, along_y(e))]
-    carried = call(carry, [((16, 16, 128), BF16)] * 8, *pieces, *totals, scratch=[slots] * 2 + [factor] * 2)
-    carried = [carried[0]] + [send(carried[e], along_row(e)) for e in range(1, 8)]
+    carried = call(carry, [((16, 16, 128), BF16)] * 8, marked, *pieces, *totals, scratch=[slots] * 2 + [factor] * 2)
+    carried = exchange(carried, (4, 5, 2, 3, 6, 7, 1), along_row)
     out = call(
         final,
         [((n, d), BF16)],

time: 147 us -> 137 us (0.932)
  the two profiles are of different devices: /device:TPU:96 before, /device:TPU:64 now
where the time goes in v3:
time: 137 us
  waiting for transfers between devices  60.5 us (44%)
  starting transfers between devices  53.1 us (39%)
  Pallas kernels  22.6 us (16%)
    ppermute x34, waiting for transfers between devices, send(): return lax.ppermute(a, BOTH, pairs(move))  60.5 us
    ppermute x34, starting transfers between devices, send(): return lax.ppermute(a, BOTH, pairs(move))  53.1 us
    pallas_call x15, Pallas kernels, call(): pl.pallas_call(kernel, in_specs=[VMEM] * near + [pl.BlockSpec(memory_spac...  22.6 us
  transfers between devices with their start and end apart: 34, of which 14 were waited for; matrix products, arithmetic and copies ran while one was open for 0% of the time, Pallas kernels for 15%

profile of v3, /device:TPU:64, one launch (start us, length us, event | category | flops | bytes accessed | tf_op | source)
XLA Modules:
  0.0 137.1 jit_solution(4210989975675112418)
XLA Ops:
  0.0 1.9 %collective-permute-start = (bf16[256,2048]{1,0:T(8,128)(2,1)}, bf16[256,2048]{1,0:T(8,128)(2,1)S(1)}, u32[]{:S(2)}, u32[]{:S(2)}) collective-permute-start(bf16[256,2048]{1,0:T(8,128)(2,1)} %bitcast.6), channel_id=1, source_target_pairs={{0,1},{4,5},{8,9},{12,13},{16,17},{20,21},{24,25},{28,29},{1,2},{5... | collective-permute-start | bytes 3145736 | tf_op jit(solution)/shard_map/ppermute | solution.py:24
  2.0 5.7 %collective-permute-start.6 = (bf16[256,2048]{1,0:T(8,128)(2,1)}, bf16[256,2048]{1,0:T(8,128)(2,1)S(1)}, u32[]{:S(2)}, u32[]{:S(2)}) collective-permute-start(bf16[256,2048]{1,0:T(8,128)(2,1)} %bitcast.8), channel_id=1, source_target_pairs={{0,2},{4,6},{8,10},{12,14},{16,18},{20,22},{24,26},{28,30},{1,35},... | collective-permute-start | bytes 3145736 | tf_op jit(solution)/shard_map/ppermute | solution.py:24
  9.8 2.0 %collective-permute-start.4 = (f32[8,256]{1,0:T(8,128)S(1)}, f32[8,256]{1,0:T(8,128)S(1)}, u32[]{:S(2)}, u32[]{:S(2)}) collective-permute-start(f32[8,256]{1,0:T(8,128)S(1)} %get-tuple-element.49), channel_id=1, source_target_pairs={{0,35},{4,39},{8,43},{12,47},{16,51},{20,55},{24,59},{28,63},{1,0}... | collective-permute-start | bytes 24584 | tf_op jit(solution)/shard_map/ppermute | solution.py:24
  11.8 2.8 %shard_map.47.w = bf16[3,2048,512]{2,1,0:T(8,128)(2,1)S(1)} custom-call(bf16[3,2048,512]{2,1,0:T(8,128)(2,1)} %w.1), custom_call_target="tpu_custom_call" | custom-call | bytes 6291456 | tf_op jit(solution)/shard_map/pallas_call | solution.py:90
  14.6 1.8 %shard_map.48 = (bf16[256,512]{1,0:T(8,128)(2,1)S(1)}, bf16[256,512]{1,0:T(8,128)(2,1)S(1)}, bf16[4,64,128]{2,1,0:T(8,128)(2,1)S(1)}, bf16[4,64,128]{2,1,0:T(8,128)(2,1)S(1)}) custom-call(bf16[256,2048]{1,0:T(8,128)(2,1)S(1)} %get-tuple-element.41.tok, bf16[3,2048,512]{2,1,0:T(8,128)(2,1)S(1)} %shard_map.47.w, f32[8,256]{1,0:T(8,128)S(1)} %get-tuple-element.42.rates), custom_call_target="tpu_custom_call" | custom-call | flops 1073741824 | bytes 7348224 | tf_op jit(solution)/shard_map/pallas_call | solution.py:90
  16.4 31.4 %collective-permute-done.1.rates = f32[8,256]{1,0:T(8,128)S(1)} collective-permute-done((f32[8,256]{1,0:T(8,128)S(1)}, f32[8,256]{1,0:T(8,128)S(1)}, u32[]{:S(2)}, u32[]{:S(2)}) %collective-permute-start.1) | collective-permute-done | bytes 8224 | tf_op jit(solution)/shard_map/ppermute | solution.py:24
  47.8 5.7 %collective-permute-start.7 = (f32[8,256]{1,0:T(8,128)S(1)}, f32[8,256]{1,0:T(8,128)S(1)}, u32[]{:S(2)}, u32[]{:S(2)}) collective-permute-start(f32[8,256]{1,0:T(8,128)S(1)} %get-tuple-element.52), channel_id=1, source_target_pairs={{0,2},{4,6},{8,10},{12,14},{16,18},{20,22},{24,26},{28,30},{1,35},... | collective-permute-start | bytes 24584 | tf_op jit(solution)/shard_map/ppermute | solution.py:24
  53.5 1.8 %shard_map.50 = (bf16[256,512]{1,0:T(8,128)(2,1)S(1)}, bf16[256,512]{1,0:T(8,128)(2,1)S(1)}, bf16[4,64,128]{2,1,0:T(8,128)(2,1)S(1)}, bf16[4,64,128]{2,1,0:T(8,128)(2,1)S(1)}) custom-call(bf16[256,2048]{1,0:T(8,128)(2,1)S(1)} %collective-permute-done.tok, bf16[3,2048,512]{2,1,0:T(8,128)(2,1)S(1)} %shard_map.47.w, f32[8,256]{1,0:T(8,128)S(1)} %collective-permute-done.1.rates, ...), custom_call_target="tpu_custom_call" | custom-call | flops 1073741824 | bytes 7413760 | tf_op jit(solution)/shard_map/pallas_call | solution.py:90
  55.9 1.8 %shard_map.52 = (bf16[256,512]{1,0:T(8,128)(2,1)S(1)}, bf16[256,512]{1,0:T(8,128)(2,1)S(1)}, bf16[4,64,128]{2,1,0:T(8,128)(2,1)S(1)}, bf16[4,64,128]{2,1,0:T(8,128)(2,1)S(1)}) custom-call(bf16[256,2048]{1,0:T(8,128)(2,1)S(1)} %collective-permute-done.3.tok, bf16[3,2048,512]{2,1,0:T(8,128)(2,1)S(1)} %shard_map.47.w, ...), custom_call_target="tpu_custom_call" | custom-call | flops 1073741824 | bytes 7413760 | tf_op jit(solution)/shard_map/pallas_call | solution.py:90
  57.7 2.3 %collective-permute-start.10 = (bf16[4,64,128]{2,1,0:T(8,128)(2,1)S(1)}, bf16[4,64,128]{2,1,0:T(8,128)(2,1)S(1)}, u32[]{:S(2)}, u32[]{:S(2)}) collective-permute-start(bf16[4,64,128]{2,1,0:T(8,128)(2,1)S(1)} %get-tuple-element.56), channel_id=1, source_target_pairs={{0,1},{4,5},{8,9},{12,13},{16,17},{20,21},{24,25},{28,29},{1,2},{5... | collective-permute-start | bytes 196616 | tf_op jit(solution)/shard_map/ppermute | solution.py:24
  60.0 1.8 %shard_map.54 = (bf16[256,512]{1,0:T(8,128)(2,1)S(1)}, bf16[256,512]{1,0:T(8,128)(2,1)S(1)}, bf16[4,64,128]{2,1,0:T(8,128)(2,1)S(1)}, bf16[4,64,128]{2,1,0:T(8,128)(2,1)S(1)}) custom-call(bf16[256,2048]{1,0:T(8,128)(2,1)S(1)} %collective-permute-done.6.tok, bf16[3,2048,512]{2,1,0:T(8,128)(2,1)S(1)} %shard_map.47.w, ...), custom_call_target="tpu_custom_call" | custom-call | flops 1073741824 | bytes 7413760 | tf_op jit(solution)/shard_map/pallas_call | solution.py:90
  63.7 2.1 %collective-permute-start.15 = (bf16[4,64,128]{2,1,0:T(8,128)(2,1)S(1)}, bf16[4,64,128]{2,1,0:T(8,128)(2,1)S(1)}, u32[]{:S(2)}, u32[]{:S(2)}) collective-permute-start(bf16[4,64,128]{2,1,0:T(8,128)(2,1)S(1)} %get-tuple-element.61), channel_id=1, source_target_pairs={{0,38},{4,34},{8,46},{12,42},{16,54},{20,50},{24,62},{28,58},{1,7}... | collective-permute-start | bytes 196616 | tf_op jit(solution)/shard_map/ppermute | solution.py:24
  65.8 2.4 %collective-permute-done.11.refs_3_ = bf16[4,64,128]{2,1,0:T(8,128)(2,1)S(1)} collective-permute-done((bf16[4,64,128]{2,1,0:T(8,128)(2,1)S(1)}, bf16[4,64,128]{2,1,0:T(8,128)(2,1)S(1)}, u32[]{:S(2)}, u32[]{:S(2)}) %collective-permute-start.11) | collective-permute-done | bytes 65568 | tf_op jit(solution)/shard_map/ppermute | solution.py:24
  68.2 1.7 %collective-permute-done.15.refs_7_ = bf16[4,64,128]{2,1,0:T(8,128)(2,1)S(1)} collective-permute-done((bf16[4,64,128]{2,1,0:T(8,128)(2,1)S(1)}, bf16[4,64,128]{2,1,0:T(8,128)(2,1)S(1)}, u32[]{:S(2)}, u32[]{:S(2)}) %collective-permute-start.15) | collective-permute-done | bytes 65568 | tf_op jit(solution)/shard_map/ppermute | solution.py:24
  71.6 2.7 %collective-permute-start.18 = (bf16[2,17,16,128]{3,2,1,0:T(8,128)(2,1)S(1)}, bf16[2,17,16,128]{3,2,1,0:T(8,128)(2,1)S(1)}, u32[]{:S(2)}, u32[]{:S(2)}) collective-permute-start(bf16[2,17,16,128]{3,2,1,0:T(8,128)(2,1)S(1)} %get-tuple-element.65), channel_id=1, source_target_pairs={{0,16},{4,20},{8,24},{12,28},{16,0},{20,4},{24,8},{28,12},{1,17},{... | collective-permute-start | bytes 417800 | tf_op jit(solution)/shard_map/ppermute | solution.py:24
  74.8 2.1 %shard_map.51 = bf16[2,256,512]{2,1,0:T(8,128)(2,1)S(1)} custom-call(bf16[256,2048]{1,0:T(8,128)(2,1)S(1)} %collective-permute-done.tok, bf16[3,2048,512]{2,1,0:T(8,128)(2,1)S(1)} %shard_map.47.w, f32[8,256]{1,0:T(8,128)S(1)} %collective-permute-done.1.rates, bf16[256,512]{1,0:T(8,128)(2,1)S(1)} %get-tuple-element.47.k_ref, ...), custom_call_target="tpu_custom_call" | custom-call | flops 1073741824 | bytes 7872512 | tf_op jit(solution)/shard_map/pallas_call | solution.py:90
  78.4 2.1 %shard_map.53 = bf16[2,256,512]{2,1,0:T(8,128)(2,1)S(1)} custom-call(bf16[256,2048]{1,0:T(8,128)(2,1)S(1)} %collective-permute-done.3.tok, bf16[3,2048,512]{2,1,0:T(8,128)(2,1)S(1)} %shard_map.47.w, f32[8,256]{1,0:T(8,128)S(1)} %collective-permute-done.4.rates, bf16[256,512]{1,0:T(8,128)(2,1)S(1)} %get-tuple-element.50.k_ref, ...), custom_call_target="tpu_custom_call" | custom-call | flops 1073741824 | bytes 7872512 | tf_op jit(solution)/shard_map/pallas_call | solution.py:90
  81.3 2.2 %collective-permute-done.19.refs_3_ = bf16[2,17,16,128]{3,2,1,0:T(8,128)(2,1)S(1)} collective-permute-done((bf16[2,17,16,128]{3,2,1,0:T(8,128)(2,1)S(1)}, bf16[2,17,16,128]{3,2,1,0:T(8,128)(2,1)S(1)}, u32[]{:S(2)}, u32[]{:S(2)}) %collective-permute-start.19) | collective-permute-done | bytes 139296 | tf_op jit(solution)/shard_map/ppermute | solution.py:24
  83.8 3.2 %collective-permute-start.20 = (bf16[17,16,128]{2,1,0:T(8,128)(2,1)S(1)}, bf16[17,16,128]{2,1,0:T(8,128)(2,1)S(1)}, u32[]{:S(2)}, u32[]{:S(2)}) collective-permute-start(bf16[17,16,128]{2,1,0:T(8,128)(2,1)S(1)} %shard_map.57.total.refs_4_), channel_id=1, source_target_pairs={{0,32},{4,36},{8,40},{12,44},{16,48},{20,52},{24,56},{28,60},{1,33... | collective-permute-start | bytes 208904 | tf_op jit(solution)/shard_map/ppermute | solution.py:24
  87.0 2.1 %shard_map.55 = bf16[2,256,512]{2,1,0:T(8,128)(2,1)S(1)} custom-call(bf16[256,2048]{1,0:T(8,128)(2,1)S(1)} %collective-permute-done.6.tok, bf16[3,2048,512]{2,1,0:T(8,128)(2,1)S(1)} %shard_map.47.w, f32[8,256]{1,0:T(8,128)S(1)} %collective-permute-done.7.rates, bf16[256,512]{1,0:T(8,128)(2,1)S(1)} %get-tuple-element.53.k_ref, ...), custom_call_target="tpu_custom_call" | custom-call | flops 1073741824 | bytes 7872512 | tf_op jit(solution)/shard_map/pallas_call | solution.py:90
  91.9 7.7 %collective-permute-done.20.refs_5_ = bf16[17,16,128]{2,1,0:T(8,128)(2,1)S(1)} collective-permute-done((bf16[17,16,128]{2,1,0:T(8,128)(2,1)S(1)}, bf16[17,16,128]{2,1,0:T(8,128)(2,1)S(1)}, u32[]{:S(2)}, u32[]{:S(2)}) %collective-permute-start.20) | collective-permute-done | bytes 69664 | tf_op jit(solution)/shard_map/ppermute | solution.py:24
  99.6 3.2 %collective-permute-start.23 = (bf16[17,16,128]{2,1,0:T(8,128)(2,1)S(1)}, bf16[17,16,128]{2,1,0:T(8,128)(2,1)S(1)}, u32[]{:S(2)}, u32[]{:S(2)}) collective-permute-start(bf16[17,16,128]{2,1,0:T(8,128)(2,1)S(1)} %shard_map.57.total.refs_4_), channel_id=1, source_target_pairs={{0,128},{4,132},{8,136},{12,140},{16,144},{20,148},{24,152},{28,15... | collective-permute-start | bytes 208904 | tf_op jit(solution)/shard_map/ppermute | solution.py:24
  105.4 2.4 %collective-permute-start.22 = (bf16[17,16,128]{2,1,0:T(8,128)(2,1)S(1)}, bf16[17,16,128]{2,1,0:T(8,128)(2,1)S(1)}, u32[]{:S(2)}, u32[]{:S(2)}) collective-permute-start(bf16[17,16,128]{2,1,0:T(8,128)(2,1)S(1)} %collective-permute-done.20.refs_5_), channel_id=1, source_target_pairs={{0,64},{4,68},{8,72},{12,76},{16,80},{20,84},{24,88},{28,92},{1,65... | collective-permute-start | bytes 208904 | tf_op jit(solution)/shard_map/ppermute | solution.py:24
  110.1 2.6 %collective-permute-start.26 = (bf16[17,16,128]{2,1,0:T(8,128)(2,1)S(1)}, bf16[17,16,128]{2,1,0:T(8,128)(2,1)S(1)}, u32[]{:S(2)}, u32[]{:S(2)}) collective-permute-start(bf16[17,16,128]{2,1,0:T(8,128)(2,1)S(1)} %collective-permute-done.20.refs_5_), channel_id=1, source_target_pairs={{0,192},{4,196},{8,200},{12,204},{16,208},{20,212},{24,216},{28,22... | collective-permute-start | bytes 208904 | tf_op jit(solution)/shard_map/ppermute | solution.py:24
  112.7 2.5 %collective-permute-done.24.refs_9_ = bf16[17,16,128]{2,1,0:T(8,128)(2,1)S(1)} collective-permute-done((bf16[17,16,128]{2,1,0:T(8,128)(2,1)S(1)}, bf16[17,16,128]{2,1,0:T(8,128)(2,1)S(1)}, u32[]{:S(2)}, u32[]{:S(2)}) %collective-permute-start.24) | collective-permute-done | bytes 69664 | tf_op jit(solution)/shard_map/ppermute | solution.py:24
  118.3 2.9 %collective-permute-done.28.refs_6_ = bf16[16,16,128]{2,1,0:T(8,128)(2,1)S(1)} collective-permute-done((bf16[16,16,128]{2,1,0:T(8,128)(2,1)S(1)}, bf16[16,16,128]{2,1,0:T(8,128)(2,1)S(1)}, u32[]{:S(2)}, u32[]{:S(2)}) %collective-permute-start.28) | collective-permute-done | bytes 65568 | tf_op jit(solution)/shard_map/ppermute | solution.py:24
  121.2 2.2 %collective-permute-start.30 = (bf16[16,16,128]{2,1,0:T(8,128)(2,1)S(1)}, bf16[16,16,128]{2,1,0:T(8,128)(2,1)S(1)}, u32[]{:S(2)}, u32[]{:S(2)}) collective-permute-start(bf16[16,16,128]{2,1,0:T(8,128)(2,1)S(1)} %get-tuple-element.71), channel_id=1, source_target_pairs={{0,16},{4,20},{8,24},{12,28},{16,0},{20,4},{24,8},{28,12},{1,17},{... | collective-permute-start | bytes 196616 | tf_op jit(solution)/shard_map/ppermute | solution.py:24
  124.6 2.4 %collective-permute-done.30.refs_8_ = bf16[16,16,128]{2,1,0:T(8,128)(2,1)S(1)} collective-permute-done((bf16[16,16,128]{2,1,0:T(8,128)(2,1)S(1)}, bf16[16,16,128]{2,1,0:T(8,128)(2,1)S(1)}, u32[]{:S(2)}, u32[]{:S(2)}) %collective-permute-start.30) | collective-permute-done | bytes 65568 | tf_op jit(solution)/shard_map/ppermute | solution.py:24
  127.0 3.2 %collective-permute-start.32 = (bf16[16,16,128]{2,1,0:T(8,128)(2,1)S(1)}, bf16[16,16,128]{2,1,0:T(8,128)(2,1)S(1)}, u32[]{:S(2)}, u32[]{:S(2)}) collective-permute-start(bf16[16,16,128]{2,1,0:T(8,128)(2,1)S(1)} %get-tuple-element.73), channel_id=1, source_target_pairs={{0,24},{4,28},{8,16},{12,20},{16,8},{20,12},{24,0},{28,4},{1,25},{... | collective-permute-start | bytes 196616 | tf_op jit(solution)/shard_map/ppermute | solution.py:24
  130.6 2.1 %shard_map.49.refs_0_ = bf16[2,256,512]{2,1,0:T(8,128)(2,1)S(1)} custom-call(bf16[256,2048]{1,0:T(8,128)(2,1)S(1)} %get-tuple-element.41.tok, bf16[3,2048,512]{2,1,0:T(8,128)(2,1)S(1)} %shard_map.47.w, f32[8,256]{1,0:T(8,128)S(1)} %get-tuple-element.42.rates, bf16[256,512]{1,0:T(8,128)(2,1)S(1)} %get-tuple-element.43.k_ref, ...), custom_call_target="tpu_custom_call" | custom-call | flops 1073741824 | bytes 7872512 | tf_op jit(solution)/shard_map/pallas_call | solution.py:90
  132.8 2.3 %collective-permute-done.33.refs_11_ = bf16[16,16,128]{2,1,0:T(8,128)(2,1)S(1)} collective-permute-done((bf16[16,16,128]{2,1,0:T(8,128)(2,1)S(1)}, bf16[16,16,128]{2,1,0:T(8,128)(2,1)S(1)}, u32[]{:S(2)}, u32[]{:S(2)}) %collective-permute-start.33) | collective-permute-done | bytes 65568 | tf_op jit(solution)/shard_map/ppermute | solution.py:24
  135.1 2.0 %shard_map.60 = bf16[256,2048]{1,0:T(8,128)(2,1)} custom-call(f32[256,128]{1,0:T(8,128)S(1)} %get-tuple-element.40.entry, f32[1,2048]{1,0:T(1,128)S(1)} %bitcast.5, bf16[2,256,512]{2,1,0:T(8,128)(2,1)S(1)} %shard_map.49.refs_0_, bf16[2,256,512]{2,1,0:T(8,128)(2,1)S(1)} %collective-permute-done.2.refs_1_, ...), custom_call_target="tpu_custom_call" | custom-call | bytes 2760704 | tf_op jit(solution)/shard_map/pallas_call | solution.py:90
  (55 shorter events, 21.6 us)
Async XLA Ops:
  0.0 53.5 %collective-permute-start = (bf16[256,2048]{1,0:T(8,128)(2,1)}, bf16[256,2048]{1,0:T(8,128)(2,1)S(1)}, u32[]{:S(2)}, u32[]{:S(2)}) collective-permute-start(bf16[256,2048]{1,0:T(8,128)(2,1)} %bitcast.6), channel_id=1, source_target_pairs={{0,1},{4,5},{8,9},{12,13},{16,17},{20,21},{24,25},{28,29},{1,2},{5... | collective-permute-start | bytes 3145736 | tf_op jit(solution)/shard_map/ppermute | solution.py:24
  1.9 54.0 %collective-permute-start.3 = (bf16[256,2048]{1,0:T(8,128)(2,1)}, bf16[256,2048]{1,0:T(8,128)(2,1)S(1)}, u32[]{:S(2)}, u32[]{:S(2)}) collective-permute-start(bf16[256,2048]{1,0:T(8,128)(2,1)} %bitcast.7), channel_id=1, source_target_pairs={{0,35},{4,39},{8,43},{12,47},{16,51},{20,55},{24,59},{28,63},{1,0}... | collective-permute-start | bytes 3145736 | tf_op jit(solution)/shard_map/ppermute | solution.py:24
  2.0 57.9 %collective-permute-start.6 = (bf16[256,2048]{1,0:T(8,128)(2,1)}, bf16[256,2048]{1,0:T(8,128)(2,1)S(1)}, u32[]{:S(2)}, u32[]{:S(2)}) collective-permute-start(bf16[256,2048]{1,0:T(8,128)(2,1)} %bitcast.8), channel_id=1, source_target_pairs={{0,2},{4,6},{8,10},{12,14},{16,18},{20,22},{24,26},{28,30},{1,35},... | collective-permute-start | bytes 3145736 | tf_op jit(solution)/shard_map/ppermute | solution.py:24
  9.7 38.1 %collective-permute-start.1 = (f32[8,256]{1,0:T(8,128)S(1)}, f32[8,256]{1,0:T(8,128)S(1)}, u32[]{:S(2)}, u32[]{:S(2)}) collective-permute-start(f32[8,256]{1,0:T(8,128)S(1)} %get-tuple-element.45), channel_id=1, source_target_pairs={{0,1},{4,5},{8,9},{12,13},{16,17},{20,21},{24,25},{28,29},{1,2},{5... | collective-permute-start | bytes 24584 | tf_op jit(solution)/shard_map/ppermute | solution.py:24
  9.8 45.5 %collective-permute-start.4 = (f32[8,256]{1,0:T(8,128)S(1)}, f32[8,256]{1,0:T(8,128)S(1)}, u32[]{:S(2)}, u32[]{:S(2)}) collective-permute-start(f32[8,256]{1,0:T(8,128)S(1)} %get-tuple-element.49), channel_id=1, source_target_pairs={{0,35},{4,39},{8,43},{12,47},{16,51},{20,55},{24,59},{28,63},{1,0}... | collective-permute-start | bytes 24584 | tf_op jit(solution)/shard_map/ppermute | solution.py:24
  47.8 9.9 %collective-permute-start.7 = (f32[8,256]{1,0:T(8,128)S(1)}, f32[8,256]{1,0:T(8,128)S(1)}, u32[]{:S(2)}, u32[]{:S(2)}) collective-permute-start(f32[8,256]{1,0:T(8,128)S(1)} %get-tuple-element.52), channel_id=1, source_target_pairs={{0,2},{4,6},{8,10},{12,14},{16,18},{20,22},{24,26},{28,30},{1,35},... | collective-permute-start | bytes 24584 | tf_op jit(solution)/shard_map/ppermute | solution.py:24
  53.5 9.1 %collective-permute-start.12 = (bf16[4,64,128]{2,1,0:T(8,128)(2,1)S(1)}, bf16[4,64,128]{2,1,0:T(8,128)(2,1)S(1)}, u32[]{:S(2)}, u32[]{:S(2)}) collective-permute-start(bf16[4,64,128]{2,1,0:T(8,128)(2,1)S(1)} %get-tuple-element.58), channel_id=1, source_target_pairs={{0,4},{4,0},{8,12},{12,8},{16,20},{20,16},{24,28},{28,24},{1,5},{5... | collective-permute-start | bytes 196616 | tf_op jit(solution)/shard_map/ppermute | solution.py:24
  55.3 6.6 %collective-permute-start.16 = (bf16[16,128]{1,0:T(8,128)(2,1)S(1)}, bf16[16,128]{1,0:T(8,128)(2,1)S(1)}, u32[]{:S(2)}, u32[]{:S(2)}) collective-permute-start(bf16[16,128]{1,0:T(8,128)(2,1)S(1)} %get-tuple-element.62.refs_8_), channel_id=1, source_target_pairs={{0,4},{4,0},{8,12},{12,8},{16,20},{20,16},{24,28},{28,24},{1,5},{5... | collective-permute-start | bytes 12296 | tf_op jit(solution)/shard_map/ppermute | solution.py:24
  55.9 7.8 %collective-permute-start.9 = (bf16[4,64,128]{2,1,0:T(8,128)(2,1)S(1)}, bf16[4,64,128]{2,1,0:T(8,128)(2,1)S(1)}, u32[]{:S(2)}, u32[]{:S(2)}) collective-permute-start(bf16[4,64,128]{2,1,0:T(8,128)(2,1)S(1)} %get-tuple-element.55), channel_id=1, source_target_pairs={{0,35},{4,39},{8,43},{12,47},{16,51},{20,55},{24,59},{28,63},{1,0}... | collective-permute-start | bytes 196616 | tf_op jit(solution)/shard_map/ppermute | solution.py:24
  57.7 8.1 %collective-permute-start.10 = (bf16[4,64,128]{2,1,0:T(8,128)(2,1)S(1)}, bf16[4,64,128]{2,1,0:T(8,128)(2,1)S(1)}, u32[]{:S(2)}, u32[]{:S(2)}) collective-permute-start(bf16[4,64,128]{2,1,0:T(8,128)(2,1)S(1)} %get-tuple-element.56), channel_id=1, source_target_pairs={{0,1},{4,5},{8,9},{12,13},{16,17},{20,21},{24,25},{28,29},{1,2},{5... | collective-permute-start | bytes 196616 | tf_op jit(solution)/shard_map/ppermute | solution.py:24
  61.8 6.5 %collective-permute-start.11 = (bf16[4,64,128]{2,1,0:T(8,128)(2,1)S(1)}, bf16[4,64,128]{2,1,0:T(8,128)(2,1)S(1)}, u32[]{:S(2)}, u32[]{:S(2)}) collective-permute-start(bf16[4,64,128]{2,1,0:T(8,128)(2,1)S(1)} %get-tuple-element.57), channel_id=1, source_target_pairs={{0,34},{4,38},{8,42},{12,46},{16,50},{20,54},{24,58},{28,62},{1,3}... | collective-permute-start | bytes 196616 | tf_op jit(solution)/shard_map/ppermute | solution.py:24
  61.9 6.4 %collective-permute-start.13 = (bf16[4,64,128]{2,1,0:T(8,128)(2,1)S(1)}, bf16[4,64,128]{2,1,0:T(8,128)(2,1)S(1)}, u32[]{:S(2)}, u32[]{:S(2)}) collective-permute-start(bf16[4,64,128]{2,1,0:T(8,128)(2,1)S(1)} %get-tuple-element.59), channel_id=1, source_target_pairs={{0,39},{4,35},{8,47},{12,43},{16,55},{20,51},{24,63},{28,59},{1,4}... | collective-permute-start | bytes 196616 | tf_op jit(solution)/shard_map/ppermute | solution.py:24
  62.5 5.7 %collective-permute-start.14 = (bf16[4,64,128]{2,1,0:T(8,128)(2,1)S(1)}, bf16[4,64,128]{2,1,0:T(8,128)(2,1)S(1)}, u32[]{:S(2)}, u32[]{:S(2)}) collective-permute-start(bf16[4,64,128]{2,1,0:T(8,128)(2,1)S(1)} %get-tuple-element.60), channel_id=1, source_target_pairs={{0,5},{4,1},{8,13},{12,9},{16,21},{20,17},{24,29},{28,25},{1,6},{5... | collective-permute-start | bytes 196616 | tf_op jit(solution)/shard_map/ppermute | solution.py:24
  63.7 6.3 %collective-permute-start.15 = (bf16[4,64,128]{2,1,0:T(8,128)(2,1)S(1)}, bf16[4,64,128]{2,1,0:T(8,128)(2,1)S(1)}, u32[]{:S(2)}, u32[]{:S(2)}) collective-permute-start(bf16[4,64,128]{2,1,0:T(8,128)(2,1)S(1)} %get-tuple-element.61), channel_id=1, source_target_pairs={{0,38},{4,34},{8,46},{12,42},{16,54},{20,50},{24,62},{28,58},{1,7}... | collective-permute-start | bytes 196616 | tf_op jit(solution)/shard_map/ppermute | solution.py:24
  70.0 11.3 %collective-permute-start.17 = (bf16[2,17,16,128]{3,2,1,0:T(8,128)(2,1)S(1)}, bf16[2,17,16,128]{3,2,1,0:T(8,128)(2,1)S(1)}, u32[]{:S(2)}, u32[]{:S(2)}) collective-permute-start(bf16[2,17,16,128]{3,2,1,0:T(8,128)(2,1)S(1)} %get-tuple-element.64), channel_id=1, source_target_pairs={{0,8},{4,12},{8,0},{12,4},{16,24},{20,28},{24,16},{28,20},{1,9},{5... | collective-permute-start | bytes 417800 | tf_op jit(solution)/shard_map/ppermute | solution.py:24
  71.6 9.7 %collective-permute-start.18 = (bf16[2,17,16,128]{3,2,1,0:T(8,128)(2,1)S(1)}, bf16[2,17,16,128]{3,2,1,0:T(8,128)(2,1)S(1)}, u32[]{:S(2)}, u32[]{:S(2)}) collective-permute-start(bf16[2,17,16,128]{3,2,1,0:T(8,128)(2,1)S(1)} %get-tuple-element.65), channel_id=1, source_target_pairs={{0,16},{4,20},{8,24},{12,28},{16,0},{20,4},{24,8},{28,12},{1,17},{... | collective-permute-start | bytes 417800 | tf_op jit(solution)/shard_map/ppermute | solution.py:24
  74.4 9.2 %collective-permute-start.19 = (bf16[2,17,16,128]{3,2,1,0:T(8,128)(2,1)S(1)}, bf16[2,17,16,128]{3,2,1,0:T(8,128)(2,1)S(1)}, u32[]{:S(2)}, u32[]{:S(2)}) collective-permute-start(bf16[2,17,16,128]{3,2,1,0:T(8,128)(2,1)S(1)} %get-tuple-element.66), channel_id=1, source_target_pairs={{0,24},{4,28},{8,16},{12,20},{16,8},{20,12},{24,0},{28,4},{1,25},{... | collective-permute-start | bytes 417800 | tf_op jit(solution)/shard_map/ppermute | solution.py:24
  77.0 58.1 %collective-permute-start.2 = (bf16[2,256,512]{2,1,0:T(8,128)(2,1)S(1)}, bf16[2,256,512]{2,1,0:T(8,128)(2,1)S(1)}, u32[]{:S(2)}, u32[]{:S(2)}) collective-permute-start(bf16[2,256,512]{2,1,0:T(8,128)(2,1)S(1)} %shard_map.51), channel_id=1, source_target_pairs={{0,35},{4,39},{8,43},{12,47},{16,51},{20,55},{24,59},{28,63},{1,0}... | collective-permute-start | bytes 1572872 | tf_op jit(solution)/shard_map/ppermute | solution.py:24
  80.5 54.5 %collective-permute-start.5 = (bf16[2,256,512]{2,1,0:T(8,128)(2,1)S(1)}, bf16[2,256,512]{2,1,0:T(8,128)(2,1)S(1)}, u32[]{:S(2)}, u32[]{:S(2)}) collective-permute-start(bf16[2,256,512]{2,1,0:T(8,128)(2,1)S(1)} %shard_map.53), channel_id=1, source_target_pairs={{0,1},{4,5},{8,9},{12,13},{16,17},{20,21},{24,25},{28,29},{1,2},{5... | collective-permute-start | bytes 1572872 | tf_op jit(solution)/shard_map/ppermute | solution.py:24
  83.8 15.8 %collective-permute-start.20 = (bf16[17,16,128]{2,1,0:T(8,128)(2,1)S(1)}, bf16[17,16,128]{2,1,0:T(8,128)(2,1)S(1)}, u32[]{:S(2)}, u32[]{:S(2)}) collective-permute-start(bf16[17,16,128]{2,1,0:T(8,128)(2,1)S(1)} %shard_map.57.total.refs_4_), channel_id=1, source_target_pairs={{0,32},{4,36},{8,40},{12,44},{16,48},{20,52},{24,56},{28,60},{1,33... | collective-permute-start | bytes 208904 | tf_op jit(solution)/shard_map/ppermute | solution.py:24
  89.2 45.9 %collective-permute-start.8 = (bf16[2,256,512]{2,1,0:T(8,128)(2,1)S(1)}, bf16[2,256,512]{2,1,0:T(8,128)(2,1)S(1)}, u32[]{:S(2)}, u32[]{:S(2)}) collective-permute-start(bf16[2,256,512]{2,1,0:T(8,128)(2,1)S(1)} %shard_map.55), channel_id=1, source_target_pairs={{0,34},{4,38},{8,42},{12,46},{16,50},{20,54},{24,58},{28,62},{1,3}... | collective-permute-start | bytes 1572872 | tf_op jit(solution)/shard_map/ppermute | solution.py:24
  90.3 12.5 %collective-permute-start.21 = (bf16[17,16,128]{2,1,0:T(8,128)(2,1)S(1)}, bf16[17,16,128]{2,1,0:T(8,128)(2,1)S(1)}, u32[]{:S(2)}, u32[]{:S(2)}) collective-permute-start(bf16[17,16,128]{2,1,0:T(8,128)(2,1)S(1)} %shard_map.57.total.refs_4_), channel_id=1, source_target_pairs={{0,64},{4,68},{8,72},{12,76},{16,80},{20,84},{24,88},{28,92},{1,65... | collective-permute-start | bytes 208904 | tf_op jit(solution)/shard_map/ppermute | solution.py:24
  99.6 5.8 %collective-permute-start.23 = (bf16[17,16,128]{2,1,0:T(8,128)(2,1)S(1)}, bf16[17,16,128]{2,1,0:T(8,128)(2,1)S(1)}, u32[]{:S(2)}, u32[]{:S(2)}) collective-permute-start(bf16[17,16,128]{2,1,0:T(8,128)(2,1)S(1)} %shard_map.57.total.refs_4_), channel_id=1, source_target_pairs={{0,128},{4,132},{8,136},{12,140},{16,144},{20,148},{24,152},{28,15... | collective-permute-start | bytes 208904 | tf_op jit(solution)/shard_map/ppermute | solution.py:24
  102.8 6.6 %collective-permute-start.25 = (bf16[17,16,128]{2,1,0:T(8,128)(2,1)S(1)}, bf16[17,16,128]{2,1,0:T(8,128)(2,1)S(1)}, u32[]{:S(2)}, u32[]{:S(2)}) collective-permute-start(bf16[17,16,128]{2,1,0:T(8,128)(2,1)S(1)} %shard_map.57.total.refs_4_), channel_id=1, source_target_pairs={{0,192},{4,196},{8,200},{12,204},{16,208},{20,212},{24,216},{28,22... | collective-permute-start | bytes 208904 | tf_op jit(solution)/shard_map/ppermute | solution.py:24
  109.4 5.8 %collective-permute-start.24 = (bf16[17,16,128]{2,1,0:T(8,128)(2,1)S(1)}, bf16[17,16,128]{2,1,0:T(8,128)(2,1)S(1)}, u32[]{:S(2)}, u32[]{:S(2)}) collective-permute-start(bf16[17,16,128]{2,1,0:T(8,128)(2,1)S(1)} %collective-permute-done.20.refs_5_), channel_id=1, source_target_pairs={{0,128},{4,132},{8,136},{12,140},{16,144},{20,148},{24,152},{28,15... | collective-permute-start | bytes 208904 | tf_op jit(solution)/shard_map/ppermute | solution.py:24
  110.1 5.8 %collective-permute-start.26 = (bf16[17,16,128]{2,1,0:T(8,128)(2,1)S(1)}, bf16[17,16,128]{2,1,0:T(8,128)(2,1)S(1)}, u32[]{:S(2)}, u32[]{:S(2)}) collective-permute-start(bf16[17,16,128]{2,1,0:T(8,128)(2,1)S(1)} %collective-permute-done.20.refs_5_), channel_id=1, source_target_pairs={{0,192},{4,196},{8,200},{12,204},{16,208},{20,212},{24,216},{28,22... | collective-permute-start | bytes 208904 | tf_op jit(solution)/shard_map/ppermute | solution.py:24
  116.5 4.8 %collective-permute-start.28 = (bf16[16,16,128]{2,1,0:T(8,128)(2,1)S(1)}, bf16[16,16,128]{2,1,0:T(8,128)(2,1)S(1)}, u32[]{:S(2)}, u32[]{:S(2)}) collective-permute-start(bf16[16,16,128]{2,1,0:T(8,128)(2,1)S(1)} %get-tuple-element.69), channel_id=1, source_target_pairs={{0,8},{4,12},{8,0},{12,4},{16,24},{20,28},{24,16},{28,20},{1,9},{5... | collective-permute-start | bytes 196616 | tf_op jit(solution)/shard_map/ppermute | solution.py:24
  117.7 5.7 %collective-permute-start.29 = (bf16[16,16,128]{2,1,0:T(8,128)(2,1)S(1)}, bf16[16,16,128]{2,1,0:T(8,128)(2,1)S(1)}, u32[]{:S(2)}, u32[]{:S(2)}) collective-permute-start(bf16[16,16,128]{2,1,0:T(8,128)(2,1)S(1)} %get-tuple-element.70), channel_id=1, source_target_pairs={{0,12},{4,8},{8,4},{12,0},{16,28},{20,24},{24,20},{28,16},{1,13},{... | collective-permute-start | bytes 196616 | tf_op jit(solution)/shard_map/ppermute | solution.py:24
  121.2 5.8 %collective-permute-start.30 = (bf16[16,16,128]{2,1,0:T(8,128)(2,1)S(1)}, bf16[16,16,128]{2,1,0:T(8,128)(2,1)S(1)}, u32[]{:S(2)}, u32[]{:S(2)}) collective-permute-start(bf16[16,16,128]{2,1,0:T(8,128)(2,1)S(1)} %get-tuple-element.71), channel_id=1, source_target_pairs={{0,16},{4,20},{8,24},{12,28},{16,0},{20,4},{24,8},{28,12},{1,17},{... | collective-permute-start | bytes 196616 | tf_op jit(solution)/shard_map/ppermute | solution.py:24
  123.5 6.7 %collective-permute-start.31 = (bf16[16,16,128]{2,1,0:T(8,128)(2,1)S(1)}, bf16[16,16,128]{2,1,0:T(8,128)(2,1)S(1)}, u32[]{:S(2)}, u32[]{:S(2)}) collective-permute-start(bf16[16,16,128]{2,1,0:T(8,128)(2,1)S(1)} %get-tuple-element.72), channel_id=1, source_target_pairs={{0,20},{4,16},{8,28},{12,24},{16,4},{20,0},{24,12},{28,8},{1,21},{... | collective-permute-start | bytes 196616 | tf_op jit(solution)/shard_map/ppermute | solution.py:24
  127.0 5.7 %collective-permute-start.32 = (bf16[16,16,128]{2,1,0:T(8,128)(2,1)S(1)}, bf16[16,16,128]{2,1,0:T(8,128)(2,1)S(1)}, u32[]{:S(2)}, u32[]{:S(2)}) collective-permute-start(bf16[16,16,128]{2,1,0:T(8,128)(2,1)S(1)} %get-tuple-element.73), channel_id=1, source_target_pairs={{0,24},{4,28},{8,16},{12,20},{16,8},{20,12},{24,0},{28,4},{1,25},{... | collective-permute-start | bytes 196616 | tf_op jit(solution)/shard_map/ppermute | solution.py:24
  130.2 4.9 %collective-permute-start.33 = (bf16[16,16,128]{2,1,0:T(8,128)(2,1)S(1)}, bf16[16,16,128]{2,1,0:T(8,128)(2,1)S(1)}, u32[]{:S(2)}, u32[]{:S(2)}) collective-permute-start(bf16[16,16,128]{2,1,0:T(8,128)(2,1)S(1)} %get-tuple-element.74), channel_id=1, source_target_pairs={{0,28},{4,24},{8,20},{12,16},{16,12},{20,8},{24,4},{28,0},{1,29},{... | collective-permute-start | bytes 196616 | tf_op jit(solution)/shard_map/ppermute | solution.py:24
  (4 other events, 52.7 us)

commit v4 on v3

v4 whole, which is shorter than its diff:
```python
import itertools

import jax
import jax.numpy as jnp
from jax import lax
from jax.experimental import pallas as pl
from jax.experimental.pallas import tpu as pltpu
from jax.sharding import PartitionSpec as P


F32 = jnp.float32
BF16 = jnp.bfloat16
BOTH = ("ctx", "fsdp")
VMEM = pl.BlockSpec(memory_space=pltpu.VMEM)


def pairs(move):
    flat = lambda y, z, x, c: (((y * 2 + z // 4) * 4 + x) * 2 + c) * 4 + z % 4
    every = itertools.product(range(4), range(8), range(4), range(2))
    return [(flat(*at), flat(*move(*at))) for at in every]


def send(a, move):
    return lax.ppermute(a, BOTH, pairs(move))


def up(y, z, x, c):
    return y, (z + 1) % 8, x, c


def down(y, z, x, c):
    return y, (z - 1) % 8, x, c


def up_two(y, z, x, c):
    return y, (z + 2) % 8, x, c


def down_two(y, z, x, c):
    return y, (z - 2) % 8, x, c


def other(y, z, x, c):
    return y, z, x, 1 - c


def along_x(d):
    return lambda y, z, x, c: (y, z, x ^ d, c)


def far(y, z, x, c):
    return y, (z + 4) % 8, x, c


def along_y(d):
    return lambda y, z, x, c: (y ^ d, z, x, c)


def exchange(parts, order, move):
    got = {d: send(parts[d], move(d)) for d in order}
    return [parts[0]] + [got[d] for d in range(1, len(parts))]


def silu(a):
    return a * jax.nn.sigmoid(a)


def dot(a, b, dims):
    return lax.dot_general(a, b, (dims, ((), ())), preferred_element_type=F32)


def call(kernel, outs, *args, flops=0, scratch=(), space=pltpu.VMEM, far=0):
    moved = sum(a.size * a.dtype.itemsize for a in args)
    near = len(args) - far
    held = [pltpu.with_memory_space_constraint(a, pltpu.VMEM) for a in args[:near]] + [
        pltpu.with_memory_space_constraint(a, pltpu.HBM) for a in args[near:]
    ]
    return pl.pallas_call(
        kernel,
        in_specs=[VMEM] * near + [pl.BlockSpec(memory_space=pltpu.HBM)] * far,
        out_specs=[VMEM] * len(outs),
        out_shape=[space(shape, dtype) for shape, dtype in outs],
        scratch_shapes=[pltpu.VMEM(shape, dtype) for shape, dtype in scratch] + [pltpu.SemaphoreType.DMA(())] * far,
        cost_estimate=pl.CostEstimate(flops=flops, bytes_accessed=moved, transcendentals=0),
        compiler_params=pltpu.CompilerParams(vmem_limit_bytes=24 << 20),
    )(*held)


def place():
    i = lax.axis_index("ctx")
    return lax.rem(i, 8), lax.div(i, 8)


def running(a, span=256):
    lane = lax.rem(lax.broadcasted_iota(jnp.int32, a.shape, 1), span)
    step = 1
    while step < span:
        a = a + jnp.where(lane >= step, pltpu.roll(a, step, axis=1), 0.0)
        step *= 2
    return a


SHIFTS = (0, 1, 3, 2)


def split(a):
    high = a.astype(BF16)
    rest = a - high.astype(F32)
    mid = rest.astype(BF16)
    return high, mid, (rest - mid.astype(F32)).astype(BF16)


def pack(column):
    lane = lax.broadcasted_iota(jnp.int32, (16, 128), 1)
    high, mid, low = (jnp.broadcast_to(a.astype(F32), (16, 128)) for a in split(column))
    return jnp.where(lane == 0, high, jnp.where(lane == 1, mid, jnp.where(lane == 2, low, 0.0))).astype(BF16)


def unpack(tile):
    a = tile.astype(F32)
    return a[:, 0:1] + a[:, 1:2] + a[:, 2:3]


def prepare(rates, tok, r0, r1, r2, r3, entry, total, second, held, sem):
    f = lax.axis_index("fsdp")
    copy = pltpu.make_async_copy(tok, held, sem)
    copy.start()
    cums = []
    for i, out in enumerate((r0, r1, r2, r3)):
        group = lax.rem(f + SHIFTS[i], 4)
        own = rates[0:4, :]
        for g in range(1, 4):
            own = jnp.where(group == g, rates[4 * g : 4 * g + 4, :], own)
        own = jnp.concatenate([own, jnp.zeros_like(own)], axis=0)
        out[...] = own
        cums.append(running(own)[:4])
    halves = running(own, 128)
    cum = jnp.concatenate(cums + [halves], axis=0)
    entry[...] = jnp.concatenate([jnp.exp(cum).T, jnp.zeros((256, 104), F32)], axis=1)
    total[...] = pack(cum[:16, 255:256])
    second[...] = jnp.broadcast_to(jnp.exp(halves[:, 255:256]), (8, 128))
    copy.wait()


def load(w, held, sem):
    copy = pltpu.make_async_copy(w, held, sem)
    copy.start()
    copy.wait()


def project(tok, w, c, j):
    return jnp.dot(tok[...], w[c, :, 256 * j : 256 * j + 256], preferred_element_type=F32)


def states_of(tok, w, cum, k_out, v_out, locals_out, span):
    ends = [cum[:, at + span - 1 : at + span] - cum[:, at : at + span] for at in range(0, 256, span)]
    tail = jnp.exp(jnp.concatenate(ends, axis=1)).T
    for j in range(2):
        pair = slice(256 * j, 256 * j + 256)
        k = silu(project(tok, w, 1, j)).astype(BF16)
        v = project(tok, w, 2, j).astype(BF16)
        k_out[:, pair] = k
        v_out[:, pair] = v
        for h in range(2):
            cols = slice(128 * h, 128 * h + 128)
            head = 2 * j + h
            scaled = (k[:, cols].astype(F32) * tail[:, head : head + 1]).astype(BF16)
            for i, local in enumerate(locals_out):
                rows = slice(span * i, span * i + span)
                local[head] = dot(scaled[rows], v[rows, cols], ((0,), (0,))).astype(BF16)


def states(tok, w, rates, *refs):
    k_out, v_out, local = refs[-3:]
    states_of(tok, w, running(rates[...]), k_out, v_out, [local], 256)


def two_rates(first, second):
    lane = lax.broadcasted_iota(jnp.int32, (8, 256), 1)
    return running(jnp.where(lane < 128, first[...], second[...]), 128)


def states_two(t0, t1, w, r0, r1, tok, k_out, v_out, local0, local1):
    tok[0:128, :] = t0[...]
    tok[128:256, :] = t1[...]
    states_of(tok, w, two_rates(r0, r1), k_out, v_out, [local0, local1], 128)


def insides_of(tok, w, cum, k_ref, v_ref, outs, span):
    col = cum.T
    t = lax.broadcasted_iota(jnp.int32, (span, span), 0)
    causal = t >= lax.broadcasted_iota(jnp.int32, (span, span), 1)
    for j in range(2):
        q = silu(project(tok, w, 0, j)).astype(BF16)
        for h in range(2):
            head = 2 * j + h
            cols = slice(128 * head, 128 * head + 128)
            for i, out in enumerate(outs):
                rows = slice(span * i, span * i + span)
                own = q[rows, 128 * h : 128 * h + 128]
                out[0, :, cols] = own
                scores = dot(own, k_ref[rows, cols], ((1,), (1,)))
                gaps = col[rows, head : head + 1] - cum[head : head + 1, rows]
                weights = (scores * jnp.exp(jnp.where(causal, gaps, -jnp.inf))).astype(BF16)
                value = jnp.dot(weights, v_ref[rows, cols], preferred_element_type=F32)
                out[1, :, cols] = value.astype(BF16)


def insides(tok, w, rates, k_ref, v_ref, out):
    insides_of(tok, w, running(rates[...]), k_ref, v_ref, [out], 256)


def insides_two(tok, w, r0, r1, k_ref, v_ref, out0, out1):
    insides_of(tok, w, two_rates(r0, r1), k_ref, v_ref, [out0, out1], 128)


def halve(s0, s1, s2, s3, s4, second, same, cross):
    core = lax.rem(place()[0], 2)
    for number, out in ((core, same), (1 - core, cross)):
        rows = pl.ds(pl.multiple_of(number * 64, 64), 64)
        for i, s in enumerate((s0, s1, s2)):
            out[4 * i : 4 * i + 4] = s[:, rows, :]
        for h in range(4):
            whole = s3[h, rows, :].astype(F32) * second[h : h + 1, :] + s4[h, rows, :].astype(F32)
            out[12 + h] = whole.astype(BF16)


def deal(own, partner, total, partner_total, *outs):
    p, _ = place()
    x, core = lax.div(p, 2), lax.rem(p, 2)
    for d in range(4):
        rows = pl.ds(pl.multiple_of(jnp.bitwise_xor(x, d) * 16, 16), 16)
        for block, half, log in ((core, own, total), (1 - core, partner, partner_total)):
            outs[d][block, 0:16] = half[:, rows, :]
            outs[d][block, 16] = log[...]


def arrange(natural, pieces):
    x = lax.div(place()[0], 2)
    for d in range(4):
        at = jnp.bitwise_xor(x, d) * 2
        for core in range(2):
            natural[at + core] = pieces[d][core]


def row_total(*refs):
    pieces, out, natural, decay = refs[:4], refs[4], refs[5], refs[6]
    arrange(natural, pieces)
    logs = jnp.zeros((16, 1), F32)
    for e in range(8):
        own = unpack(natural[e, 16])
        logs += own
        decay[e] = jnp.broadcast_to(jnp.exp(own), (16, 128))
    for h in range(16):
        run = natural[0, h].astype(F32)
        for e in range(1, 8):
            run = run * decay[e, h : h + 1, :] + natural[e, h].astype(F32)
        out[h] = run.astype(BF16)
    out[16] = pack(logs)


def mark(total, out):
    out[...] = total[16]


def carry(_, *refs):
    pieces, totals, outs, natural, rows, decay, row_decay = refs[:4], refs[4:12], refs[12:16], *refs[16:]
    p, r = place()
    x = lax.div(p, 2)
    arrange(natural, pieces)
    for d in range(8):
        rows[jnp.bitwise_xor(r, d)] = totals[d][...]
    for e in range(8):
        decay[e] = jnp.broadcast_to(jnp.exp(unpack(natural[e, 16])), (16, 128))
        row_decay[e] = jnp.broadcast_to(jnp.exp(jnp.where(e < r, unpack(rows[e, 16]), 0.0)), (16, 128))
    for h in range(16):
        run = jnp.zeros((16, 128), F32)
        for e in range(7):
            run = run * row_decay[e, h : h + 1, :] + jnp.where(e < r, rows[e, h].astype(F32), 0.0)
        for e in range(8):
            piece = natural[e, h].astype(F32)
            natural[e, h] = run.astype(BF16)
            run = run * decay[e, h : h + 1, :] + piece
    for d in range(4):
        for block in range(2):
            outs[d][block] = natural[jnp.bitwise_xor(x, d) * 2 + block, 0:16]


def gather(p0, p1, p2, p3, out):
    p, _ = place()
    x, core = lax.div(p, 2), lax.rem(p, 2)
    for d, piece in enumerate((p0, p1, p2, p3)):
        out[:, pl.ds(pl.multiple_of(jnp.bitwise_xor(x, d) * 16, 16), 16), :] = piece[1 - core]


def final(entry, gain, first_half, crossed, *refs):
    parts, pieces, out, memory, attended = refs[:5], refs[5:9], refs[9], refs[10], refs[11]
    p, _ = place()
    x, core = lax.div(p, 2), lax.rem(p, 2)
    f = lax.axis_index("fsdp")
    for d in range(4):
        at = core * 64 + jnp.bitwise_xor(x, d) * 16
        memory[:, pl.ds(pl.multiple_of(at, 16), 16), :] = pieces[d][core]
    memory[:, pl.ds(pl.multiple_of(64 - core * 64, 64), 64), :] = crossed[...]
    squares = [jnp.zeros((128, 128), F32)] * 2
    for i, shift in enumerate(SHIFTS):
        group = lax.rem(f + shift, 4)
        for h in range(4):
            cols = slice(128 * h, 128 * h + 128)
            head = 4 * i + h
            for half in range(2):
                rows = slice(128 * half, 128 * half + 128)
                part, at = (parts[i], rows) if i < 3 else (parts[3 + half], slice(0, 128))
                q = part[0, at, cols]
                value = part[1, at, cols].astype(F32)
                value += jnp.dot(q, memory[head], preferred_element_type=F32) * entry[rows, head : head + 1]
                if i == 3 and half == 1:
                    value += jnp.dot(q, first_half[h], preferred_element_type=F32) * entry[rows, 16 + h : 17 + h]
                squares[half] += value * value
                attended[rows, pl.ds(pl.multiple_of(group * 512 + 128 * h, 128), 128)] = value
    for half in range(2):
        rows = slice(128 * half, 128 * half + 128)
        scale = lax.rsqrt(jnp.sum(squares[half], axis=-1, keepdims=True) / out.shape[1] + 1e-05)
        out[rows, :] = (attended[rows, :] * scale * gain[...]).astype(BF16)


def body(tokens, qkv_weight, log_decay, norm_gain):
    tok = tokens[0]
    n, d = tok.shape
    slots = ((8, 17, 16, 128), BF16)
    factor = ((8, 16, 128), F32)
    state = ((4, 128, 128), BF16)
    half = ((n, 512), BF16)

    from_up = send(tok, up)
    from_down = send(tok, down)
    *rates, entry, total, second, held = call(
        prepare,
        [((8, n), F32)] * 4 + [((n, 128), F32), ((16, 128), BF16), ((8, 128), F32), ((n, d), BF16)],
        log_decay[0],
        tok,
        far=1,
    )
    rates = [rates[0]] + [
        send(a, m) for a, m in zip((*rates[1:], rates[3]), (up, down, up_two, down_two))
    ]
    partner_total = send(total, other)
    first = send(from_up[:128], up)
    last = send(from_down[128:], down)
    weight = call(load, [(qkv_weight.shape, BF16)], qkv_weight, far=1)[0]

    toks, made = [held, from_up, from_down], []
    for i in range(3):
        after = (made[0][2],) if made else ()
        made.append(call(states, [half, half, state], toks[i], weight, rates[i], *after, flops=1 << 30))
    two = call(
        states_two, [((n, d), BF16), half, half, state, state], first, last, weight, *rates[3:], flops=1 << 30
    )
    first_half, last_half = send(two[3], down_two), send(two[4], up_two)
    back_1 = send(made[1][2], down)
    back_2 = send(made[2][2], up)

    parts = []
    for i in range(3):
        parts += call(
            insides, [((2, n, 512), BF16)], toks[i], weight, rates[i], *made[i][:2], flops=1 << 30
        )
    parts += call(insides_two, [((2, 128, 512), BF16)] * 2, two[0], weight, *rates[3:], *two[1:3], flops=1 << 30)
    for i, m in enumerate((down, up, down_two, up_two)):
        parts[i + 1] = send(parts[i + 1], m)

    same, cross = call(
        halve, [((16, 64, 128), BF16)] * 2, made[0][2], back_1, back_2, first_half, last_half, second
    )
    partner = send(cross, other)
    pieces = call(deal, [((2, 17, 16, 128), BF16)] * 4, same, partner, total, partner_total)
    pieces = exchange(pieces, (2, 1, 3), along_x)
    own_total = call(row_total, [((17, 16, 128), BF16)], *pieces, scratch=[slots, factor])[0]

    marked = call(mark, [((16, 128), BF16)], own_total)[0]
    far_total = send(own_total, far)
    near = [send(own_total, along_y(e)) for e in range(1, 4)]
    totals = [own_total, far_total]
    for e in range(1, 4):
        totals += [near[e - 1], send(far_total, along_y(e))]
    carried = call(
        carry,
        [((2, 16, 16, 128), BF16)] * 4,
        marked,
        *pieces,
        *totals,
        scratch=[slots] * 2 + [factor] * 2,
    )
    carried = exchange(carried, (2, 1, 3), along_x)
    crossed = send(call(gather, [((16, 64, 128), BF16)], *carried)[0], other)
    out = call(
        final,
        [((n, d), BF16)],
        entry,
        norm_gain[None],
        first_half,
        crossed,
        *parts,
        *carried,
        scratch=[((16, 128, 128), BF16), ((n, d), F32)],
        space=jax.ShapeDtypeStruct,
    )[0]
    return out[None]


def solution(mesh):
    placed = (P("fsdp", "ctx", None), P(None, None, "fsdp"), P("fsdp", None, "ctx"), P())
    return jax.shard_map(body, mesh=mesh, in_specs=placed, out_specs=P("fsdp", "ctx", None), check_vma=False)
```

time: 137 us -> 126 us (0.920)
  the two profiles are of different devices: /device:TPU:64 before, /device:TPU:32 now
where the time goes in v4:
time: 126 us; the launch traced here: 125 us
  waiting for transfers between devices  56.5 us (45%)
  starting transfers between devices  44.7 us (35%)
  Pallas kernels  23.1 us (18%)
    ppermute x32, waiting for transfers between devices, send(): return lax.ppermute(a, BOTH, pairs(move))  56.5 us
    ppermute x32, starting transfers between devices, send(): return lax.ppermute(a, BOTH, pairs(move))  44.7 us
    pallas_call x17, Pallas kernels, call(): pl.pallas_call(kernel, in_specs=[VMEM] * near + [pl.BlockSpec(memory_spac...  23.1 us
  transfers between devices with their start and end apart: 32, of which 14 were waited for; matrix products, arithmetic and copies ran while one was open for 0% of the time, Pallas kernels for 17%

profile of v4, /device:TPU:32, one launch (start us, length us, event | category | flops | bytes accessed | tf_op | source)
XLA Modules:
  0.0 125.3 jit_solution(1725987664974943783)
XLA Ops:
  0.0 1.8 %collective-permute-start.2 = (bf16[256,2048]{1,0:T(8,128)(2,1)}, bf16[256,2048]{1,0:T(8,128)(2,1)S(1)}, u32[]{:S(2)}, u32[]{:S(2)}) collective-permute-start(bf16[256,2048]{1,0:T(8,128)(2,1)} %bitcast.6), channel_id=1, source_target_pairs={{0,35},{4,39},{8,43},{12,47},{16,51},{20,55},{24,59},{28,63},{1,0}... | collective-permute-start | bytes 3145736 | tf_op jit(solution)/shard_map/ppermute | solution.py:24
  2.0 23.3 %collective-permute-done.2.tok = bf16[256,2048]{1,0:T(8,128)(2,1)S(1)} collective-permute-done((bf16[256,2048]{1,0:T(8,128)(2,1)}, bf16[256,2048]{1,0:T(8,128)(2,1)S(1)}, u32[]{:S(2)}, u32[]{:S(2)}) %collective-permute-start.2) | collective-permute-done | bytes 1048608 | tf_op jit(solution)/shard_map/ppermute | solution.py:24
  25.3 3.5 %collective-permute-start.3 = (bf16[128,2048]{1,0:T(8,128)(2,1)S(1)}, bf16[128,2048]{1,0:T(8,128)(2,1)S(1)}, u32[]{:S(2)}, u32[]{:S(2)}) collective-permute-start(bf16[128,2048]{1,0:T(8,128)(2,1)S(1)} %slice.9), channel_id=1, source_target_pairs={{0,35},{4,39},{8,43},{12,47},{16,51},{20,55},{24,59},{28,63},{1,0}... | collective-permute-start | bytes 1572872 | tf_op jit(solution)/shard_map/ppermute | solution.py:24
  31.2 6.1 %collective-permute-start.5 = (f32[8,256]{1,0:T(8,128)S(1)}, f32[8,256]{1,0:T(8,128)S(1)}, u32[]{:S(2)}, u32[]{:S(2)}) collective-permute-start(f32[8,256]{1,0:T(8,128)S(1)} %get-tuple-element.40), channel_id=1, source_target_pairs={{0,34},{4,38},{8,42},{12,46},{16,50},{20,54},{24,58},{28,62},{1,35... | collective-permute-start | bytes 24584 | tf_op jit(solution)/shard_map/ppermute | solution.py:24
  37.5 2.8 %shard_map.47.w = bf16[3,2048,512]{2,1,0:T(8,128)(2,1)S(1)} custom-call(bf16[3,2048,512]{2,1,0:T(8,128)(2,1)} %w.1), custom_call_target="tpu_custom_call" | custom-call | bytes 6291456 | tf_op jit(solution)/shard_map/pallas_call | solution.py:78
  40.3 1.8 %shard_map.49 = (bf16[256,512]{1,0:T(8,128)(2,1)S(1)}, bf16[256,512]{1,0:T(8,128)(2,1)S(1)}, bf16[4,128,128]{2,1,0:T(8,128)(2,1)S(1)}) custom-call(bf16[256,2048]{1,0:T(8,128)(2,1)S(1)} %get-tuple-element.42.tok, bf16[3,2048,512]{2,1,0:T(8,128)(2,1)S(1)} %shard_map.47.w, f32[8,256]{1,0:T(8,128)S(1)} %get-tuple-element.43.rates), custom_call_target="tpu_custom_call" | custom-call | flops 1073741824 | bytes 7348224 | tf_op jit(solution)/shard_map/pallas_call | solution.py:78
  42.1 1.8 %collective-permute-start.7 = (f32[8,256]{1,0:T(8,128)S(1)}, f32[8,256]{1,0:T(8,128)S(1)}, u32[]{:S(2)}, u32[]{:S(2)}) collective-permute-start(f32[8,256]{1,0:T(8,128)S(1)} %get-tuple-element.45), channel_id=1, source_target_pairs={{0,1},{4,5},{8,9},{12,13},{16,17},{20,21},{24,25},{28,29},{1,2},{5... | collective-permute-start | bytes 24584 | tf_op jit(solution)/shard_map/ppermute | solution.py:24
  43.9 1.8 %shard_map.51 = (bf16[256,512]{1,0:T(8,128)(2,1)S(1)}, bf16[256,512]{1,0:T(8,128)(2,1)S(1)}, bf16[4,128,128]{2,1,0:T(8,128)(2,1)S(1)}) custom-call(bf16[256,2048]{1,0:T(8,128)(2,1)S(1)} %collective-permute-done.2.tok, bf16[3,2048,512]{2,1,0:T(8,128)(2,1)S(1)} %shard_map.47.w, f32[8,256]{1,0:T(8,128)S(1)} %collective-permute-done.9.rates, ...), custom_call_target="tpu_custom_call" | custom-call | flops 1073741824 | bytes 7479296 | tf_op jit(solution)/shard_map/pallas_call | solution.py:78
  45.7 2.5 %collective-permute-done.7.rates = f32[8,256]{1,0:T(8,128)S(1)} collective-permute-done((f32[8,256]{1,0:T(8,128)S(1)}, f32[8,256]{1,0:T(8,128)S(1)}, u32[]{:S(2)}, u32[]{:S(2)}) %collective-permute-start.7) | collective-permute-done | bytes 8224 | tf_op jit(solution)/shard_map/ppermute | solution.py:24
  48.3 1.8 %shard_map.50 = (bf16[256,512]{1,0:T(8,128)(2,1)S(1)}, bf16[256,512]{1,0:T(8,128)(2,1)S(1)}, bf16[4,128,128]{2,1,0:T(8,128)(2,1)S(1)}) custom-call(bf16[256,2048]{1,0:T(8,128)(2,1)S(1)} %collective-permute-done.tok, bf16[3,2048,512]{2,1,0:T(8,128)(2,1)S(1)} %shard_map.47.w, f32[8,256]{1,0:T(8,128)S(1)} %collective-permute-done.7.rates, ...), custom_call_target="tpu_custom_call" | custom-call | flops 1073741824 | bytes 7479296 | tf_op jit(solution)/shard_map/pallas_call | solution.py:78
  50.0 3.5 %collective-permute-start.8 = (bf16[4,128,128]{2,1,0:T(8,128)(2,1)S(1)}, bf16[4,128,128]{2,1,0:T(8,128)(2,1)S(1)}, u32[]{:S(2)}, u32[]{:S(2)}) collective-permute-start(bf16[4,128,128]{2,1,0:T(8,128)(2,1)S(1)} %get-tuple-element.46), channel_id=1, source_target_pairs={{0,35},{4,39},{8,43},{12,47},{16,51},{20,55},{24,59},{28,63},{1,0}... | collective-permute-start | bytes 393224 | tf_op jit(solution)/shard_map/ppermute | solution.py:24
  53.5 1.8 %shard_map.48 = (bf16[256,2048]{1,0:T(8,128)(2,1)S(1)}, bf16[256,512]{1,0:T(8,128)(2,1)S(1)}, bf16[256,512]{1,0:T(8,128)(2,1)S(1)}, bf16[4,128,128]{2,1,0:T(8,128)(2,1)S(1)}, bf16[4,128,128]{2,1,0:T(8,128)(2,1)S(1)}) custom-call(bf16[128,2048]{1,0:T(8,128)(2,1)S(1)} %collective-permute-done.1.t0, bf16[128,2048]{1,0:T(8,128)(2,1)S(1)} %collective-permute-done.3.t1, ...), custom_call_target="tpu_custom_call" | custom-call | flops 1073741824 | bytes 7356416 | tf_op jit(solution)/shard_map/pallas_call | solution.py:78
  55.3 2.8 %collective-permute-start.6 = (bf16[4,128,128]{2,1,0:T(8,128)(2,1)S(1)}, bf16[4,128,128]{2,1,0:T(8,128)(2,1)S(1)}, u32[]{:S(2)}, u32[]{:S(2)}) collective-permute-start(bf16[4,128,128]{2,1,0:T(8,128)(2,1)S(1)} %get-tuple-element.41), channel_id=1, source_target_pairs={{0,34},{4,38},{8,42},{12,46},{16,50},{20,54},{24,58},{28,62},{1,35... | collective-permute-start | bytes 393224 | tf_op jit(solution)/shard_map/ppermute | solution.py:24
  58.6 3.7 %collective-permute-done.6.s3.first_half = bf16[4,128,128]{2,1,0:T(8,128)(2,1)S(1)} collective-permute-done((bf16[4,128,128]{2,1,0:T(8,128)(2,1)S(1)}, bf16[4,128,128]{2,1,0:T(8,128)(2,1)S(1)}, u32[]{:S(2)}, u32[]{:S(2)}) %collective-permute-start.6) | collective-permute-done | bytes 131104 | tf_op jit(solution)/shard_map/ppermute | solution.py:24
  62.3 4.3 %collective-permute-done.11.s4 = bf16[4,128,128]{2,1,0:T(8,128)(2,1)S(1)} collective-permute-done((bf16[4,128,128]{2,1,0:T(8,128)(2,1)S(1)}, bf16[4,128,128]{2,1,0:T(8,128)(2,1)S(1)}, u32[]{:S(2)}, u32[]{:S(2)}) %collective-permute-start.11) | collective-permute-done | bytes 131104 | tf_op jit(solution)/shard_map/ppermute | solution.py:24
  69.9 2.7 %collective-permute-start.15 = (bf16[2,17,16,128]{3,2,1,0:T(8,128)(2,1)S(1)}, bf16[2,17,16,128]{3,2,1,0:T(8,128)(2,1)S(1)}, u32[]{:S(2)}, u32[]{:S(2)}) collective-permute-start(bf16[2,17,16,128]{3,2,1,0:T(8,128)(2,1)S(1)} %get-tuple-element.56), channel_id=1, source_target_pairs={{0,16},{4,20},{8,24},{12,28},{16,0},{20,4},{24,8},{28,12},{1,17},{... | collective-permute-start | bytes 417800 | tf_op jit(solution)/shard_map/ppermute | solution.py:24
  73.1 2.1 %shard_map.60 = bf16[2,256,512]{2,1,0:T(8,128)(2,1)S(1)} custom-call(bf16[256,2048]{1,0:T(8,128)(2,1)S(1)} %collective-permute-done.2.tok, bf16[3,2048,512]{2,1,0:T(8,128)(2,1)S(1)} %shard_map.47.w, f32[8,256]{1,0:T(8,128)S(1)} %collective-permute-done.9.rates, bf16[256,512]{1,0:T(8,128)(2,1)S(1)} %get-tuple-element.66.k_ref, ...), custom_call_target="tpu_custom_call" | custom-call | flops 1073741824 | bytes 7872512 | tf_op jit(solution)/shard_map/pallas_call | solution.py:78
  75.4 4.1 %collective-permute-done.15.refs_2_ = bf16[2,17,16,128]{3,2,1,0:T(8,128)(2,1)S(1)} collective-permute-done((bf16[2,17,16,128]{3,2,1,0:T(8,128)(2,1)S(1)}, bf16[2,17,16,128]{3,2,1,0:T(8,128)(2,1)S(1)}, u32[]{:S(2)}, u32[]{:S(2)}) %collective-permute-start.15) | collective-permute-done | bytes 139296 | tf_op jit(solution)/shard_map/ppermute | solution.py:24
  79.4 2.3 %collective-permute-done.16.refs_3_ = bf16[2,17,16,128]{3,2,1,0:T(8,128)(2,1)S(1)} collective-permute-done((bf16[2,17,16,128]{3,2,1,0:T(8,128)(2,1)S(1)}, bf16[2,17,16,128]{3,2,1,0:T(8,128)(2,1)S(1)}, u32[]{:S(2)}, u32[]{:S(2)}) %collective-permute-start.16) | collective-permute-done | bytes 139296 | tf_op jit(solution)/shard_map/ppermute | solution.py:24
  82.0 3.1 %collective-permute-start.22 = (bf16[17,16,128]{2,1,0:T(8,128)(2,1)S(1)}, bf16[17,16,128]{2,1,0:T(8,128)(2,1)S(1)}, u32[]{:S(2)}, u32[]{:S(2)}) collective-permute-start(bf16[17,16,128]{2,1,0:T(8,128)(2,1)S(1)} %shard_map.54.total.refs_4_), channel_id=1, source_target_pairs={{0,192},{4,196},{8,200},{12,204},{16,208},{20,212},{24,216},{28,22... | collective-permute-start | bytes 208904 | tf_op jit(solution)/shard_map/ppermute | solution.py:24
  86.5 2.1 %shard_map.59 = bf16[2,256,512]{2,1,0:T(8,128)(2,1)S(1)} custom-call(bf16[256,2048]{1,0:T(8,128)(2,1)S(1)} %collective-permute-done.tok, bf16[3,2048,512]{2,1,0:T(8,128)(2,1)S(1)} %shard_map.47.w, f32[8,256]{1,0:T(8,128)S(1)} %collective-permute-done.7.rates, bf16[256,512]{1,0:T(8,128)(2,1)S(1)} %get-tuple-element.64.k_ref, ...), custom_call_target="tpu_custom_call" | custom-call | flops 1073741824 | bytes 7872512 | tf_op jit(solution)/shard_map/pallas_call | solution.py:78
  88.7 2.6 %collective-permute-start.28 = (bf16[2,256,512]{2,1,0:T(8,128)(2,1)S(1)}, bf16[2,256,512]{2,1,0:T(8,128)(2,1)S(1)}, u32[]{:S(2)}, u32[]{:S(2)}) collective-permute-start(bf16[2,256,512]{2,1,0:T(8,128)(2,1)S(1)} %shard_map.59), channel_id=1, source_target_pairs={{0,35},{4,39},{8,43},{12,47},{16,51},{20,55},{24,59},{28,63},{1,0}... | collective-permute-start | bytes 1572872 | tf_op jit(solution)/shard_map/ppermute | solution.py:24
  91.3 3.7 %collective-permute-done.17.refs_5_ = bf16[17,16,128]{2,1,0:T(8,128)(2,1)S(1)} collective-permute-done((bf16[17,16,128]{2,1,0:T(8,128)(2,1)S(1)}, bf16[17,16,128]{2,1,0:T(8,128)(2,1)S(1)}, u32[]{:S(2)}, u32[]{:S(2)}) %collective-permute-start.17) | collective-permute-done | bytes 69664 | tf_op jit(solution)/shard_map/ppermute | solution.py:24
  95.0 3.1 %collective-permute-start.23 = (bf16[17,16,128]{2,1,0:T(8,128)(2,1)S(1)}, bf16[17,16,128]{2,1,0:T(8,128)(2,1)S(1)}, u32[]{:S(2)}, u32[]{:S(2)}) collective-permute-start(bf16[17,16,128]{2,1,0:T(8,128)(2,1)S(1)} %collective-permute-done.17.refs_5_), channel_id=1, source_target_pairs={{0,192},{4,196},{8,200},{12,204},{16,208},{20,212},{24,216},{28,22... | collective-permute-start | bytes 208904 | tf_op jit(solution)/shard_map/ppermute | solution.py:24
  100.7 3.2 %collective-permute-done.21.refs_9_ = bf16[17,16,128]{2,1,0:T(8,128)(2,1)S(1)} collective-permute-done((bf16[17,16,128]{2,1,0:T(8,128)(2,1)S(1)}, bf16[17,16,128]{2,1,0:T(8,128)(2,1)S(1)}, u32[]{:S(2)}, u32[]{:S(2)}) %collective-permute-start.21) | collective-permute-done | bytes 69664 | tf_op jit(solution)/shard_map/ppermute | solution.py:24
  104.5 1.9 %collective-permute-start.25 = (bf16[2,16,16,128]{3,2,1,0:T(8,128)(2,1)S(1)}, bf16[2,16,16,128]{3,2,1,0:T(8,128)(2,1)S(1)}, u32[]{:S(2)}, u32[]{:S(2)}) collective-permute-start(bf16[2,16,16,128]{3,2,1,0:T(8,128)(2,1)S(1)} %get-tuple-element.60), channel_id=1, source_target_pairs={{0,16},{4,20},{8,24},{12,28},{16,0},{20,4},{24,8},{28,12},{1,17},{... | collective-permute-start | bytes 393224 | tf_op jit(solution)/shard_map/ppermute | solution.py:24
  106.4 2.8 %collective-permute-start.26 = (bf16[2,16,16,128]{3,2,1,0:T(8,128)(2,1)S(1)}, bf16[2,16,16,128]{3,2,1,0:T(8,128)(2,1)S(1)}, u32[]{:S(2)}, u32[]{:S(2)}) collective-permute-start(bf16[2,16,16,128]{3,2,1,0:T(8,128)(2,1)S(1)} %get-tuple-element.61), channel_id=1, source_target_pairs={{0,24},{4,28},{8,16},{12,20},{16,8},{20,12},{24,0},{28,4},{1,25},{... | collective-permute-start | bytes 393224 | tf_op jit(solution)/shard_map/ppermute | solution.py:24
  109.2 2.6 %shard_map.61 = (bf16[2,128,512]{2,1,0:T(8,128)(2,1)S(1)}, bf16[2,128,512]{2,1,0:T(8,128)(2,1)S(1)}) custom-call(bf16[256,2048]{1,0:T(8,128)(2,1)S(1)} %get-tuple-element.68.tok, bf16[3,2048,512]{2,1,0:T(8,128)(2,1)S(1)} %shard_map.47.w, f32[8,256]{1,0:T(8,128)S(1)} %collective-permute-done.4.r0, f32[8,256]{1,0:T(8,128)S(1)} %collective-permute-done.5.r1, ...), custom_call_target="tpu_custom_call" | custom-call | flops 1073741824 | bytes 7880704 | tf_op jit(solution)/shard_map/pallas_call | solution.py:78
  111.9 2.9 %collective-permute-start.31 = (bf16[2,128,512]{2,1,0:T(8,128)(2,1)S(1)}, bf16[2,128,512]{2,1,0:T(8,128)(2,1)S(1)}, u32[]{:S(2)}, u32[]{:S(2)}) collective-permute-start(bf16[2,128,512]{2,1,0:T(8,128)(2,1)S(1)} %get-tuple-element.72), channel_id=1, source_target_pairs={{0,2},{4,6},{8,10},{12,14},{16,18},{20,22},{24,26},{28,30},{1,3},{... | collective-permute-start | bytes 786440 | tf_op jit(solution)/shard_map/ppermute | solution.py:24
  114.9 2.1 %shard_map.58.refs_0_ = bf16[2,256,512]{2,1,0:T(8,128)(2,1)S(1)} custom-call(bf16[256,2048]{1,0:T(8,128)(2,1)S(1)} %get-tuple-element.42.tok, bf16[3,2048,512]{2,1,0:T(8,128)(2,1)S(1)} %shard_map.47.w, f32[8,256]{1,0:T(8,128)S(1)} %get-tuple-element.43.rates, bf16[256,512]{1,0:T(8,128)(2,1)S(1)} %get-tuple-element.62.k_ref, ...), custom_call_target="tpu_custom_call" | custom-call | flops 1073741824 | bytes 7872512 | tf_op jit(solution)/shard_map/pallas_call | solution.py:78
  117.1 4.8 %collective-permute-done.30.refs_3_ = bf16[2,128,512]{2,1,0:T(8,128)(2,1)S(1)} collective-permute-done((bf16[2,128,512]{2,1,0:T(8,128)(2,1)S(1)}, bf16[2,128,512]{2,1,0:T(8,128)(2,1)S(1)}, u32[]{:S(2)}, u32[]{:S(2)}) %collective-permute-start.30) | collective-permute-done | bytes 262176 | tf_op jit(solution)/shard_map/ppermute | solution.py:24
  123.2 2.1 %shard_map.62 = bf16[256,2048]{1,0:T(8,128)(2,1)} custom-call(f32[256,128]{1,0:T(8,128)S(1)} %get-tuple-element.39.entry, f32[1,2048]{1,0:T(1,128)S(1)} %bitcast.5, bf16[4,128,128]{2,1,0:T(8,128)(2,1)S(1)} %collective-permute-done.6.s3.first_half, bf16[16,64,128]{2,1,0:T(8,128)(2,1)S(1)} %collective-permute-done.27.crossed, ...), custom_call_target="tpu_custom_call" | custom-call | bytes 3153920 | tf_op jit(solution)/shard_map/pallas_call | solution.py:78
  (55 shorter events, 13.6 us)
Async XLA Ops:
  0.0 25.3 %collective-permute-start.2 = (bf16[256,2048]{1,0:T(8,128)(2,1)}, bf16[256,2048]{1,0:T(8,128)(2,1)S(1)}, u32[]{:S(2)}, u32[]{:S(2)}) collective-permute-start(bf16[256,2048]{1,0:T(8,128)(2,1)} %bitcast.6), channel_id=1, source_target_pairs={{0,35},{4,39},{8,43},{12,47},{16,51},{20,55},{24,59},{28,63},{1,0}... | collective-permute-start | bytes 3145736 | tf_op jit(solution)/shard_map/ppermute | solution.py:24
  1.8 27.3 %collective-permute-start = (bf16[256,2048]{1,0:T(8,128)(2,1)}, bf16[256,2048]{1,0:T(8,128)(2,1)S(1)}, u32[]{:S(2)}, u32[]{:S(2)}) collective-permute-start(bf16[256,2048]{1,0:T(8,128)(2,1)} %bitcast.7), channel_id=1, source_target_pairs={{0,1},{4,5},{8,9},{12,13},{16,17},{20,21},{24,25},{28,29},{1,2},{5... | collective-permute-start | bytes 3145736 | tf_op jit(solution)/shard_map/ppermute | solution.py:24
  25.3 28.2 %collective-permute-start.3 = (bf16[128,2048]{1,0:T(8,128)(2,1)S(1)}, bf16[128,2048]{1,0:T(8,128)(2,1)S(1)}, u32[]{:S(2)}, u32[]{:S(2)}) collective-permute-start(bf16[128,2048]{1,0:T(8,128)(2,1)S(1)} %slice.9), channel_id=1, source_target_pairs={{0,35},{4,39},{8,43},{12,47},{16,51},{20,55},{24,59},{28,63},{1,0}... | collective-permute-start | bytes 1572872 | tf_op jit(solution)/shard_map/ppermute | solution.py:24
  29.1 24.4 %collective-permute-start.1 = (bf16[128,2048]{1,0:T(8,128)(2,1)S(1)}, bf16[128,2048]{1,0:T(8,128)(2,1)S(1)}, u32[]{:S(2)}, u32[]{:S(2)}) collective-permute-start(bf16[128,2048]{1,0:T(8,128)(2,1)S(1)} %slice.8), channel_id=1, source_target_pairs={{0,1},{4,5},{8,9},{12,13},{16,17},{20,21},{24,25},{28,29},{1,2},{5... | collective-permute-start | bytes 1572872 | tf_op jit(solution)/shard_map/ppermute | solution.py:24
  31.2 18.8 %collective-permute-start.5 = (f32[8,256]{1,0:T(8,128)S(1)}, f32[8,256]{1,0:T(8,128)S(1)}, u32[]{:S(2)}, u32[]{:S(2)}) collective-permute-start(f32[8,256]{1,0:T(8,128)S(1)} %get-tuple-element.40), channel_id=1, source_target_pairs={{0,34},{4,38},{8,42},{12,46},{16,50},{20,54},{24,58},{28,62},{1,35... | collective-permute-start | bytes 24584 | tf_op jit(solution)/shard_map/ppermute | solution.py:24
  37.3 16.3 %collective-permute-start.4 = (f32[8,256]{1,0:T(8,128)S(1)}, f32[8,256]{1,0:T(8,128)S(1)}, u32[]{:S(2)}, u32[]{:S(2)}) collective-permute-start(f32[8,256]{1,0:T(8,128)S(1)} %get-tuple-element.40), channel_id=1, source_target_pairs={{0,2},{4,6},{8,10},{12,14},{16,18},{20,22},{24,26},{28,30},{1,3},{... | collective-permute-start | bytes 24584 | tf_op jit(solution)/shard_map/ppermute | solution.py:24
  37.3 4.8 %collective-permute-start.9 = (f32[8,256]{1,0:T(8,128)S(1)}, f32[8,256]{1,0:T(8,128)S(1)}, u32[]{:S(2)}, u32[]{:S(2)}) collective-permute-start(f32[8,256]{1,0:T(8,128)S(1)} %get-tuple-element.47), channel_id=1, source_target_pairs={{0,35},{4,39},{8,43},{12,47},{16,51},{20,55},{24,59},{28,63},{1,0}... | collective-permute-start | bytes 24584 | tf_op jit(solution)/shard_map/ppermute | solution.py:24
  42.1 6.1 %collective-permute-start.7 = (f32[8,256]{1,0:T(8,128)S(1)}, f32[8,256]{1,0:T(8,128)S(1)}, u32[]{:S(2)}, u32[]{:S(2)}) collective-permute-start(f32[8,256]{1,0:T(8,128)S(1)} %get-tuple-element.45), channel_id=1, source_target_pairs={{0,1},{4,5},{8,9},{12,13},{16,17},{20,21},{24,25},{28,29},{1,2},{5... | collective-permute-start | bytes 24584 | tf_op jit(solution)/shard_map/ppermute | solution.py:24
  48.2 10.1 %collective-permute-start.10 = (bf16[4,128,128]{2,1,0:T(8,128)(2,1)S(1)}, bf16[4,128,128]{2,1,0:T(8,128)(2,1)S(1)}, u32[]{:S(2)}, u32[]{:S(2)}) collective-permute-start(bf16[4,128,128]{2,1,0:T(8,128)(2,1)S(1)} %get-tuple-element.48), channel_id=1, source_target_pairs={{0,1},{4,5},{8,9},{12,13},{16,17},{20,21},{24,25},{28,29},{1,2},{5... | collective-permute-start | bytes 393224 | tf_op jit(solution)/shard_map/ppermute | solution.py:24
  50.0 8.5 %collective-permute-start.8 = (bf16[4,128,128]{2,1,0:T(8,128)(2,1)S(1)}, bf16[4,128,128]{2,1,0:T(8,128)(2,1)S(1)}, u32[]{:S(2)}, u32[]{:S(2)}) collective-permute-start(bf16[4,128,128]{2,1,0:T(8,128)(2,1)S(1)} %get-tuple-element.46), channel_id=1, source_target_pairs={{0,35},{4,39},{8,43},{12,47},{16,51},{20,55},{24,59},{28,63},{1,0}... | collective-permute-start | bytes 393224 | tf_op jit(solution)/shard_map/ppermute | solution.py:24
  55.3 6.9 %collective-permute-start.6 = (bf16[4,128,128]{2,1,0:T(8,128)(2,1)S(1)}, bf16[4,128,128]{2,1,0:T(8,128)(2,1)S(1)}, u32[]{:S(2)}, u32[]{:S(2)}) collective-permute-start(bf16[4,128,128]{2,1,0:T(8,128)(2,1)S(1)} %get-tuple-element.41), channel_id=1, source_target_pairs={{0,34},{4,38},{8,42},{12,46},{16,50},{20,54},{24,58},{28,62},{1,35... | collective-permute-start | bytes 393224 | tf_op jit(solution)/shard_map/ppermute | solution.py:24
  58.1 8.5 %collective-permute-start.11 = (bf16[4,128,128]{2,1,0:T(8,128)(2,1)S(1)}, bf16[4,128,128]{2,1,0:T(8,128)(2,1)S(1)}, u32[]{:S(2)}, u32[]{:S(2)}) collective-permute-start(bf16[4,128,128]{2,1,0:T(8,128)(2,1)S(1)} %get-tuple-element.49), channel_id=1, source_target_pairs={{0,2},{4,6},{8,10},{12,14},{16,18},{20,22},{24,26},{28,30},{1,3},{... | collective-permute-start | bytes 393224 | tf_op jit(solution)/shard_map/ppermute | solution.py:24
  66.7 1.6 %collective-permute-start.12 = (bf16[16,64,128]{2,1,0:T(8,128)(2,1)S(1)}, bf16[16,64,128]{2,1,0:T(8,128)(2,1)S(1)}, u32[]{:S(2)}, u32[]{:S(2)}) collective-permute-start(bf16[16,64,128]{2,1,0:T(8,128)(2,1)S(1)} %get-tuple-element.52), channel_id=1, source_target_pairs={{0,4},{4,0},{8,12},{12,8},{16,20},{20,16},{24,28},{28,24},{1,5},{5... | collective-permute-start | bytes 786440 | tf_op jit(solution)/shard_map/ppermute | solution.py:24
  66.8 1.5 %collective-permute-start.13 = (bf16[16,128]{1,0:T(8,128)(2,1)S(1)}, bf16[16,128]{1,0:T(8,128)(2,1)S(1)}, u32[]{:S(2)}, u32[]{:S(2)}) collective-permute-start(bf16[16,128]{1,0:T(8,128)(2,1)S(1)} %get-tuple-element.53.total), channel_id=1, source_target_pairs={{0,4},{4,0},{8,12},{12,8},{16,20},{20,16},{24,28},{28,24},{1,5},{5... | collective-permute-start | bytes 12296 | tf_op jit(solution)/shard_map/ppermute | solution.py:24
  68.4 7.0 %collective-permute-start.14 = (bf16[2,17,16,128]{3,2,1,0:T(8,128)(2,1)S(1)}, bf16[2,17,16,128]{3,2,1,0:T(8,128)(2,1)S(1)}, u32[]{:S(2)}, u32[]{:S(2)}) collective-permute-start(bf16[2,17,16,128]{3,2,1,0:T(8,128)(2,1)S(1)} %get-tuple-element.55), channel_id=1, source_target_pairs={{0,8},{4,12},{8,0},{12,4},{16,24},{20,28},{24,16},{28,20},{1,9},{5... | collective-permute-start | bytes 417800 | tf_op jit(solution)/shard_map/ppermute | solution.py:24
  69.9 9.5 %collective-permute-start.15 = (bf16[2,17,16,128]{3,2,1,0:T(8,128)(2,1)S(1)}, bf16[2,17,16,128]{3,2,1,0:T(8,128)(2,1)S(1)}, u32[]{:S(2)}, u32[]{:S(2)}) collective-permute-start(bf16[2,17,16,128]{3,2,1,0:T(8,128)(2,1)S(1)} %get-tuple-element.56), channel_id=1, source_target_pairs={{0,16},{4,20},{8,24},{12,28},{16,0},{20,4},{24,8},{28,12},{1,17},{... | collective-permute-start | bytes 417800 | tf_op jit(solution)/shard_map/ppermute | solution.py:24
  72.7 9.1 %collective-permute-start.16 = (bf16[2,17,16,128]{3,2,1,0:T(8,128)(2,1)S(1)}, bf16[2,17,16,128]{3,2,1,0:T(8,128)(2,1)S(1)}, u32[]{:S(2)}, u32[]{:S(2)}) collective-permute-start(bf16[2,17,16,128]{3,2,1,0:T(8,128)(2,1)S(1)} %get-tuple-element.57), channel_id=1, source_target_pairs={{0,24},{4,28},{8,16},{12,20},{16,8},{20,12},{24,0},{28,4},{1,25},{... | collective-permute-start | bytes 417800 | tf_op jit(solution)/shard_map/ppermute | solution.py:24
  75.3 41.8 %collective-permute-start.29 = (bf16[2,256,512]{2,1,0:T(8,128)(2,1)S(1)}, bf16[2,256,512]{2,1,0:T(8,128)(2,1)S(1)}, u32[]{:S(2)}, u32[]{:S(2)}) collective-permute-start(bf16[2,256,512]{2,1,0:T(8,128)(2,1)S(1)} %shard_map.60), channel_id=1, source_target_pairs={{0,1},{4,5},{8,9},{12,13},{16,17},{20,21},{24,25},{28,29},{1,2},{5... | collective-permute-start | bytes 1572872 | tf_op jit(solution)/shard_map/ppermute | solution.py:24
  82.0 6.6 %collective-permute-start.22 = (bf16[17,16,128]{2,1,0:T(8,128)(2,1)S(1)}, bf16[17,16,128]{2,1,0:T(8,128)(2,1)S(1)}, u32[]{:S(2)}, u32[]{:S(2)}) collective-permute-start(bf16[17,16,128]{2,1,0:T(8,128)(2,1)S(1)} %shard_map.54.total.refs_4_), channel_id=1, source_target_pairs={{0,192},{4,196},{8,200},{12,204},{16,208},{20,212},{24,216},{28,22... | collective-permute-start | bytes 208904 | tf_op jit(solution)/shard_map/ppermute | solution.py:24
  85.1 13.0 %collective-permute-start.20 = (bf16[17,16,128]{2,1,0:T(8,128)(2,1)S(1)}, bf16[17,16,128]{2,1,0:T(8,128)(2,1)S(1)}, u32[]{:S(2)}, u32[]{:S(2)}) collective-permute-start(bf16[17,16,128]{2,1,0:T(8,128)(2,1)S(1)} %shard_map.54.total.refs_4_), channel_id=1, source_target_pairs={{0,128},{4,132},{8,136},{12,140},{16,144},{20,148},{24,152},{28,15... | collective-permute-start | bytes 208904 | tf_op jit(solution)/shard_map/ppermute | solution.py:24
  85.8 13.0 %collective-permute-start.18 = (bf16[17,16,128]{2,1,0:T(8,128)(2,1)S(1)}, bf16[17,16,128]{2,1,0:T(8,128)(2,1)S(1)}, u32[]{:S(2)}, u32[]{:S(2)}) collective-permute-start(bf16[17,16,128]{2,1,0:T(8,128)(2,1)S(1)} %shard_map.54.total.refs_4_), channel_id=1, source_target_pairs={{0,64},{4,68},{8,72},{12,76},{16,80},{20,84},{24,88},{28,92},{1,65... | collective-permute-start | bytes 208904 | tf_op jit(solution)/shard_map/ppermute | solution.py:24
  86.2 8.7 %collective-permute-start.17 = (bf16[17,16,128]{2,1,0:T(8,128)(2,1)S(1)}, bf16[17,16,128]{2,1,0:T(8,128)(2,1)S(1)}, u32[]{:S(2)}, u32[]{:S(2)}) collective-permute-start(bf16[17,16,128]{2,1,0:T(8,128)(2,1)S(1)} %shard_map.54.total.refs_4_), channel_id=1, source_target_pairs={{0,32},{4,36},{8,40},{12,44},{16,48},{20,52},{24,56},{28,60},{1,33... | collective-permute-start | bytes 208904 | tf_op jit(solution)/shard_map/ppermute | solution.py:24
  88.7 28.4 %collective-permute-start.28 = (bf16[2,256,512]{2,1,0:T(8,128)(2,1)S(1)}, bf16[2,256,512]{2,1,0:T(8,128)(2,1)S(1)}, u32[]{:S(2)}, u32[]{:S(2)}) collective-permute-start(bf16[2,256,512]{2,1,0:T(8,128)(2,1)S(1)} %shard_map.59), channel_id=1, source_target_pairs={{0,35},{4,39},{8,43},{12,47},{16,51},{20,55},{24,59},{28,63},{1,0}... | collective-permute-start | bytes 1572872 | tf_op jit(solution)/shard_map/ppermute | solution.py:24
  95.0 5.8 %collective-permute-start.23 = (bf16[17,16,128]{2,1,0:T(8,128)(2,1)S(1)}, bf16[17,16,128]{2,1,0:T(8,128)(2,1)S(1)}, u32[]{:S(2)}, u32[]{:S(2)}) collective-permute-start(bf16[17,16,128]{2,1,0:T(8,128)(2,1)S(1)} %collective-permute-done.17.refs_5_), channel_id=1, source_target_pairs={{0,192},{4,196},{8,200},{12,204},{16,208},{20,212},{24,216},{28,22... | collective-permute-start | bytes 208904 | tf_op jit(solution)/shard_map/ppermute | solution.py:24
  98.1 5.8 %collective-permute-start.21 = (bf16[17,16,128]{2,1,0:T(8,128)(2,1)S(1)}, bf16[17,16,128]{2,1,0:T(8,128)(2,1)S(1)}, u32[]{:S(2)}, u32[]{:S(2)}) collective-permute-start(bf16[17,16,128]{2,1,0:T(8,128)(2,1)S(1)} %collective-permute-done.17.refs_5_), channel_id=1, source_target_pairs={{0,128},{4,132},{8,136},{12,140},{16,144},{20,148},{24,152},{28,15... | collective-permute-start | bytes 208904 | tf_op jit(solution)/shard_map/ppermute | solution.py:24
  98.7 5.2 %collective-permute-start.19 = (bf16[17,16,128]{2,1,0:T(8,128)(2,1)S(1)}, bf16[17,16,128]{2,1,0:T(8,128)(2,1)S(1)}, u32[]{:S(2)}, u32[]{:S(2)}) collective-permute-start(bf16[17,16,128]{2,1,0:T(8,128)(2,1)S(1)} %collective-permute-done.17.refs_5_), channel_id=1, source_target_pairs={{0,64},{4,68},{8,72},{12,76},{16,80},{20,84},{24,88},{28,92},{1,65... | collective-permute-start | bytes 208904 | tf_op jit(solution)/shard_map/ppermute | solution.py:24
  104.4 7.4 %collective-permute-start.24 = (bf16[2,16,16,128]{3,2,1,0:T(8,128)(2,1)S(1)}, bf16[2,16,16,128]{3,2,1,0:T(8,128)(2,1)S(1)}, u32[]{:S(2)}, u32[]{:S(2)}) collective-permute-start(bf16[2,16,16,128]{3,2,1,0:T(8,128)(2,1)S(1)} %get-tuple-element.59), channel_id=1, source_target_pairs={{0,8},{4,12},{8,0},{12,4},{16,24},{20,28},{24,16},{28,20},{1,9},{5... | collective-permute-start | bytes 393224 | tf_op jit(solution)/shard_map/ppermute | solution.py:24
  104.5 7.4 %collective-permute-start.25 = (bf16[2,16,16,128]{3,2,1,0:T(8,128)(2,1)S(1)}, bf16[2,16,16,128]{3,2,1,0:T(8,128)(2,1)S(1)}, u32[]{:S(2)}, u32[]{:S(2)}) collective-permute-start(bf16[2,16,16,128]{3,2,1,0:T(8,128)(2,1)S(1)} %get-tuple-element.60), channel_id=1, source_target_pairs={{0,16},{4,20},{8,24},{12,28},{16,0},{20,4},{24,8},{28,12},{1,17},{... | collective-permute-start | bytes 393224 | tf_op jit(solution)/shard_map/ppermute | solution.py:24
  106.4 8.4 %collective-permute-start.26 = (bf16[2,16,16,128]{3,2,1,0:T(8,128)(2,1)S(1)}, bf16[2,16,16,128]{3,2,1,0:T(8,128)(2,1)S(1)}, u32[]{:S(2)}, u32[]{:S(2)}) collective-permute-start(bf16[2,16,16,128]{3,2,1,0:T(8,128)(2,1)S(1)} %get-tuple-element.61), channel_id=1, source_target_pairs={{0,24},{4,28},{8,16},{12,20},{16,8},{20,12},{24,0},{28,4},{1,25},{... | collective-permute-start | bytes 393224 | tf_op jit(solution)/shard_map/ppermute | solution.py:24
  111.8 10.1 %collective-permute-start.30 = (bf16[2,128,512]{2,1,0:T(8,128)(2,1)S(1)}, bf16[2,128,512]{2,1,0:T(8,128)(2,1)S(1)}, u32[]{:S(2)}, u32[]{:S(2)}) collective-permute-start(bf16[2,128,512]{2,1,0:T(8,128)(2,1)S(1)} %get-tuple-element.71), channel_id=1, source_target_pairs={{0,34},{4,38},{8,42},{12,46},{16,50},{20,54},{24,58},{28,62},{1,35... | collective-permute-start | bytes 786440 | tf_op jit(solution)/shard_map/ppermute | solution.py:24
  111.9 11.4 %collective-permute-start.31 = (bf16[2,128,512]{2,1,0:T(8,128)(2,1)S(1)}, bf16[2,128,512]{2,1,0:T(8,128)(2,1)S(1)}, u32[]{:S(2)}, u32[]{:S(2)}) collective-permute-start(bf16[2,128,512]{2,1,0:T(8,128)(2,1)S(1)} %get-tuple-element.72), channel_id=1, source_target_pairs={{0,2},{4,6},{8,10},{12,14},{16,18},{20,22},{24,26},{28,30},{1,3},{... | collective-permute-start | bytes 786440 | tf_op jit(solution)/shard_map/ppermute | solution.py:24
  114.8 8.4 %collective-permute-start.27 = (bf16[16,64,128]{2,1,0:T(8,128)(2,1)S(1)}, bf16[16,64,128]{2,1,0:T(8,128)(2,1)S(1)}, u32[]{:S(2)}, u32[]{:S(2)}) collective-permute-start(bf16[16,64,128]{2,1,0:T(8,128)(2,1)S(1)} %shard_map.57), channel_id=1, source_target_pairs={{0,4},{4,0},{8,12},{12,8},{16,20},{20,16},{24,28},{28,24},{1,5},{5... | collective-permute-start | bytes 786440 | tf_op jit(solution)/shard_map/ppermute | solution.py:24
  (2 other events, 12.2 us)

commit v5 on v4

--- a/solution.py
+++ b/solution.py
@@ -175,6 +175,13 @@
     states_of(tok, w, running(rates[...]), k_out, v_out, [local], 256)
 
 
+def states_joined(t0, t1, w, rates, *refs):
+    tok, k_out, v_out, local = refs[-4:]
+    tok[0:128, :] = t0[...]
+    tok[128:256, :] = t1[...]
+    states_of(tok, w, running(rates[...]), k_out, v_out, [local], 256)
+
+
 def two_rates(first, second):
     lane = lax.broadcasted_iota(jnp.int32, (8, 256), 1)
     return running(jnp.where(lane < 128, first[...], second[...]), 128)
@@ -206,8 +213,8 @@
                 out[1, :, cols] = value.astype(BF16)
 
 
-def insides(tok, w, rates, k_ref, v_ref, out):
-    insides_of(tok, w, running(rates[...]), k_ref, v_ref, [out], 256)
+def insides(tok, w, rates, k_ref, v_ref, *refs):
+    insides_of(tok, w, running(rates[...]), k_ref, v_ref, [refs[-1]], 256)
 
 
 def insides_two(tok, w, r0, r1, k_ref, v_ref, out0, out1):
@@ -332,8 +339,9 @@
     state = ((4, 128, 128), BF16)
     half = ((n, 512), BF16)
 
-    from_up = send(tok, up)
-    from_down = send(tok, down)
+    early, late = tok[:128], tok[128:]
+    early_up, late_down = send(early, up), send(late, down)
+    late_up, early_down = send(late, up), send(early, down)
     *rates, entry, total, second, held = call(
         prepare,
         [((8, n), F32)] * 4 + [((n, 128), F32), ((16, 128), BF16), ((8, 128), F32), ((n, d), BF16)],
@@ -345,32 +353,41 @@
         send(a, m) for a, m in zip((*rates[1:], rates[3]), (up, down, up_two, down_two))
     ]
     partner_total = send(total, other)
-    first = send(from_up[:128], up)
-    last = send(from_down[128:], down)
+    first = send(early_up, up)
+    last = send(late_down, down)
     weight = call(load, [(qkv_weight.shape, BF16)], qkv_weight, far=1)[0]
 
-    toks, made = [held, from_up, from_down], []
-    for i in range(3):
-        after = (made[0][2],) if made else ()
-        made.append(call(states, [half, half, state], toks[i], weight, rates[i], *after, flops=1 << 30))
+    made = [[held, *call(states, [half, half, state], held, weight, rates[0], flops=1 << 30)]]
+    for i, halves in ((1, (early_up, late_up)), (2, (early_down, late_down))):
+        made.append(
+            call(
+                states_joined,
+                [((n, d), BF16), half, half, state],
+                *halves,
+                weight,
+                rates[i],
+                made[0][3],
+                flops=1 << 30,
+            )
+        )
     two = call(
         states_two, [((n, d), BF16), half, half, state, state], first, last, weight, *rates[3:], flops=1 << 30
     )
     first_half, last_half = send(two[3], down_two), send(two[4], up_two)
-    back_1 = send(made[1][2], down)
-    back_2 = send(made[2][2], up)
-
+    back_1 = send(made[1][3], down)
+    back_2 = send(made[2][3], up)
+
+    last_parts = call(insides_two, [((2, 128, 512), BF16)] * 2, two[0], weight, *rates[3:], *two[1:3], flops=1 << 30)
     parts = []
     for i in range(3):
-        parts += call(
-            insides, [((2, n, 512), BF16)], toks[i], weight, rates[i], *made[i][:2], flops=1 << 30
-        )
-    parts += call(insides_two, [((2, 128, 512), BF16)] * 2, two[0], weight, *rates[3:], *two[1:3], flops=1 << 30)
+        after = (last_parts[0],) if i == 2 else ()
+        parts += call(insides, [((2, n, 512), BF16)], made[i][0], weight, rates[i], *made[i][1:3], *after, flops=1 << 30)
+    parts += last_parts
     for i, m in enumerate((down, up, down_two, up_two)):
         parts[i + 1] = send(parts[i + 1], m)
 
     same, cross = call(
-        halve, [((16, 64, 128), BF16)] * 2, made[0][2], back_1, back_2, first_half, last_half, second
+        halve, [((16, 64, 128), BF16)] * 2, made[0][3], back_1, back_2, first_half, last_half, second
     )
     partner = send(cross, other)
     pieces = call(deal, [((2, 17, 16, 128), BF16)] * 4, same, partner, total, partner_total)

time: 126 us -> 124 us (0.984)
  the two profiles are of different devices: /device:TPU:32 before, /device:TPU:2 now
where the time goes in v5:
time: 124 us
  waiting for transfers between devices  49.1 us (40%)
  starting transfers between devices  48.9 us (39%)
  Pallas kernels  23.3 us (19%)
  local copies, waits for them, and re-layouts  2.01 us (2%)
    ppermute x34, waiting for transfers between devices, send(): return lax.ppermute(a, BOTH, pairs(move))  49.1 us
    ppermute x34, starting transfers between devices, send(): return lax.ppermute(a, BOTH, pairs(move))  48.9 us
    pallas_call x17, Pallas kernels, call(): pl.pallas_call(kernel, in_specs=[VMEM] * near + [pl.BlockSpec(memory_spac...  23.3 us
  transfers between devices with their start and end apart: 34, of which 14 were waited for; matrix products, arithmetic and copies ran while one was open for 0% of the time, Pallas kernels for 17%

profile of v5, /device:TPU:2, one launch (start us, length us, event | category | flops | bytes accessed | tf_op | source)
XLA Modules:
  0.0 123.6 jit_solution(11708659325342533643)
XLA Ops:
  1.3 5.9 %collective-permute-start.2 = (bf16[128,2048]{1,0:T(8,128)(2,1)S(1)}, bf16[128,2048]{1,0:T(8,128)(2,1)S(1)}, u32[]{:S(2)}, u32[]{:S(2)}) collective-permute-start(bf16[128,2048]{1,0:T(8,128)(2,1)S(1)} %get-tuple-element.77), channel_id=1, source_target_pairs={{0,35},{4,39},{8,43},{12,47},{16,51},{20,55},{24,59},{28,63},{1,0}... | collective-permute-start | bytes 1572872 | tf_op jit(solution)/shard_map/ppermute | solution.py:24
  7.2 3.2 %collective-permute-start.10 = (bf16[128,2048]{1,0:T(8,128)(2,1)S(1)}, bf16[128,2048]{1,0:T(8,128)(2,1)S(1)}, u32[]{:S(2)}, u32[]{:S(2)}) collective-permute-start(bf16[128,2048]{1,0:T(8,128)(2,1)S(1)} %get-tuple-element.78), channel_id=1, source_target_pairs={{0,35},{4,39},{8,43},{12,47},{16,51},{20,55},{24,59},{28,63},{1,0}... | collective-permute-start | bytes 1572872 | tf_op jit(solution)/shard_map/ppermute | solution.py:24
  10.5 9.1 %collective-permute-done.2.t1 = bf16[128,2048]{1,0:T(8,128)(2,1)S(1)} collective-permute-done((bf16[128,2048]{1,0:T(8,128)(2,1)S(1)}, bf16[128,2048]{1,0:T(8,128)(2,1)S(1)}, u32[]{:S(2)}, u32[]{:S(2)}) %collective-permute-start.2) | collective-permute-done | bytes 524320 | tf_op jit(solution)/shard_map/ppermute | solution.py:24
  19.5 3.7 %collective-permute-start.3 = (bf16[128,2048]{1,0:T(8,128)(2,1)S(1)}, bf16[128,2048]{1,0:T(8,128)(2,1)S(1)}, u32[]{:S(2)}, u32[]{:S(2)}) collective-permute-start(bf16[128,2048]{1,0:T(8,128)(2,1)S(1)} %collective-permute-done.2.t1), channel_id=1, source_target_pairs={{0,35},{4,39},{8,43},{12,47},{16,51},{20,55},{24,59},{28,63},{1,0}... | collective-permute-start | bytes 1572872 | tf_op jit(solution)/shard_map/ppermute | solution.py:24
  25.2 3.3 %collective-permute-start.11 = (f32[8,256]{1,0:T(8,128)S(1)}, f32[8,256]{1,0:T(8,128)S(1)}, u32[]{:S(2)}, u32[]{:S(2)}) collective-permute-start(f32[8,256]{1,0:T(8,128)S(1)} %get-tuple-element.49), channel_id=1, source_target_pairs={{0,35},{4,39},{8,43},{12,47},{16,51},{20,55},{24,59},{28,63},{1,0}... | collective-permute-start | bytes 24584 | tf_op jit(solution)/shard_map/ppermute | solution.py:24
  28.5 2.8 %shard_map.47.w = bf16[3,2048,512]{2,1,0:T(8,128)(2,1)S(1)} custom-call(bf16[3,2048,512]{2,1,0:T(8,128)(2,1)} %w.1), custom_call_target="tpu_custom_call" | custom-call | bytes 6291456 | tf_op jit(solution)/shard_map/pallas_call | solution.py:78
  31.3 1.8 %shard_map.49 = (bf16[256,512]{1,0:T(8,128)(2,1)S(1)}, bf16[256,512]{1,0:T(8,128)(2,1)S(1)}, bf16[4,128,128]{2,1,0:T(8,128)(2,1)S(1)}) custom-call(bf16[256,2048]{1,0:T(8,128)(2,1)S(1)} %get-tuple-element.44.tok, bf16[3,2048,512]{2,1,0:T(8,128)(2,1)S(1)} %shard_map.47.w, f32[8,256]{1,0:T(8,128)S(1)} %get-tuple-element.45.rates), custom_call_target="tpu_custom_call" | custom-call | flops 1073741824 | bytes 7348224 | tf_op jit(solution)/shard_map/pallas_call | solution.py:78
  33.1 7.9 %collective-permute-done.11.rates = f32[8,256]{1,0:T(8,128)S(1)} collective-permute-done((f32[8,256]{1,0:T(8,128)S(1)}, f32[8,256]{1,0:T(8,128)S(1)}, u32[]{:S(2)}, u32[]{:S(2)}) %collective-permute-start.11) | collective-permute-done | bytes 8224 | tf_op jit(solution)/shard_map/ppermute | solution.py:24
  41.1 5.2 %collective-permute-start.5 = (f32[8,256]{1,0:T(8,128)S(1)}, f32[8,256]{1,0:T(8,128)S(1)}, u32[]{:S(2)}, u32[]{:S(2)}) collective-permute-start(f32[8,256]{1,0:T(8,128)S(1)} %get-tuple-element.42), channel_id=1, source_target_pairs={{0,34},{4,38},{8,42},{12,46},{16,50},{20,54},{24,58},{28,62},{1,35... | collective-permute-start | bytes 24584 | tf_op jit(solution)/shard_map/ppermute | solution.py:24
  46.2 1.8 %shard_map.51 = (bf16[256,2048]{1,0:T(8,128)(2,1)S(1)}, bf16[256,512]{1,0:T(8,128)(2,1)S(1)}, bf16[256,512]{1,0:T(8,128)(2,1)S(1)}, bf16[4,128,128]{2,1,0:T(8,128)(2,1)S(1)}) custom-call(bf16[128,2048]{1,0:T(8,128)(2,1)S(1)} %collective-permute-done.10.t0, bf16[128,2048]{1,0:T(8,128)(2,1)S(1)} %collective-permute-done.2.t1, ...), custom_call_target="tpu_custom_call" | custom-call | flops 1073741824 | bytes 7479296 | tf_op jit(solution)/shard_map/pallas_call | solution.py:78
  48.4 1.8 %shard_map.50 = (bf16[256,2048]{1,0:T(8,128)(2,1)S(1)}, bf16[256,512]{1,0:T(8,128)(2,1)S(1)}, bf16[256,512]{1,0:T(8,128)(2,1)S(1)}, bf16[4,128,128]{2,1,0:T(8,128)(2,1)S(1)}) custom-call(bf16[128,2048]{1,0:T(8,128)(2,1)S(1)} %collective-permute-done.t0, bf16[128,2048]{1,0:T(8,128)(2,1)S(1)} %collective-permute-done.7.t1, ...), custom_call_target="tpu_custom_call" | custom-call | flops 1073741824 | bytes 7479296 | tf_op jit(solution)/shard_map/pallas_call | solution.py:78
  50.2 3.3 %collective-permute-start.9 = (bf16[4,128,128]{2,1,0:T(8,128)(2,1)S(1)}, bf16[4,128,128]{2,1,0:T(8,128)(2,1)S(1)}, u32[]{:S(2)}, u32[]{:S(2)}) collective-permute-start(bf16[4,128,128]{2,1,0:T(8,128)(2,1)S(1)} %get-tuple-element.48), channel_id=1, source_target_pairs={{0,35},{4,39},{8,43},{12,47},{16,51},{20,55},{24,59},{28,63},{1,0}... | collective-permute-start | bytes 393224 | tf_op jit(solution)/shard_map/ppermute | solution.py:24
  54.0 1.8 %shard_map.48 = (bf16[256,2048]{1,0:T(8,128)(2,1)S(1)}, bf16[256,512]{1,0:T(8,128)(2,1)S(1)}, bf16[256,512]{1,0:T(8,128)(2,1)S(1)}, bf16[4,128,128]{2,1,0:T(8,128)(2,1)S(1)}, bf16[4,128,128]{2,1,0:T(8,128)(2,1)S(1)}) custom-call(bf16[128,2048]{1,0:T(8,128)(2,1)S(1)} %collective-permute-done.1.t0, bf16[128,2048]{1,0:T(8,128)(2,1)S(1)} %collective-permute-done.3.t1, ...), custom_call_target="tpu_custom_call" | custom-call | flops 1073741824 | bytes 7356416 | tf_op jit(solution)/shard_map/pallas_call | solution.py:78
  55.8 2.3 %collective-permute-start.6 = (bf16[4,128,128]{2,1,0:T(8,128)(2,1)S(1)}, bf16[4,128,128]{2,1,0:T(8,128)(2,1)S(1)}, u32[]{:S(2)}, u32[]{:S(2)}) collective-permute-start(bf16[4,128,128]{2,1,0:T(8,128)(2,1)S(1)} %get-tuple-element.43), channel_id=1, source_target_pairs={{0,34},{4,38},{8,42},{12,46},{16,50},{20,54},{24,58},{28,62},{1,35... | collective-permute-start | bytes 393224 | tf_op jit(solution)/shard_map/ppermute | solution.py:24
  58.8 4.0 %collective-permute-done.6.s3.first_half = bf16[4,128,128]{2,1,0:T(8,128)(2,1)S(1)} collective-permute-done((bf16[4,128,128]{2,1,0:T(8,128)(2,1)S(1)}, bf16[4,128,128]{2,1,0:T(8,128)(2,1)S(1)}, u32[]{:S(2)}, u32[]{:S(2)}) %collective-permute-start.6) | collective-permute-done | bytes 131104 | tf_op jit(solution)/shard_map/ppermute | solution.py:24
  62.8 3.2 %collective-permute-done.13.s4 = bf16[4,128,128]{2,1,0:T(8,128)(2,1)S(1)} collective-permute-done((bf16[4,128,128]{2,1,0:T(8,128)(2,1)S(1)}, bf16[4,128,128]{2,1,0:T(8,128)(2,1)S(1)}, u32[]{:S(2)}, u32[]{:S(2)}) %collective-permute-start.13) | collective-permute-done | bytes 131104 | tf_op jit(solution)/shard_map/ppermute | solution.py:24
  68.4 2.4 %collective-permute-start.17 = (bf16[2,17,16,128]{3,2,1,0:T(8,128)(2,1)S(1)}, bf16[2,17,16,128]{3,2,1,0:T(8,128)(2,1)S(1)}, u32[]{:S(2)}, u32[]{:S(2)}) collective-permute-start(bf16[2,17,16,128]{3,2,1,0:T(8,128)(2,1)S(1)} %get-tuple-element.58), channel_id=1, source_target_pairs={{0,16},{4,20},{8,24},{12,28},{16,0},{20,4},{24,8},{28,12},{1,17},{... | collective-permute-start | bytes 417800 | tf_op jit(solution)/shard_map/ppermute | solution.py:24
  71.4 2.1 %shard_map.59 = bf16[2,256,512]{2,1,0:T(8,128)(2,1)S(1)} custom-call(bf16[256,2048]{1,0:T(8,128)(2,1)S(1)} %get-tuple-element.66.tok, bf16[3,2048,512]{2,1,0:T(8,128)(2,1)S(1)} %shard_map.47.w, f32[8,256]{1,0:T(8,128)S(1)} %collective-permute-done.8.rates, bf16[256,512]{1,0:T(8,128)(2,1)S(1)} %get-tuple-element.67.k_ref, ...), custom_call_target="tpu_custom_call" | custom-call | flops 1073741824 | bytes 7872512 | tf_op jit(solution)/shard_map/pallas_call | solution.py:78
  73.6 2.6 %shard_map.60 = (bf16[2,128,512]{2,1,0:T(8,128)(2,1)S(1)}, bf16[2,128,512]{2,1,0:T(8,128)(2,1)S(1)}) custom-call(bf16[256,2048]{1,0:T(8,128)(2,1)S(1)} %get-tuple-element.72.tok, bf16[3,2048,512]{2,1,0:T(8,128)(2,1)S(1)} %shard_map.47.w, f32[8,256]{1,0:T(8,128)S(1)} %collective-permute-done.4.r0, f32[8,256]{1,0:T(8,128)S(1)} %collective-permute-done.5.r1, ...), custom_call_target="tpu_custom_call" | custom-call | flops 1073741824 | bytes 7880704 | tf_op jit(solution)/shard_map/pallas_call | solution.py:78
  79.2 3.1 %collective-permute-start.24 = (bf16[17,16,128]{2,1,0:T(8,128)(2,1)S(1)}, bf16[17,16,128]{2,1,0:T(8,128)(2,1)S(1)}, u32[]{:S(2)}, u32[]{:S(2)}) collective-permute-start(bf16[17,16,128]{2,1,0:T(8,128)(2,1)S(1)} %shard_map.54.total.refs_4_), channel_id=1, source_target_pairs={{0,192},{4,196},{8,200},{12,204},{16,208},{20,212},{24,216},{28,22... | collective-permute-start | bytes 208904 | tf_op jit(solution)/shard_map/ppermute | solution.py:24
  83.5 1.6 %collective-permute-start.19 = (bf16[17,16,128]{2,1,0:T(8,128)(2,1)S(1)}, bf16[17,16,128]{2,1,0:T(8,128)(2,1)S(1)}, u32[]{:S(2)}, u32[]{:S(2)}) collective-permute-start(bf16[17,16,128]{2,1,0:T(8,128)(2,1)S(1)} %shard_map.54.total.refs_4_), channel_id=1, source_target_pairs={{0,32},{4,36},{8,40},{12,44},{16,48},{20,52},{24,56},{28,60},{1,33... | collective-permute-start | bytes 208904 | tf_op jit(solution)/shard_map/ppermute | solution.py:24
  85.1 2.1 %shard_map.61 = bf16[2,256,512]{2,1,0:T(8,128)(2,1)S(1)} custom-call(bf16[256,2048]{1,0:T(8,128)(2,1)S(1)} %get-tuple-element.69.tok, bf16[3,2048,512]{2,1,0:T(8,128)(2,1)S(1)} %shard_map.47.w, f32[8,256]{1,0:T(8,128)S(1)} %collective-permute-done.11.rates, bf16[256,512]{1,0:T(8,128)(2,1)S(1)} %get-tuple-element.70.k_ref, ...), custom_call_target="tpu_custom_call" | custom-call | flops 1073741824 | bytes 8134656 | tf_op jit(solution)/shard_map/pallas_call | solution.py:78
  87.3 2.4 %collective-permute-start.31 = (bf16[2,256,512]{2,1,0:T(8,128)(2,1)S(1)}, bf16[2,256,512]{2,1,0:T(8,128)(2,1)S(1)}, u32[]{:S(2)}, u32[]{:S(2)}) collective-permute-start(bf16[2,256,512]{2,1,0:T(8,128)(2,1)S(1)} %shard_map.61), channel_id=1, source_target_pairs={{0,1},{4,5},{8,9},{12,13},{16,17},{20,21},{24,25},{28,29},{1,2},{5... | collective-permute-start | bytes 1572872 | tf_op jit(solution)/shard_map/ppermute | solution.py:24
  89.7 3.4 %collective-permute-done.19.refs_5_ = bf16[17,16,128]{2,1,0:T(8,128)(2,1)S(1)} collective-permute-done((bf16[17,16,128]{2,1,0:T(8,128)(2,1)S(1)}, bf16[17,16,128]{2,1,0:T(8,128)(2,1)S(1)}, u32[]{:S(2)}, u32[]{:S(2)}) %collective-permute-start.19) | collective-permute-done | bytes 69664 | tf_op jit(solution)/shard_map/ppermute | solution.py:24
  93.1 3.0 %collective-permute-start.25 = (bf16[17,16,128]{2,1,0:T(8,128)(2,1)S(1)}, bf16[17,16,128]{2,1,0:T(8,128)(2,1)S(1)}, u32[]{:S(2)}, u32[]{:S(2)}) collective-permute-start(bf16[17,16,128]{2,1,0:T(8,128)(2,1)S(1)} %collective-permute-done.19.refs_5_), channel_id=1, source_target_pairs={{0,192},{4,196},{8,200},{12,204},{16,208},{20,212},{24,216},{28,22... | collective-permute-start | bytes 208904 | tf_op jit(solution)/shard_map/ppermute | solution.py:24
  98.6 3.3 %collective-permute-done.23.refs_9_ = bf16[17,16,128]{2,1,0:T(8,128)(2,1)S(1)} collective-permute-done((bf16[17,16,128]{2,1,0:T(8,128)(2,1)S(1)}, bf16[17,16,128]{2,1,0:T(8,128)(2,1)S(1)}, u32[]{:S(2)}, u32[]{:S(2)}) %collective-permute-start.23) | collective-permute-done | bytes 69664 | tf_op jit(solution)/shard_map/ppermute | solution.py:24
  102.3 2.7 %collective-permute-start.26 = (bf16[2,16,16,128]{3,2,1,0:T(8,128)(2,1)S(1)}, bf16[2,16,16,128]{3,2,1,0:T(8,128)(2,1)S(1)}, u32[]{:S(2)}, u32[]{:S(2)}) collective-permute-start(bf16[2,16,16,128]{3,2,1,0:T(8,128)(2,1)S(1)} %get-tuple-element.61), channel_id=1, source_target_pairs={{0,8},{4,12},{8,0},{12,4},{16,24},{20,28},{24,16},{28,20},{1,9},{5... | collective-permute-start | bytes 393224 | tf_op jit(solution)/shard_map/ppermute | solution.py:24
  105.1 1.6 %collective-permute-start.28 = (bf16[2,16,16,128]{3,2,1,0:T(8,128)(2,1)S(1)}, bf16[2,16,16,128]{3,2,1,0:T(8,128)(2,1)S(1)}, u32[]{:S(2)}, u32[]{:S(2)}) collective-permute-start(bf16[2,16,16,128]{3,2,1,0:T(8,128)(2,1)S(1)} %get-tuple-element.63), channel_id=1, source_target_pairs={{0,24},{4,28},{8,16},{12,20},{16,8},{20,12},{24,0},{28,4},{1,25},{... | collective-permute-start | bytes 393224 | tf_op jit(solution)/shard_map/ppermute | solution.py:24
  108.0 3.5 %collective-permute-done.27.p2.refs_7_ = bf16[2,16,16,128]{3,2,1,0:T(8,128)(2,1)S(1)} collective-permute-done((bf16[2,16,16,128]{3,2,1,0:T(8,128)(2,1)S(1)}, bf16[2,16,16,128]{3,2,1,0:T(8,128)(2,1)S(1)}, u32[]{:S(2)}, u32[]{:S(2)}) %collective-permute-start.27) | collective-permute-done | bytes 131104 | tf_op jit(solution)/shard_map/ppermute | solution.py:24
  111.7 2.1 %shard_map.58.refs_0_ = bf16[2,256,512]{2,1,0:T(8,128)(2,1)S(1)} custom-call(bf16[256,2048]{1,0:T(8,128)(2,1)S(1)} %get-tuple-element.44.tok, bf16[3,2048,512]{2,1,0:T(8,128)(2,1)S(1)} %shard_map.47.w, f32[8,256]{1,0:T(8,128)S(1)} %get-tuple-element.45.rates, bf16[256,512]{1,0:T(8,128)(2,1)S(1)} %get-tuple-element.64.k_ref, ...), custom_call_target="tpu_custom_call" | custom-call | flops 1073741824 | bytes 7872512 | tf_op jit(solution)/shard_map/pallas_call | solution.py:78
  113.8 7.6 %collective-permute-done.33.refs_4_ = bf16[2,128,512]{2,1,0:T(8,128)(2,1)S(1)} collective-permute-done((bf16[2,128,512]{2,1,0:T(8,128)(2,1)S(1)}, bf16[2,128,512]{2,1,0:T(8,128)(2,1)S(1)}, u32[]{:S(2)}, u32[]{:S(2)}) %collective-permute-start.33) | collective-permute-done | bytes 262176 | tf_op jit(solution)/shard_map/ppermute | solution.py:24
  121.5 2.1 %shard_map.62 = bf16[256,2048]{1,0:T(8,128)(2,1)} custom-call(f32[256,128]{1,0:T(8,128)S(1)} %get-tuple-element.41.entry, f32[1,2048]{1,0:T(1,128)S(1)} %bitcast.9, bf16[4,128,128]{2,1,0:T(8,128)(2,1)S(1)} %collective-permute-done.6.s3.first_half, bf16[16,64,128]{2,1,0:T(8,128)(2,1)S(1)} %collective-permute-done.29.crossed, ...), custom_call_target="tpu_custom_call" | custom-call | bytes 3153920 | tf_op jit(solution)/shard_map/pallas_call | solution.py:78
  (58 shorter events, 16.5 us)
Async XLA Ops:
  1.3 18.2 %collective-permute-start.2 = (bf16[128,2048]{1,0:T(8,128)(2,1)S(1)}, bf16[128,2048]{1,0:T(8,128)(2,1)S(1)}, u32[]{:S(2)}, u32[]{:S(2)}) collective-permute-start(bf16[128,2048]{1,0:T(8,128)(2,1)S(1)} %get-tuple-element.77), channel_id=1, source_target_pairs={{0,35},{4,39},{8,43},{12,47},{16,51},{20,55},{24,59},{28,63},{1,0}... | collective-permute-start | bytes 1572872 | tf_op jit(solution)/shard_map/ppermute | solution.py:24
  7.2 16.0 %collective-permute-start = (bf16[128,2048]{1,0:T(8,128)(2,1)S(1)}, bf16[128,2048]{1,0:T(8,128)(2,1)S(1)}, u32[]{:S(2)}, u32[]{:S(2)}) collective-permute-start(bf16[128,2048]{1,0:T(8,128)(2,1)S(1)} %get-tuple-element.78), channel_id=1, source_target_pairs={{0,1},{4,5},{8,9},{12,13},{16,17},{20,21},{24,25},{28,29},{1,2},{5... | collective-permute-start | bytes 1572872 | tf_op jit(solution)/shard_map/ppermute | solution.py:24
  7.2 33.8 %collective-permute-start.10 = (bf16[128,2048]{1,0:T(8,128)(2,1)S(1)}, bf16[128,2048]{1,0:T(8,128)(2,1)S(1)}, u32[]{:S(2)}, u32[]{:S(2)}) collective-permute-start(bf16[128,2048]{1,0:T(8,128)(2,1)S(1)} %get-tuple-element.78), channel_id=1, source_target_pairs={{0,35},{4,39},{8,43},{12,47},{16,51},{20,55},{24,59},{28,63},{1,0}... | collective-permute-start | bytes 1572872 | tf_op jit(solution)/shard_map/ppermute | solution.py:24
  10.5 37.7 %collective-permute-start.7 = (bf16[128,2048]{1,0:T(8,128)(2,1)S(1)}, bf16[128,2048]{1,0:T(8,128)(2,1)S(1)}, u32[]{:S(2)}, u32[]{:S(2)}) collective-permute-start(bf16[128,2048]{1,0:T(8,128)(2,1)S(1)} %get-tuple-element.77), channel_id=1, source_target_pairs={{0,1},{4,5},{8,9},{12,13},{16,17},{20,21},{24,25},{28,29},{1,2},{5... | collective-permute-start | bytes 1572872 | tf_op jit(solution)/shard_map/ppermute | solution.py:24
  19.5 34.4 %collective-permute-start.3 = (bf16[128,2048]{1,0:T(8,128)(2,1)S(1)}, bf16[128,2048]{1,0:T(8,128)(2,1)S(1)}, u32[]{:S(2)}, u32[]{:S(2)}) collective-permute-start(bf16[128,2048]{1,0:T(8,128)(2,1)S(1)} %collective-permute-done.2.t1), channel_id=1, source_target_pairs={{0,35},{4,39},{8,43},{12,47},{16,51},{20,55},{24,59},{28,63},{1,0}... | collective-permute-start | bytes 1572872 | tf_op jit(solution)/shard_map/ppermute | solution.py:24
  23.2 30.7 %collective-permute-start.1 = (bf16[128,2048]{1,0:T(8,128)(2,1)S(1)}, bf16[128,2048]{1,0:T(8,128)(2,1)S(1)}, u32[]{:S(2)}, u32[]{:S(2)}) collective-permute-start(bf16[128,2048]{1,0:T(8,128)(2,1)S(1)} %collective-permute-done.t0), channel_id=1, source_target_pairs={{0,1},{4,5},{8,9},{12,13},{16,17},{20,21},{24,25},{28,29},{1,2},{5... | collective-permute-start | bytes 1572872 | tf_op jit(solution)/shard_map/ppermute | solution.py:24
  25.2 15.8 %collective-permute-start.11 = (f32[8,256]{1,0:T(8,128)S(1)}, f32[8,256]{1,0:T(8,128)S(1)}, u32[]{:S(2)}, u32[]{:S(2)}) collective-permute-start(f32[8,256]{1,0:T(8,128)S(1)} %get-tuple-element.49), channel_id=1, source_target_pairs={{0,35},{4,39},{8,43},{12,47},{16,51},{20,55},{24,59},{28,63},{1,0}... | collective-permute-start | bytes 24584 | tf_op jit(solution)/shard_map/ppermute | solution.py:24
  41.1 7.0 %collective-permute-start.8 = (f32[8,256]{1,0:T(8,128)S(1)}, f32[8,256]{1,0:T(8,128)S(1)}, u32[]{:S(2)}, u32[]{:S(2)}) collective-permute-start(f32[8,256]{1,0:T(8,128)S(1)} %get-tuple-element.47), channel_id=1, source_target_pairs={{0,1},{4,5},{8,9},{12,13},{16,17},{20,21},{24,25},{28,29},{1,2},{5... | collective-permute-start | bytes 24584 | tf_op jit(solution)/shard_map/ppermute | solution.py:24
  41.1 9.2 %collective-permute-start.5 = (f32[8,256]{1,0:T(8,128)S(1)}, f32[8,256]{1,0:T(8,128)S(1)}, u32[]{:S(2)}, u32[]{:S(2)}) collective-permute-start(f32[8,256]{1,0:T(8,128)S(1)} %get-tuple-element.42), channel_id=1, source_target_pairs={{0,34},{4,38},{8,42},{12,46},{16,50},{20,54},{24,58},{28,62},{1,35... | collective-permute-start | bytes 24584 | tf_op jit(solution)/shard_map/ppermute | solution.py:24
  48.0 5.9 %collective-permute-start.4 = (f32[8,256]{1,0:T(8,128)S(1)}, f32[8,256]{1,0:T(8,128)S(1)}, u32[]{:S(2)}, u32[]{:S(2)}) collective-permute-start(f32[8,256]{1,0:T(8,128)S(1)} %get-tuple-element.42), channel_id=1, source_target_pairs={{0,2},{4,6},{8,10},{12,14},{16,18},{20,22},{24,26},{28,30},{1,3},{... | collective-permute-start | bytes 24584 | tf_op jit(solution)/shard_map/ppermute | solution.py:24
  48.1 10.7 %collective-permute-start.12 = (bf16[4,128,128]{2,1,0:T(8,128)(2,1)S(1)}, bf16[4,128,128]{2,1,0:T(8,128)(2,1)S(1)}, u32[]{:S(2)}, u32[]{:S(2)}) collective-permute-start(bf16[4,128,128]{2,1,0:T(8,128)(2,1)S(1)} %get-tuple-element.50), channel_id=1, source_target_pairs={{0,1},{4,5},{8,9},{12,13},{16,17},{20,21},{24,25},{28,29},{1,2},{5... | collective-permute-start | bytes 393224 | tf_op jit(solution)/shard_map/ppermute | solution.py:24
  50.2 8.6 %collective-permute-start.9 = (bf16[4,128,128]{2,1,0:T(8,128)(2,1)S(1)}, bf16[4,128,128]{2,1,0:T(8,128)(2,1)S(1)}, u32[]{:S(2)}, u32[]{:S(2)}) collective-permute-start(bf16[4,128,128]{2,1,0:T(8,128)(2,1)S(1)} %get-tuple-element.48), channel_id=1, source_target_pairs={{0,35},{4,39},{8,43},{12,47},{16,51},{20,55},{24,59},{28,63},{1,0}... | collective-permute-start | bytes 393224 | tf_op jit(solution)/shard_map/ppermute | solution.py:24
  55.8 7.1 %collective-permute-start.6 = (bf16[4,128,128]{2,1,0:T(8,128)(2,1)S(1)}, bf16[4,128,128]{2,1,0:T(8,128)(2,1)S(1)}, u32[]{:S(2)}, u32[]{:S(2)}) collective-permute-start(bf16[4,128,128]{2,1,0:T(8,128)(2,1)S(1)} %get-tuple-element.43), channel_id=1, source_target_pairs={{0,34},{4,38},{8,42},{12,46},{16,50},{20,54},{24,58},{28,62},{1,35... | collective-permute-start | bytes 393224 | tf_op jit(solution)/shard_map/ppermute | solution.py:24
  58.1 8.0 %collective-permute-start.13 = (bf16[4,128,128]{2,1,0:T(8,128)(2,1)S(1)}, bf16[4,128,128]{2,1,0:T(8,128)(2,1)S(1)}, u32[]{:S(2)}, u32[]{:S(2)}) collective-permute-start(bf16[4,128,128]{2,1,0:T(8,128)(2,1)S(1)} %get-tuple-element.51), channel_id=1, source_target_pairs={{0,2},{4,6},{8,10},{12,14},{16,18},{20,22},{24,26},{28,30},{1,3},{... | collective-permute-start | bytes 393224 | tf_op jit(solution)/shard_map/ppermute | solution.py:24
  67.8 8.4 %collective-permute-start.16 = (bf16[2,17,16,128]{3,2,1,0:T(8,128)(2,1)S(1)}, bf16[2,17,16,128]{3,2,1,0:T(8,128)(2,1)S(1)}, u32[]{:S(2)}, u32[]{:S(2)}) collective-permute-start(bf16[2,17,16,128]{3,2,1,0:T(8,128)(2,1)S(1)} %get-tuple-element.57), channel_id=1, source_target_pairs={{0,8},{4,12},{8,0},{12,4},{16,24},{20,28},{24,16},{28,20},{1,9},{5... | collective-permute-start | bytes 417800 | tf_op jit(solution)/shard_map/ppermute | solution.py:24
  68.4 9.2 %collective-permute-start.17 = (bf16[2,17,16,128]{3,2,1,0:T(8,128)(2,1)S(1)}, bf16[2,17,16,128]{3,2,1,0:T(8,128)(2,1)S(1)}, u32[]{:S(2)}, u32[]{:S(2)}) collective-permute-start(bf16[2,17,16,128]{3,2,1,0:T(8,128)(2,1)S(1)} %get-tuple-element.58), channel_id=1, source_target_pairs={{0,16},{4,20},{8,24},{12,28},{16,0},{20,4},{24,8},{28,12},{1,17},{... | collective-permute-start | bytes 417800 | tf_op jit(solution)/shard_map/ppermute | solution.py:24
  70.8 8.1 %collective-permute-start.18 = (bf16[2,17,16,128]{3,2,1,0:T(8,128)(2,1)S(1)}, bf16[2,17,16,128]{3,2,1,0:T(8,128)(2,1)S(1)}, u32[]{:S(2)}, u32[]{:S(2)}) collective-permute-start(bf16[2,17,16,128]{3,2,1,0:T(8,128)(2,1)S(1)} %get-tuple-element.59), channel_id=1, source_target_pairs={{0,24},{4,28},{8,16},{12,20},{16,8},{20,12},{24,0},{28,4},{1,25},{... | collective-permute-start | bytes 417800 | tf_op jit(solution)/shard_map/ppermute | solution.py:24
  73.5 40.3 %collective-permute-start.30 = (bf16[2,256,512]{2,1,0:T(8,128)(2,1)S(1)}, bf16[2,256,512]{2,1,0:T(8,128)(2,1)S(1)}, u32[]{:S(2)}, u32[]{:S(2)}) collective-permute-start(bf16[2,256,512]{2,1,0:T(8,128)(2,1)S(1)} %shard_map.59), channel_id=1, source_target_pairs={{0,35},{4,39},{8,43},{12,47},{16,51},{20,55},{24,59},{28,63},{1,0}... | collective-permute-start | bytes 1572872 | tf_op jit(solution)/shard_map/ppermute | solution.py:24
  79.2 8.0 %collective-permute-start.24 = (bf16[17,16,128]{2,1,0:T(8,128)(2,1)S(1)}, bf16[17,16,128]{2,1,0:T(8,128)(2,1)S(1)}, u32[]{:S(2)}, u32[]{:S(2)}) collective-permute-start(bf16[17,16,128]{2,1,0:T(8,128)(2,1)S(1)} %shard_map.54.total.refs_4_), channel_id=1, source_target_pairs={{0,192},{4,196},{8,200},{12,204},{16,208},{20,212},{24,216},{28,22... | collective-permute-start | bytes 208904 | tf_op jit(solution)/shard_map/ppermute | solution.py:24
  82.4 13.7 %collective-permute-start.22 = (bf16[17,16,128]{2,1,0:T(8,128)(2,1)S(1)}, bf16[17,16,128]{2,1,0:T(8,128)(2,1)S(1)}, u32[]{:S(2)}, u32[]{:S(2)}) collective-permute-start(bf16[17,16,128]{2,1,0:T(8,128)(2,1)S(1)} %shard_map.54.total.refs_4_), channel_id=1, source_target_pairs={{0,128},{4,132},{8,136},{12,140},{16,144},{20,148},{24,152},{28,15... | collective-permute-start | bytes 208904 | tf_op jit(solution)/shard_map/ppermute | solution.py:24
  83.0 13.7 %collective-permute-start.20 = (bf16[17,16,128]{2,1,0:T(8,128)(2,1)S(1)}, bf16[17,16,128]{2,1,0:T(8,128)(2,1)S(1)}, u32[]{:S(2)}, u32[]{:S(2)}) collective-permute-start(bf16[17,16,128]{2,1,0:T(8,128)(2,1)S(1)} %shard_map.54.total.refs_4_), channel_id=1, source_target_pairs={{0,64},{4,68},{8,72},{12,76},{16,80},{20,84},{24,88},{28,92},{1,65... | collective-permute-start | bytes 208904 | tf_op jit(solution)/shard_map/ppermute | solution.py:24
  83.5 9.5 %collective-permute-start.19 = (bf16[17,16,128]{2,1,0:T(8,128)(2,1)S(1)}, bf16[17,16,128]{2,1,0:T(8,128)(2,1)S(1)}, u32[]{:S(2)}, u32[]{:S(2)}) collective-permute-start(bf16[17,16,128]{2,1,0:T(8,128)(2,1)S(1)} %shard_map.54.total.refs_4_), channel_id=1, source_target_pairs={{0,32},{4,36},{8,40},{12,44},{16,48},{20,52},{24,56},{28,60},{1,33... | collective-permute-start | bytes 208904 | tf_op jit(solution)/shard_map/ppermute | solution.py:24
  87.3 34.2 %collective-permute-start.31 = (bf16[2,256,512]{2,1,0:T(8,128)(2,1)S(1)}, bf16[2,256,512]{2,1,0:T(8,128)(2,1)S(1)}, u32[]{:S(2)}, u32[]{:S(2)}) collective-permute-start(bf16[2,256,512]{2,1,0:T(8,128)(2,1)S(1)} %shard_map.61), channel_id=1, source_target_pairs={{0,1},{4,5},{8,9},{12,13},{16,17},{20,21},{24,25},{28,29},{1,2},{5... | collective-permute-start | bytes 1572872 | tf_op jit(solution)/shard_map/ppermute | solution.py:24
  93.1 5.5 %collective-permute-start.25 = (bf16[17,16,128]{2,1,0:T(8,128)(2,1)S(1)}, bf16[17,16,128]{2,1,0:T(8,128)(2,1)S(1)}, u32[]{:S(2)}, u32[]{:S(2)}) collective-permute-start(bf16[17,16,128]{2,1,0:T(8,128)(2,1)S(1)} %collective-permute-done.19.refs_5_), channel_id=1, source_target_pairs={{0,192},{4,196},{8,200},{12,204},{16,208},{20,212},{24,216},{28,22... | collective-permute-start | bytes 208904 | tf_op jit(solution)/shard_map/ppermute | solution.py:24
  96.1 5.8 %collective-permute-start.23 = (bf16[17,16,128]{2,1,0:T(8,128)(2,1)S(1)}, bf16[17,16,128]{2,1,0:T(8,128)(2,1)S(1)}, u32[]{:S(2)}, u32[]{:S(2)}) collective-permute-start(bf16[17,16,128]{2,1,0:T(8,128)(2,1)S(1)} %collective-permute-done.19.refs_5_), channel_id=1, source_target_pairs={{0,128},{4,132},{8,136},{12,140},{16,144},{20,148},{24,152},{28,15... | collective-permute-start | bytes 208904 | tf_op jit(solution)/shard_map/ppermute | solution.py:24
  96.7 5.2 %collective-permute-start.21 = (bf16[17,16,128]{2,1,0:T(8,128)(2,1)S(1)}, bf16[17,16,128]{2,1,0:T(8,128)(2,1)S(1)}, u32[]{:S(2)}, u32[]{:S(2)}) collective-permute-start(bf16[17,16,128]{2,1,0:T(8,128)(2,1)S(1)} %collective-permute-done.19.refs_5_), channel_id=1, source_target_pairs={{0,64},{4,68},{8,72},{12,76},{16,80},{20,84},{24,88},{28,92},{1,65... | collective-permute-start | bytes 208904 | tf_op jit(solution)/shard_map/ppermute | solution.py:24
  102.3 5.7 %collective-permute-start.26 = (bf16[2,16,16,128]{3,2,1,0:T(8,128)(2,1)S(1)}, bf16[2,16,16,128]{3,2,1,0:T(8,128)(2,1)S(1)}, u32[]{:S(2)}, u32[]{:S(2)}) collective-permute-start(bf16[2,16,16,128]{3,2,1,0:T(8,128)(2,1)S(1)} %get-tuple-element.61), channel_id=1, source_target_pairs={{0,8},{4,12},{8,0},{12,4},{16,24},{20,28},{24,16},{28,20},{1,9},{5... | collective-permute-start | bytes 393224 | tf_op jit(solution)/shard_map/ppermute | solution.py:24
  105.1 6.5 %collective-permute-start.27 = (bf16[2,16,16,128]{3,2,1,0:T(8,128)(2,1)S(1)}, bf16[2,16,16,128]{3,2,1,0:T(8,128)(2,1)S(1)}, u32[]{:S(2)}, u32[]{:S(2)}) collective-permute-start(bf16[2,16,16,128]{3,2,1,0:T(8,128)(2,1)S(1)} %get-tuple-element.62), channel_id=1, source_target_pairs={{0,16},{4,20},{8,24},{12,28},{16,0},{20,4},{24,8},{28,12},{1,17},{... | collective-permute-start | bytes 393224 | tf_op jit(solution)/shard_map/ppermute | solution.py:24
  105.1 6.5 %collective-permute-start.28 = (bf16[2,16,16,128]{3,2,1,0:T(8,128)(2,1)S(1)}, bf16[2,16,16,128]{3,2,1,0:T(8,128)(2,1)S(1)}, u32[]{:S(2)}, u32[]{:S(2)}) collective-permute-start(bf16[2,16,16,128]{3,2,1,0:T(8,128)(2,1)S(1)} %get-tuple-element.63), channel_id=1, source_target_pairs={{0,24},{4,28},{8,16},{12,20},{16,8},{20,12},{24,0},{28,4},{1,25},{... | collective-permute-start | bytes 393224 | tf_op jit(solution)/shard_map/ppermute | solution.py:24
  108.0 13.5 %collective-permute-start.32 = (bf16[2,128,512]{2,1,0:T(8,128)(2,1)S(1)}, bf16[2,128,512]{2,1,0:T(8,128)(2,1)S(1)}, u32[]{:S(2)}, u32[]{:S(2)}) collective-permute-start(bf16[2,128,512]{2,1,0:T(8,128)(2,1)S(1)} %get-tuple-element.75.refs_0_), channel_id=1, source_target_pairs={{0,34},{4,38},{8,42},{12,46},{16,50},{20,54},{24,58},{28,62},{1,35... | collective-permute-start | bytes 786440 | tf_op jit(solution)/shard_map/ppermute | solution.py:24
  111.5 9.9 %collective-permute-start.33 = (bf16[2,128,512]{2,1,0:T(8,128)(2,1)S(1)}, bf16[2,128,512]{2,1,0:T(8,128)(2,1)S(1)}, u32[]{:S(2)}, u32[]{:S(2)}) collective-permute-start(bf16[2,128,512]{2,1,0:T(8,128)(2,1)S(1)} %get-tuple-element.76), channel_id=1, source_target_pairs={{0,2},{4,6},{8,10},{12,14},{16,18},{20,22},{24,26},{28,30},{1,3},{... | collective-permute-start | bytes 786440 | tf_op jit(solution)/shard_map/ppermute | solution.py:24
  111.6 9.9 %collective-permute-start.29 = (bf16[16,64,128]{2,1,0:T(8,128)(2,1)S(1)}, bf16[16,64,128]{2,1,0:T(8,128)(2,1)S(1)}, u32[]{:S(2)}, u32[]{:S(2)}) collective-permute-start(bf16[16,64,128]{2,1,0:T(8,128)(2,1)S(1)} %shard_map.57), channel_id=1, source_target_pairs={{0,4},{4,0},{8,12},{12,8},{16,20},{20,16},{24,28},{28,24},{1,5},{5... | collective-permute-start | bytes 786440 | tf_op jit(solution)/shard_map/ppermute | solution.py:24
  (4 other events, 38.1 us)

commit v6 on v5

--- a/solution.py
+++ b/solution.py
@@ -69,7 +69,7 @@
     return lax.dot_general(a, b, (dims, ((), ())), preferred_element_type=F32)
 
 
-def call(kernel, outs, *args, flops=0, scratch=(), space=pltpu.VMEM, far=0):
+def call(kernel, outs, *args, flops=0, scratch=(), far=0):
     moved = sum(a.size * a.dtype.itemsize for a in args)
     near = len(args) - far
     held = [pltpu.with_memory_space_constraint(a, pltpu.VMEM) for a in args[:near]] + [
@@ -79,7 +79,7 @@
         kernel,
         in_specs=[VMEM] * near + [pl.BlockSpec(memory_space=pltpu.HBM)] * far,
         out_specs=[VMEM] * len(outs),
-        out_shape=[space(shape, dtype) for shape, dtype in outs],
+        out_shape=[pltpu.VMEM(shape, dtype) for shape, dtype in outs],
         scratch_shapes=[pltpu.VMEM(shape, dtype) for shape, dtype in scratch] + [pltpu.SemaphoreType.DMA(())] * far,
         cost_estimate=pl.CostEstimate(flops=flops, bytes_accessed=moved, transcendentals=0),
         compiler_params=pltpu.CompilerParams(vmem_limit_bytes=24 << 20),
@@ -215,6 +215,12 @@
 
 def insides(tok, w, rates, k_ref, v_ref, *refs):
     insides_of(tok, w, running(rates[...]), k_ref, v_ref, [refs[-1]], 256)
+
+
+def insides_first(tok, w, rates, k_ref, v_ref, s1, s2, out, t1, t2):
+    t1[...] = s1[...]
+    t2[...] = s2[...]
+    insides_of(tok, w, running(rates[...]), k_ref, v_ref, [out], 256)
 
 
 def insides_two(tok, w, r0, r1, k_ref, v_ref, out0, out1):
@@ -301,7 +307,7 @@
 
 
 def final(entry, gain, first_half, crossed, *refs):
-    parts, pieces, out, memory, attended = refs[:5], refs[5:9], refs[9], refs[10], refs[11]
+    parts, pieces, out, memory, attended, normed, sems = refs[:5], refs[5:9], *refs[9:]
     p, _ = place()
     x, core = lax.div(p, 2), lax.rem(p, 2)
     f = lax.axis_index("fsdp")
@@ -309,26 +315,29 @@
         at = core * 64 + jnp.bitwise_xor(x, d) * 16
         memory[:, pl.ds(pl.multiple_of(at, 16), 16), :] = pieces[d][core]
     memory[:, pl.ds(pl.multiple_of(64 - core * 64, 64), 64), :] = crossed[...]
-    squares = [jnp.zeros((128, 128), F32)] * 2
-    for i, shift in enumerate(SHIFTS):
-        group = lax.rem(f + shift, 4)
-        for h in range(4):
-            cols = slice(128 * h, 128 * h + 128)
-            head = 4 * i + h
-            for half in range(2):
-                rows = slice(128 * half, 128 * half + 128)
-                part, at = (parts[i], rows) if i < 3 else (parts[3 + half], slice(0, 128))
+    copies = []
+    for half in range(2):
+        rows = slice(128 * half, 128 * half + 128)
+        squares = jnp.zeros((128, 128), F32)
+        for i, shift in enumerate(SHIFTS):
+            group = lax.rem(f + shift, 4)
+            part, at = (parts[i], rows) if i < 3 else (parts[3 + half], slice(0, 128))
+            for h in range(4):
+                cols = slice(128 * h, 128 * h + 128)
+                head = 4 * i + h
                 q = part[0, at, cols]
                 value = part[1, at, cols].astype(F32)
                 value += jnp.dot(q, memory[head], preferred_element_type=F32) * entry[rows, head : head + 1]
                 if i == 3 and half == 1:
                     value += jnp.dot(q, first_half[h], preferred_element_type=F32) * entry[rows, 16 + h : 17 + h]
-                squares[half] += value * value
-                attended[rows, pl.ds(pl.multiple_of(group * 512 + 128 * h, 128), 128)] = value
-    for half in range(2):
-        rows = slice(128 * half, 128 * half + 128)
-        scale = lax.rsqrt(jnp.sum(squares[half], axis=-1, keepdims=True) / out.shape[1] + 1e-05)
-        out[rows, :] = (attended[rows, :] * scale * gain[...]).astype(BF16)
+                squares += value * value
+                attended[:, pl.ds(pl.multiple_of(group * 512 + 128 * h, 128), 128)] = value
+        scale = lax.rsqrt(jnp.sum(squares, axis=-1, keepdims=True) / out.shape[1] + 1e-05)
+        normed[rows, :] = (attended[...] * scale * gain[...]).astype(BF16)
+        copies.append(pltpu.make_async_copy(normed.at[rows, :], out.at[rows, :], sems.at[half]))
+        copies[-1].start()
+    for copy in copies:
+        copy.wait()
 
 
 def body(tokens, qkv_weight, log_decay, norm_gain):
@@ -370,19 +379,29 @@
                 flops=1 << 30,
             )
         )
+    middle, state_1, state_2 = call(
+        insides_first,
+        [((2, n, 512), BF16), state, state],
+        made[1][0],
+        weight,
+        rates[1],
+        *made[1][1:],
+        made[2][3],
+        flops=1 << 30,
+    )
     two = call(
         states_two, [((n, d), BF16), half, half, state, state], first, last, weight, *rates[3:], flops=1 << 30
     )
     first_half, last_half = send(two[3], down_two), send(two[4], up_two)
-    back_1 = send(made[1][3], down)
-    back_2 = send(made[2][3], up)
+    back_1 = send(state_1, down)
+    back_2 = send(state_2, up)
 
     last_parts = call(insides_two, [((2, 128, 512), BF16)] * 2, two[0], weight, *rates[3:], *two[1:3], flops=1 << 30)
     parts = []
-    for i in range(3):
+    for i in (0, 2):
         after = (last_parts[0],) if i == 2 else ()
         parts += call(insides, [((2, n, 512), BF16)], made[i][0], weight, rates[i], *made[i][1:3], *after, flops=1 << 30)
-    parts += last_parts
+    parts = [parts[0], middle, parts[1], *last_parts]
     for i, m in enumerate((down, up, down_two, up_two)):
         parts[i + 1] = send(parts[i + 1], m)
 
@@ -410,18 +429,21 @@
     )
     carried = exchange(carried, (2, 1, 3), along_x)
     crossed = send(call(gather, [((16, 64, 128), BF16)], *carried)[0], other)
-    out = call(
+    args = (entry, norm_gain[None], first_half, crossed, *parts, *carried)
+    out = pl.pallas_call(
         final,
-        [((n, d), BF16)],
-        entry,
-        norm_gain[None],
-        first_half,
-        crossed,
-        *parts,
-        *carried,
-        scratch=[((16, 128, 128), BF16), ((n, d), F32)],
-        space=jax.ShapeDtypeStruct,
-    )[0]
+        in_specs=[VMEM] * len(args),
+        out_specs=pl.BlockSpec(memory_space=pltpu.HBM),
+        out_shape=jax.ShapeDtypeStruct((n, d), BF16),
+        scratch_shapes=[
+            pltpu.VMEM((16, 128, 128), BF16),
+            pltpu.VMEM((128, d), F32),
+            pltpu.VMEM((n, d), BF16),
+            pltpu.SemaphoreType.DMA((2,)),
+        ],
+        compiler_params=pltpu.CompilerParams(vmem_limit_bytes=24 << 20),
+        name="final",
+    )(*(pltpu.with_memory_space_constraint(a, pltpu.VMEM) for a in args))
     return out[None]
 
 

time: 124 us -> 129 us (1.040)
  the two profiles are of different devices: /device:TPU:2 before, /device:TPU:34 now
where the time goes in v6:
time: 129 us; the launch traced here: 128 us
  waiting for transfers between devices  55.5 us (43%)
  starting transfers between devices  47.2 us (37%)
  Pallas kernels  23.3 us (18%)
  local copies, waits for them, and re-layouts  2 us (2%)
    ppermute x34, waiting for transfers between devices, send(): return lax.ppermute(a, BOTH, pairs(move))  55.5 us
    ppermute x34, starting transfers between devices, send(): return lax.ppermute(a, BOTH, pairs(move))  47.2 us
    pallas_call x16, Pallas kernels, call(): pl.pallas_call(kernel, in_specs=[VMEM] * near + [pl.BlockSpec(memory_spac...  21.1 us
  transfers between devices with their start and end apart: 34, of which 14 were waited for; matrix products, arithmetic and copies ran while one was open for 0% of the time, Pallas kernels for 16%

profile of v6, /device:TPU:34, one launch (start us, length us, event | category | flops | bytes accessed | tf_op | source)
XLA Modules:
  0.0 128.4 jit_solution(10843123158066393308)
XLA Ops:
  1.5 1.9 %collective-permute-start = (bf16[128,2048]{1,0:T(8,128)(2,1)S(1)}, bf16[128,2048]{1,0:T(8,128)(2,1)S(1)}, u32[]{:S(2)}, u32[]{:S(2)}) collective-permute-start(bf16[128,2048]{1,0:T(8,128)(2,1)S(1)} %get-tuple-element.84), channel_id=1, source_target_pairs={{0,1},{4,5},{8,9},{12,13},{16,17},{20,21},{24,25},{28,29},{1,2},{5... | collective-permute-start | bytes 1572872 | tf_op jit(solution)/shard_map/ppermute | solution.py:24
  3.4 3.9 %collective-permute-start.9 = (bf16[128,2048]{1,0:T(8,128)(2,1)S(1)}, bf16[128,2048]{1,0:T(8,128)(2,1)S(1)}, u32[]{:S(2)}, u32[]{:S(2)}) collective-permute-start(bf16[128,2048]{1,0:T(8,128)(2,1)S(1)} %get-tuple-element.84), channel_id=1, source_target_pairs={{0,35},{4,39},{8,43},{12,47},{16,51},{20,55},{24,59},{28,63},{1,0}... | collective-permute-start | bytes 1572872 | tf_op jit(solution)/shard_map/ppermute | solution.py:24
  7.3 8.8 %collective-permute-done.2.t1 = bf16[128,2048]{1,0:T(8,128)(2,1)S(1)} collective-permute-done((bf16[128,2048]{1,0:T(8,128)(2,1)S(1)}, bf16[128,2048]{1,0:T(8,128)(2,1)S(1)}, u32[]{:S(2)}, u32[]{:S(2)}) %collective-permute-start.2) | collective-permute-done | bytes 524320 | tf_op jit(solution)/shard_map/ppermute | solution.py:24
  16.2 3.5 %collective-permute-start.3 = (bf16[128,2048]{1,0:T(8,128)(2,1)S(1)}, bf16[128,2048]{1,0:T(8,128)(2,1)S(1)}, u32[]{:S(2)}, u32[]{:S(2)}) collective-permute-start(bf16[128,2048]{1,0:T(8,128)(2,1)S(1)} %collective-permute-done.2.t1), channel_id=1, source_target_pairs={{0,35},{4,39},{8,43},{12,47},{16,51},{20,55},{24,59},{28,63},{1,0}... | collective-permute-start | bytes 1572872 | tf_op jit(solution)/shard_map/ppermute | solution.py:24
  22.1 3.3 %collective-permute-start.10 = (f32[8,256]{1,0:T(8,128)S(1)}, f32[8,256]{1,0:T(8,128)S(1)}, u32[]{:S(2)}, u32[]{:S(2)}) collective-permute-start(f32[8,256]{1,0:T(8,128)S(1)} %get-tuple-element.55), channel_id=1, source_target_pairs={{0,35},{4,39},{8,43},{12,47},{16,51},{20,55},{24,59},{28,63},{1,0}... | collective-permute-start | bytes 24584 | tf_op jit(solution)/shard_map/ppermute | solution.py:24
  25.4 2.8 %shard_map.47.w = bf16[3,2048,512]{2,1,0:T(8,128)(2,1)S(1)} custom-call(bf16[3,2048,512]{2,1,0:T(8,128)(2,1)} %w.1), custom_call_target="tpu_custom_call" | custom-call | bytes 6291456 | tf_op jit(solution)/shard_map/pallas_call | solution.py:78
  28.2 1.8 %shard_map.49 = (bf16[256,512]{1,0:T(8,128)(2,1)S(1)}, bf16[256,512]{1,0:T(8,128)(2,1)S(1)}, bf16[4,128,128]{2,1,0:T(8,128)(2,1)S(1)}) custom-call(bf16[256,2048]{1,0:T(8,128)(2,1)S(1)} %get-tuple-element.47.tok, bf16[3,2048,512]{2,1,0:T(8,128)(2,1)S(1)} %shard_map.47.w, f32[8,256]{1,0:T(8,128)S(1)} %get-tuple-element.48.rates), custom_call_target="tpu_custom_call" | custom-call | flops 1073741824 | bytes 7348224 | tf_op jit(solution)/shard_map/pallas_call | solution.py:78
  30.0 7.9 %collective-permute-done.10.rates = f32[8,256]{1,0:T(8,128)S(1)} collective-permute-done((f32[8,256]{1,0:T(8,128)S(1)}, f32[8,256]{1,0:T(8,128)S(1)}, u32[]{:S(2)}, u32[]{:S(2)}) %collective-permute-start.10) | collective-permute-done | bytes 8224 | tf_op jit(solution)/shard_map/ppermute | solution.py:24
  37.9 1.9 %collective-permute-start.8 = (f32[8,256]{1,0:T(8,128)S(1)}, f32[8,256]{1,0:T(8,128)S(1)}, u32[]{:S(2)}, u32[]{:S(2)}) collective-permute-start(f32[8,256]{1,0:T(8,128)S(1)} %get-tuple-element.50), channel_id=1, source_target_pairs={{0,1},{4,5},{8,9},{12,13},{16,17},{20,21},{24,25},{28,29},{1,2},{5... | collective-permute-start | bytes 24584 | tf_op jit(solution)/shard_map/ppermute | solution.py:24
  39.8 4.5 %collective-permute-start.5 = (f32[8,256]{1,0:T(8,128)S(1)}, f32[8,256]{1,0:T(8,128)S(1)}, u32[]{:S(2)}, u32[]{:S(2)}) collective-permute-start(f32[8,256]{1,0:T(8,128)S(1)} %get-tuple-element.45), channel_id=1, source_target_pairs={{0,34},{4,38},{8,42},{12,46},{16,50},{20,54},{24,58},{28,62},{1,35... | collective-permute-start | bytes 24584 | tf_op jit(solution)/shard_map/ppermute | solution.py:24
  44.3 1.8 %shard_map.51 = (bf16[256,2048]{1,0:T(8,128)(2,1)S(1)}, bf16[256,512]{1,0:T(8,128)(2,1)S(1)}, bf16[256,512]{1,0:T(8,128)(2,1)S(1)}, bf16[4,128,128]{2,1,0:T(8,128)(2,1)S(1)}) custom-call(bf16[128,2048]{1,0:T(8,128)(2,1)S(1)} %collective-permute-done.9.t0, bf16[128,2048]{1,0:T(8,128)(2,1)S(1)} %collective-permute-done.2.t1, ...), custom_call_target="tpu_custom_call" | custom-call | flops 1073741824 | bytes 7479296 | tf_op jit(solution)/shard_map/pallas_call | solution.py:78
  46.4 1.8 %shard_map.50 = (bf16[256,2048]{1,0:T(8,128)(2,1)S(1)}, bf16[256,512]{1,0:T(8,128)(2,1)S(1)}, bf16[256,512]{1,0:T(8,128)(2,1)S(1)}, bf16[4,128,128]{2,1,0:T(8,128)(2,1)S(1)}) custom-call(bf16[128,2048]{1,0:T(8,128)(2,1)S(1)} %collective-permute-done.t0, bf16[128,2048]{1,0:T(8,128)(2,1)S(1)} %collective-permute-done.7.t1, ...), custom_call_target="tpu_custom_call" | custom-call | flops 1073741824 | bytes 7479296 | tf_op jit(solution)/shard_map/pallas_call | solution.py:78
  48.2 2.2 %shard_map.52 = (bf16[2,256,512]{2,1,0:T(8,128)(2,1)S(1)}, bf16[4,128,128]{2,1,0:T(8,128)(2,1)S(1)}, bf16[4,128,128]{2,1,0:T(8,128)(2,1)S(1)}) custom-call(bf16[256,2048]{1,0:T(8,128)(2,1)S(1)} %get-tuple-element.51.tok, bf16[3,2048,512]{2,1,0:T(8,128)(2,1)S(1)} %shard_map.47.w, f32[8,256]{1,0:T(8,128)S(1)} %collective-permute-done.8.rates, ...), custom_call_target="tpu_custom_call" | custom-call | flops 1073741824 | bytes 8134656 | tf_op jit(solution)/shard_map/pallas_call | solution.py:78
  50.4 2.1 %collective-permute-start.11 = (bf16[4,128,128]{2,1,0:T(8,128)(2,1)S(1)}, bf16[4,128,128]{2,1,0:T(8,128)(2,1)S(1)}, u32[]{:S(2)}, u32[]{:S(2)}) collective-permute-start(bf16[4,128,128]{2,1,0:T(8,128)(2,1)S(1)} %get-tuple-element.57), channel_id=1, source_target_pairs={{0,35},{4,39},{8,43},{12,47},{16,51},{20,55},{24,59},{28,63},{1,0}... | collective-permute-start | bytes 393224 | tf_op jit(solution)/shard_map/ppermute | solution.py:24
  53.3 1.8 %shard_map.48 = (bf16[256,2048]{1,0:T(8,128)(2,1)S(1)}, bf16[256,512]{1,0:T(8,128)(2,1)S(1)}, bf16[256,512]{1,0:T(8,128)(2,1)S(1)}, bf16[4,128,128]{2,1,0:T(8,128)(2,1)S(1)}, bf16[4,128,128]{2,1,0:T(8,128)(2,1)S(1)}) custom-call(bf16[128,2048]{1,0:T(8,128)(2,1)S(1)} %collective-permute-done.1.t0, bf16[128,2048]{1,0:T(8,128)(2,1)S(1)} %collective-permute-done.3.t1, ...), custom_call_target="tpu_custom_call" | custom-call | flops 1073741824 | bytes 7356416 | tf_op jit(solution)/shard_map/pallas_call | solution.py:78
  55.1 4.6 %collective-permute-start.6 = (bf16[4,128,128]{2,1,0:T(8,128)(2,1)S(1)}, bf16[4,128,128]{2,1,0:T(8,128)(2,1)S(1)}, u32[]{:S(2)}, u32[]{:S(2)}) collective-permute-start(bf16[4,128,128]{2,1,0:T(8,128)(2,1)S(1)} %get-tuple-element.46), channel_id=1, source_target_pairs={{0,34},{4,38},{8,42},{12,46},{16,50},{20,54},{24,58},{28,62},{1,35... | collective-permute-start | bytes 393224 | tf_op jit(solution)/shard_map/ppermute | solution.py:24
  59.7 3.2 %collective-permute-done.6.s3.first_half = bf16[4,128,128]{2,1,0:T(8,128)(2,1)S(1)} collective-permute-done((bf16[4,128,128]{2,1,0:T(8,128)(2,1)S(1)}, bf16[4,128,128]{2,1,0:T(8,128)(2,1)S(1)}, u32[]{:S(2)}, u32[]{:S(2)}) %collective-permute-start.6) | collective-permute-done | bytes 131104 | tf_op jit(solution)/shard_map/ppermute | solution.py:24
  62.9 5.3 %collective-permute-done.13.s4 = bf16[4,128,128]{2,1,0:T(8,128)(2,1)S(1)} collective-permute-done((bf16[4,128,128]{2,1,0:T(8,128)(2,1)S(1)}, bf16[4,128,128]{2,1,0:T(8,128)(2,1)S(1)}, u32[]{:S(2)}, u32[]{:S(2)}) %collective-permute-start.13) | collective-permute-done | bytes 131104 | tf_op jit(solution)/shard_map/ppermute | solution.py:24
  70.6 2.4 %collective-permute-start.17 = (bf16[2,17,16,128]{3,2,1,0:T(8,128)(2,1)S(1)}, bf16[2,17,16,128]{3,2,1,0:T(8,128)(2,1)S(1)}, u32[]{:S(2)}, u32[]{:S(2)}) collective-permute-start(bf16[2,17,16,128]{3,2,1,0:T(8,128)(2,1)S(1)} %get-tuple-element.66), channel_id=1, source_target_pairs={{0,16},{4,20},{8,24},{12,28},{16,0},{20,4},{24,8},{28,12},{1,17},{... | collective-permute-start | bytes 417800 | tf_op jit(solution)/shard_map/ppermute | solution.py:24
  73.7 2.6 %shard_map.60 = (bf16[2,128,512]{2,1,0:T(8,128)(2,1)S(1)}, bf16[2,128,512]{2,1,0:T(8,128)(2,1)S(1)}) custom-call(bf16[256,2048]{1,0:T(8,128)(2,1)S(1)} %get-tuple-element.78.tok, bf16[3,2048,512]{2,1,0:T(8,128)(2,1)S(1)} %shard_map.47.w, f32[8,256]{1,0:T(8,128)S(1)} %collective-permute-done.4.r0, f32[8,256]{1,0:T(8,128)S(1)} %collective-permute-done.5.r1, ...), custom_call_target="tpu_custom_call" | custom-call | flops 1073741824 | bytes 7880704 | tf_op jit(solution)/shard_map/pallas_call | solution.py:78
  76.4 3.4 %collective-permute-done.17.refs_2_ = bf16[2,17,16,128]{3,2,1,0:T(8,128)(2,1)S(1)} collective-permute-done((bf16[2,17,16,128]{3,2,1,0:T(8,128)(2,1)S(1)}, bf16[2,17,16,128]{3,2,1,0:T(8,128)(2,1)S(1)}, u32[]{:S(2)}, u32[]{:S(2)}) %collective-permute-start.17) | collective-permute-done | bytes 139296 | tf_op jit(solution)/shard_map/ppermute | solution.py:24
  81.4 3.1 %collective-permute-start.24 = (bf16[17,16,128]{2,1,0:T(8,128)(2,1)S(1)}, bf16[17,16,128]{2,1,0:T(8,128)(2,1)S(1)}, u32[]{:S(2)}, u32[]{:S(2)}) collective-permute-start(bf16[17,16,128]{2,1,0:T(8,128)(2,1)S(1)} %shard_map.55.total.refs_4_), channel_id=1, source_target_pairs={{0,192},{4,196},{8,200},{12,204},{16,208},{20,212},{24,216},{28,22... | collective-permute-start | bytes 208904 | tf_op jit(solution)/shard_map/ppermute | solution.py:24
  85.6 2.6 %collective-permute-start.19 = (bf16[17,16,128]{2,1,0:T(8,128)(2,1)S(1)}, bf16[17,16,128]{2,1,0:T(8,128)(2,1)S(1)}, u32[]{:S(2)}, u32[]{:S(2)}) collective-permute-start(bf16[17,16,128]{2,1,0:T(8,128)(2,1)S(1)} %shard_map.55.total.refs_4_), channel_id=1, source_target_pairs={{0,32},{4,36},{8,40},{12,44},{16,48},{20,52},{24,56},{28,60},{1,33... | collective-permute-start | bytes 208904 | tf_op jit(solution)/shard_map/ppermute | solution.py:24
  88.2 2.1 %shard_map.61 = bf16[2,256,512]{2,1,0:T(8,128)(2,1)S(1)} custom-call(bf16[256,2048]{1,0:T(8,128)(2,1)S(1)} %get-tuple-element.75.tok, bf16[3,2048,512]{2,1,0:T(8,128)(2,1)S(1)} %shard_map.47.w, f32[8,256]{1,0:T(8,128)S(1)} %collective-permute-done.10.rates, bf16[256,512]{1,0:T(8,128)(2,1)S(1)} %get-tuple-element.76.k_ref, ...), custom_call_target="tpu_custom_call" | custom-call | flops 1073741824 | bytes 8134656 | tf_op jit(solution)/shard_map/pallas_call | solution.py:78
  90.5 3.3 %collective-permute-done.19.refs_5_ = bf16[17,16,128]{2,1,0:T(8,128)(2,1)S(1)} collective-permute-done((bf16[17,16,128]{2,1,0:T(8,128)(2,1)S(1)}, bf16[17,16,128]{2,1,0:T(8,128)(2,1)S(1)}, u32[]{:S(2)}, u32[]{:S(2)}) %collective-permute-start.19) | collective-permute-done | bytes 69664 | tf_op jit(solution)/shard_map/ppermute | solution.py:24
  93.8 3.0 %collective-permute-start.25 = (bf16[17,16,128]{2,1,0:T(8,128)(2,1)S(1)}, bf16[17,16,128]{2,1,0:T(8,128)(2,1)S(1)}, u32[]{:S(2)}, u32[]{:S(2)}) collective-permute-start(bf16[17,16,128]{2,1,0:T(8,128)(2,1)S(1)} %collective-permute-done.19.refs_5_), channel_id=1, source_target_pairs={{0,192},{4,196},{8,200},{12,204},{16,208},{20,212},{24,216},{28,22... | collective-permute-start | bytes 208904 | tf_op jit(solution)/shard_map/ppermute | solution.py:24
  99.3 3.3 %collective-permute-done.23.refs_9_ = bf16[17,16,128]{2,1,0:T(8,128)(2,1)S(1)} collective-permute-done((bf16[17,16,128]{2,1,0:T(8,128)(2,1)S(1)}, bf16[17,16,128]{2,1,0:T(8,128)(2,1)S(1)}, u32[]{:S(2)}, u32[]{:S(2)}) %collective-permute-start.23) | collective-permute-done | bytes 69664 | tf_op jit(solution)/shard_map/ppermute | solution.py:24
  103.1 2.8 %collective-permute-start.26 = (bf16[2,16,16,128]{3,2,1,0:T(8,128)(2,1)S(1)}, bf16[2,16,16,128]{3,2,1,0:T(8,128)(2,1)S(1)}, u32[]{:S(2)}, u32[]{:S(2)}) collective-permute-start(bf16[2,16,16,128]{3,2,1,0:T(8,128)(2,1)S(1)} %get-tuple-element.69), channel_id=1, source_target_pairs={{0,8},{4,12},{8,0},{12,4},{16,24},{20,28},{24,16},{28,20},{1,9},{5... | collective-permute-start | bytes 393224 | tf_op jit(solution)/shard_map/ppermute | solution.py:24
  108.9 3.5 %collective-permute-done.27.p2.refs_7_ = bf16[2,16,16,128]{3,2,1,0:T(8,128)(2,1)S(1)} collective-permute-done((bf16[2,16,16,128]{3,2,1,0:T(8,128)(2,1)S(1)}, bf16[2,16,16,128]{3,2,1,0:T(8,128)(2,1)S(1)}, u32[]{:S(2)}, u32[]{:S(2)}) %collective-permute-start.27) | collective-permute-done | bytes 131104 | tf_op jit(solution)/shard_map/ppermute | solution.py:24
  112.8 2.1 %shard_map.59.refs_0_ = bf16[2,256,512]{2,1,0:T(8,128)(2,1)S(1)} custom-call(bf16[256,2048]{1,0:T(8,128)(2,1)S(1)} %get-tuple-element.47.tok, bf16[3,2048,512]{2,1,0:T(8,128)(2,1)S(1)} %shard_map.47.w, f32[8,256]{1,0:T(8,128)S(1)} %get-tuple-element.48.rates, bf16[256,512]{1,0:T(8,128)(2,1)S(1)} %get-tuple-element.72.k_ref, ...), custom_call_target="tpu_custom_call" | custom-call | flops 1073741824 | bytes 7872512 | tf_op jit(solution)/shard_map/pallas_call | solution.py:78
  115.0 11.1 %collective-permute-done.33.refs_4_ = bf16[2,128,512]{2,1,0:T(8,128)(2,1)S(1)} collective-permute-done((bf16[2,128,512]{2,1,0:T(8,128)(2,1)S(1)}, bf16[2,128,512]{2,1,0:T(8,128)(2,1)S(1)}, u32[]{:S(2)}, u32[]{:S(2)}) %collective-permute-start.33) | collective-permute-done | bytes 262176 | tf_op jit(solution)/shard_map/ppermute | solution.py:24
  126.1 2.2 %final.1 = bf16[256,2048]{1,0:T(8,128)(2,1)} custom-call(f32[256,128]{1,0:T(8,128)S(1)} %get-tuple-element.44.entry, f32[1,2048]{1,0:T(1,128)S(1)} %bitcast.9, bf16[4,128,128]{2,1,0:T(8,128)(2,1)S(1)} %collective-permute-done.6.s3.first_half, bf16[16,64,128]{2,1,0:T(8,128)(2,1)S(1)} %collective-permute-done.29.crossed, ...), custom_call_target="tpu_custom_call" | custom-call | tf_op jit(solution)/shard_map/final/pallas_call | solution.py:433
  (58 shorter events, 17.2 us)
Async XLA Ops:
  1.3 14.9 %collective-permute-start.2 = (bf16[128,2048]{1,0:T(8,128)(2,1)S(1)}, bf16[128,2048]{1,0:T(8,128)(2,1)S(1)}, u32[]{:S(2)}, u32[]{:S(2)}) collective-permute-start(bf16[128,2048]{1,0:T(8,128)(2,1)S(1)} %get-tuple-element.83), channel_id=1, source_target_pairs={{0,35},{4,39},{8,43},{12,47},{16,51},{20,55},{24,59},{28,63},{1,0}... | collective-permute-start | bytes 1572872 | tf_op jit(solution)/shard_map/ppermute | solution.py:24
  1.5 18.6 %collective-permute-start = (bf16[128,2048]{1,0:T(8,128)(2,1)S(1)}, bf16[128,2048]{1,0:T(8,128)(2,1)S(1)}, u32[]{:S(2)}, u32[]{:S(2)}) collective-permute-start(bf16[128,2048]{1,0:T(8,128)(2,1)S(1)} %get-tuple-element.84), channel_id=1, source_target_pairs={{0,1},{4,5},{8,9},{12,13},{16,17},{20,21},{24,25},{28,29},{1,2},{5... | collective-permute-start | bytes 1572872 | tf_op jit(solution)/shard_map/ppermute | solution.py:24
  3.4 36.4 %collective-permute-start.9 = (bf16[128,2048]{1,0:T(8,128)(2,1)S(1)}, bf16[128,2048]{1,0:T(8,128)(2,1)S(1)}, u32[]{:S(2)}, u32[]{:S(2)}) collective-permute-start(bf16[128,2048]{1,0:T(8,128)(2,1)S(1)} %get-tuple-element.84), channel_id=1, source_target_pairs={{0,35},{4,39},{8,43},{12,47},{16,51},{20,55},{24,59},{28,63},{1,0}... | collective-permute-start | bytes 1572872 | tf_op jit(solution)/shard_map/ppermute | solution.py:24
  7.3 39.0 %collective-permute-start.7 = (bf16[128,2048]{1,0:T(8,128)(2,1)S(1)}, bf16[128,2048]{1,0:T(8,128)(2,1)S(1)}, u32[]{:S(2)}, u32[]{:S(2)}) collective-permute-start(bf16[128,2048]{1,0:T(8,128)(2,1)S(1)} %get-tuple-element.83), channel_id=1, source_target_pairs={{0,1},{4,5},{8,9},{12,13},{16,17},{20,21},{24,25},{28,29},{1,2},{5... | collective-permute-start | bytes 1572872 | tf_op jit(solution)/shard_map/ppermute | solution.py:24
  16.2 37.1 %collective-permute-start.3 = (bf16[128,2048]{1,0:T(8,128)(2,1)S(1)}, bf16[128,2048]{1,0:T(8,128)(2,1)S(1)}, u32[]{:S(2)}, u32[]{:S(2)}) collective-permute-start(bf16[128,2048]{1,0:T(8,128)(2,1)S(1)} %collective-permute-done.2.t1), channel_id=1, source_target_pairs={{0,35},{4,39},{8,43},{12,47},{16,51},{20,55},{24,59},{28,63},{1,0}... | collective-permute-start | bytes 1572872 | tf_op jit(solution)/shard_map/ppermute | solution.py:24
  20.1 33.2 %collective-permute-start.1 = (bf16[128,2048]{1,0:T(8,128)(2,1)S(1)}, bf16[128,2048]{1,0:T(8,128)(2,1)S(1)}, u32[]{:S(2)}, u32[]{:S(2)}) collective-permute-start(bf16[128,2048]{1,0:T(8,128)(2,1)S(1)} %collective-permute-done.t0), channel_id=1, source_target_pairs={{0,1},{4,5},{8,9},{12,13},{16,17},{20,21},{24,25},{28,29},{1,2},{5... | collective-permute-start | bytes 1572872 | tf_op jit(solution)/shard_map/ppermute | solution.py:24
  22.1 15.8 %collective-permute-start.10 = (f32[8,256]{1,0:T(8,128)S(1)}, f32[8,256]{1,0:T(8,128)S(1)}, u32[]{:S(2)}, u32[]{:S(2)}) collective-permute-start(f32[8,256]{1,0:T(8,128)S(1)} %get-tuple-element.55), channel_id=1, source_target_pairs={{0,35},{4,39},{8,43},{12,47},{16,51},{20,55},{24,59},{28,63},{1,0}... | collective-permute-start | bytes 24584 | tf_op jit(solution)/shard_map/ppermute | solution.py:24
  37.9 8.2 %collective-permute-start.8 = (f32[8,256]{1,0:T(8,128)S(1)}, f32[8,256]{1,0:T(8,128)S(1)}, u32[]{:S(2)}, u32[]{:S(2)}) collective-permute-start(f32[8,256]{1,0:T(8,128)S(1)} %get-tuple-element.50), channel_id=1, source_target_pairs={{0,1},{4,5},{8,9},{12,13},{16,17},{20,21},{24,25},{28,29},{1,2},{5... | collective-permute-start | bytes 24584 | tf_op jit(solution)/shard_map/ppermute | solution.py:24
  39.8 12.7 %collective-permute-start.5 = (f32[8,256]{1,0:T(8,128)S(1)}, f32[8,256]{1,0:T(8,128)S(1)}, u32[]{:S(2)}, u32[]{:S(2)}) collective-permute-start(f32[8,256]{1,0:T(8,128)S(1)} %get-tuple-element.45), channel_id=1, source_target_pairs={{0,34},{4,38},{8,42},{12,46},{16,50},{20,54},{24,58},{28,62},{1,35... | collective-permute-start | bytes 24584 | tf_op jit(solution)/shard_map/ppermute | solution.py:24
  46.1 7.2 %collective-permute-start.4 = (f32[8,256]{1,0:T(8,128)S(1)}, f32[8,256]{1,0:T(8,128)S(1)}, u32[]{:S(2)}, u32[]{:S(2)}) collective-permute-start(f32[8,256]{1,0:T(8,128)S(1)} %get-tuple-element.45), channel_id=1, source_target_pairs={{0,2},{4,6},{8,10},{12,14},{16,18},{20,22},{24,26},{28,30},{1,3},{... | collective-permute-start | bytes 24584 | tf_op jit(solution)/shard_map/ppermute | solution.py:24
  50.4 9.3 %collective-permute-start.11 = (bf16[4,128,128]{2,1,0:T(8,128)(2,1)S(1)}, bf16[4,128,128]{2,1,0:T(8,128)(2,1)S(1)}, u32[]{:S(2)}, u32[]{:S(2)}) collective-permute-start(bf16[4,128,128]{2,1,0:T(8,128)(2,1)S(1)} %get-tuple-element.57), channel_id=1, source_target_pairs={{0,35},{4,39},{8,43},{12,47},{16,51},{20,55},{24,59},{28,63},{1,0}... | collective-permute-start | bytes 393224 | tf_op jit(solution)/shard_map/ppermute | solution.py:24
  52.5 7.3 %collective-permute-start.12 = (bf16[4,128,128]{2,1,0:T(8,128)(2,1)S(1)}, bf16[4,128,128]{2,1,0:T(8,128)(2,1)S(1)}, u32[]{:S(2)}, u32[]{:S(2)}) collective-permute-start(bf16[4,128,128]{2,1,0:T(8,128)(2,1)S(1)} %get-tuple-element.58), channel_id=1, source_target_pairs={{0,1},{4,5},{8,9},{12,13},{16,17},{20,21},{24,25},{28,29},{1,2},{5... | collective-permute-start | bytes 393224 | tf_op jit(solution)/shard_map/ppermute | solution.py:24
  55.1 7.8 %collective-permute-start.6 = (bf16[4,128,128]{2,1,0:T(8,128)(2,1)S(1)}, bf16[4,128,128]{2,1,0:T(8,128)(2,1)S(1)}, u32[]{:S(2)}, u32[]{:S(2)}) collective-permute-start(bf16[4,128,128]{2,1,0:T(8,128)(2,1)S(1)} %get-tuple-element.46), channel_id=1, source_target_pairs={{0,34},{4,38},{8,42},{12,46},{16,50},{20,54},{24,58},{28,62},{1,35... | collective-permute-start | bytes 393224 | tf_op jit(solution)/shard_map/ppermute | solution.py:24
  59.7 8.5 %collective-permute-start.13 = (bf16[4,128,128]{2,1,0:T(8,128)(2,1)S(1)}, bf16[4,128,128]{2,1,0:T(8,128)(2,1)S(1)}, u32[]{:S(2)}, u32[]{:S(2)}) collective-permute-start(bf16[4,128,128]{2,1,0:T(8,128)(2,1)S(1)} %get-tuple-element.59), channel_id=1, source_target_pairs={{0,2},{4,6},{8,10},{12,14},{16,18},{20,22},{24,26},{28,30},{1,3},{... | collective-permute-start | bytes 393224 | tf_op jit(solution)/shard_map/ppermute | solution.py:24
  69.9 6.4 %collective-permute-start.16 = (bf16[2,17,16,128]{3,2,1,0:T(8,128)(2,1)S(1)}, bf16[2,17,16,128]{3,2,1,0:T(8,128)(2,1)S(1)}, u32[]{:S(2)}, u32[]{:S(2)}) collective-permute-start(bf16[2,17,16,128]{3,2,1,0:T(8,128)(2,1)S(1)} %get-tuple-element.65), channel_id=1, source_target_pairs={{0,8},{4,12},{8,0},{12,4},{16,24},{20,28},{24,16},{28,20},{1,9},{5... | collective-permute-start | bytes 417800 | tf_op jit(solution)/shard_map/ppermute | solution.py:24
  70.6 9.2 %collective-permute-start.17 = (bf16[2,17,16,128]{3,2,1,0:T(8,128)(2,1)S(1)}, bf16[2,17,16,128]{3,2,1,0:T(8,128)(2,1)S(1)}, u32[]{:S(2)}, u32[]{:S(2)}) collective-permute-start(bf16[2,17,16,128]{3,2,1,0:T(8,128)(2,1)S(1)} %get-tuple-element.66), channel_id=1, source_target_pairs={{0,16},{4,20},{8,24},{12,28},{16,0},{20,4},{24,8},{28,12},{1,17},{... | collective-permute-start | bytes 417800 | tf_op jit(solution)/shard_map/ppermute | solution.py:24
  73.0 8.1 %collective-permute-start.18 = (bf16[2,17,16,128]{3,2,1,0:T(8,128)(2,1)S(1)}, bf16[2,17,16,128]{3,2,1,0:T(8,128)(2,1)S(1)}, u32[]{:S(2)}, u32[]{:S(2)}) collective-permute-start(bf16[2,17,16,128]{3,2,1,0:T(8,128)(2,1)S(1)} %get-tuple-element.67), channel_id=1, source_target_pairs={{0,24},{4,28},{8,16},{12,20},{16,8},{20,12},{24,0},{28,4},{1,25},{... | collective-permute-start | bytes 417800 | tf_op jit(solution)/shard_map/ppermute | solution.py:24
  73.5 41.4 %collective-permute-start.30 = (bf16[2,256,512]{2,1,0:T(8,128)(2,1)S(1)}, bf16[2,256,512]{2,1,0:T(8,128)(2,1)S(1)}, u32[]{:S(2)}, u32[]{:S(2)}) collective-permute-start(bf16[2,256,512]{2,1,0:T(8,128)(2,1)S(1)} %get-tuple-element.74), channel_id=1, source_target_pairs={{0,35},{4,39},{8,43},{12,47},{16,51},{20,55},{24,59},{28,63},{1,0}... | collective-permute-start | bytes 1572872 | tf_op jit(solution)/shard_map/ppermute | solution.py:24
  81.4 9.0 %collective-permute-start.24 = (bf16[17,16,128]{2,1,0:T(8,128)(2,1)S(1)}, bf16[17,16,128]{2,1,0:T(8,128)(2,1)S(1)}, u32[]{:S(2)}, u32[]{:S(2)}) collective-permute-start(bf16[17,16,128]{2,1,0:T(8,128)(2,1)S(1)} %shard_map.55.total.refs_4_), channel_id=1, source_target_pairs={{0,192},{4,196},{8,200},{12,204},{16,208},{20,212},{24,216},{28,22... | collective-permute-start | bytes 208904 | tf_op jit(solution)/shard_map/ppermute | solution.py:24
  84.5 12.3 %collective-permute-start.22 = (bf16[17,16,128]{2,1,0:T(8,128)(2,1)S(1)}, bf16[17,16,128]{2,1,0:T(8,128)(2,1)S(1)}, u32[]{:S(2)}, u32[]{:S(2)}) collective-permute-start(bf16[17,16,128]{2,1,0:T(8,128)(2,1)S(1)} %shard_map.55.total.refs_4_), channel_id=1, source_target_pairs={{0,128},{4,132},{8,136},{12,140},{16,144},{20,148},{24,152},{28,15... | collective-permute-start | bytes 208904 | tf_op jit(solution)/shard_map/ppermute | solution.py:24
  85.1 12.3 %collective-permute-start.20 = (bf16[17,16,128]{2,1,0:T(8,128)(2,1)S(1)}, bf16[17,16,128]{2,1,0:T(8,128)(2,1)S(1)}, u32[]{:S(2)}, u32[]{:S(2)}) collective-permute-start(bf16[17,16,128]{2,1,0:T(8,128)(2,1)S(1)} %shard_map.55.total.refs_4_), channel_id=1, source_target_pairs={{0,64},{4,68},{8,72},{12,76},{16,80},{20,84},{24,88},{28,92},{1,65... | collective-permute-start | bytes 208904 | tf_op jit(solution)/shard_map/ppermute | solution.py:24
  85.6 8.2 %collective-permute-start.19 = (bf16[17,16,128]{2,1,0:T(8,128)(2,1)S(1)}, bf16[17,16,128]{2,1,0:T(8,128)(2,1)S(1)}, u32[]{:S(2)}, u32[]{:S(2)}) collective-permute-start(bf16[17,16,128]{2,1,0:T(8,128)(2,1)S(1)} %shard_map.55.total.refs_4_), channel_id=1, source_target_pairs={{0,32},{4,36},{8,40},{12,44},{16,48},{20,52},{24,56},{28,60},{1,33... | collective-permute-start | bytes 208904 | tf_op jit(solution)/shard_map/ppermute | solution.py:24
  90.4 35.7 %collective-permute-start.31 = (bf16[2,256,512]{2,1,0:T(8,128)(2,1)S(1)}, bf16[2,256,512]{2,1,0:T(8,128)(2,1)S(1)}, u32[]{:S(2)}, u32[]{:S(2)}) collective-permute-start(bf16[2,256,512]{2,1,0:T(8,128)(2,1)S(1)} %shard_map.61), channel_id=1, source_target_pairs={{0,1},{4,5},{8,9},{12,13},{16,17},{20,21},{24,25},{28,29},{1,2},{5... | collective-permute-start | bytes 1572872 | tf_op jit(solution)/shard_map/ppermute | solution.py:24
  93.8 5.5 %collective-permute-start.25 = (bf16[17,16,128]{2,1,0:T(8,128)(2,1)S(1)}, bf16[17,16,128]{2,1,0:T(8,128)(2,1)S(1)}, u32[]{:S(2)}, u32[]{:S(2)}) collective-permute-start(bf16[17,16,128]{2,1,0:T(8,128)(2,1)S(1)} %collective-permute-done.19.refs_5_), channel_id=1, source_target_pairs={{0,192},{4,196},{8,200},{12,204},{16,208},{20,212},{24,216},{28,22... | collective-permute-start | bytes 208904 | tf_op jit(solution)/shard_map/ppermute | solution.py:24
  96.8 5.8 %collective-permute-start.23 = (bf16[17,16,128]{2,1,0:T(8,128)(2,1)S(1)}, bf16[17,16,128]{2,1,0:T(8,128)(2,1)S(1)}, u32[]{:S(2)}, u32[]{:S(2)}) collective-permute-start(bf16[17,16,128]{2,1,0:T(8,128)(2,1)S(1)} %collective-permute-done.19.refs_5_), channel_id=1, source_target_pairs={{0,128},{4,132},{8,136},{12,140},{16,144},{20,148},{24,152},{28,15... | collective-permute-start | bytes 208904 | tf_op jit(solution)/shard_map/ppermute | solution.py:24
  97.5 5.2 %collective-permute-start.21 = (bf16[17,16,128]{2,1,0:T(8,128)(2,1)S(1)}, bf16[17,16,128]{2,1,0:T(8,128)(2,1)S(1)}, u32[]{:S(2)}, u32[]{:S(2)}) collective-permute-start(bf16[17,16,128]{2,1,0:T(8,128)(2,1)S(1)} %collective-permute-done.19.refs_5_), channel_id=1, source_target_pairs={{0,64},{4,68},{8,72},{12,76},{16,80},{20,84},{24,88},{28,92},{1,65... | collective-permute-start | bytes 208904 | tf_op jit(solution)/shard_map/ppermute | solution.py:24
  103.1 5.8 %collective-permute-start.26 = (bf16[2,16,16,128]{3,2,1,0:T(8,128)(2,1)S(1)}, bf16[2,16,16,128]{3,2,1,0:T(8,128)(2,1)S(1)}, u32[]{:S(2)}, u32[]{:S(2)}) collective-permute-start(bf16[2,16,16,128]{3,2,1,0:T(8,128)(2,1)S(1)} %get-tuple-element.69), channel_id=1, source_target_pairs={{0,8},{4,12},{8,0},{12,4},{16,24},{20,28},{24,16},{28,20},{1,9},{5... | collective-permute-start | bytes 393224 | tf_op jit(solution)/shard_map/ppermute | solution.py:24
  105.9 6.5 %collective-permute-start.27 = (bf16[2,16,16,128]{3,2,1,0:T(8,128)(2,1)S(1)}, bf16[2,16,16,128]{3,2,1,0:T(8,128)(2,1)S(1)}, u32[]{:S(2)}, u32[]{:S(2)}) collective-permute-start(bf16[2,16,16,128]{3,2,1,0:T(8,128)(2,1)S(1)} %get-tuple-element.70), channel_id=1, source_target_pairs={{0,16},{4,20},{8,24},{12,28},{16,0},{20,4},{24,8},{28,12},{1,17},{... | collective-permute-start | bytes 393224 | tf_op jit(solution)/shard_map/ppermute | solution.py:24
  105.9 6.5 %collective-permute-start.28 = (bf16[2,16,16,128]{3,2,1,0:T(8,128)(2,1)S(1)}, bf16[2,16,16,128]{3,2,1,0:T(8,128)(2,1)S(1)}, u32[]{:S(2)}, u32[]{:S(2)}) collective-permute-start(bf16[2,16,16,128]{3,2,1,0:T(8,128)(2,1)S(1)} %get-tuple-element.71), channel_id=1, source_target_pairs={{0,24},{4,28},{8,16},{12,20},{16,8},{20,12},{24,0},{28,4},{1,25},{... | collective-permute-start | bytes 393224 | tf_op jit(solution)/shard_map/ppermute | solution.py:24
  108.9 17.2 %collective-permute-start.32 = (bf16[2,128,512]{2,1,0:T(8,128)(2,1)S(1)}, bf16[2,128,512]{2,1,0:T(8,128)(2,1)S(1)}, u32[]{:S(2)}, u32[]{:S(2)}) collective-permute-start(bf16[2,128,512]{2,1,0:T(8,128)(2,1)S(1)} %get-tuple-element.81.refs_0_), channel_id=1, source_target_pairs={{0,34},{4,38},{8,42},{12,46},{16,50},{20,54},{24,58},{28,62},{1,35... | collective-permute-start | bytes 786440 | tf_op jit(solution)/shard_map/ppermute | solution.py:24
  112.4 13.6 %collective-permute-start.33 = (bf16[2,128,512]{2,1,0:T(8,128)(2,1)S(1)}, bf16[2,128,512]{2,1,0:T(8,128)(2,1)S(1)}, u32[]{:S(2)}, u32[]{:S(2)}) collective-permute-start(bf16[2,128,512]{2,1,0:T(8,128)(2,1)S(1)} %get-tuple-element.82), channel_id=1, source_target_pairs={{0,2},{4,6},{8,10},{12,14},{16,18},{20,22},{24,26},{28,30},{1,3},{... | collective-permute-start | bytes 786440 | tf_op jit(solution)/shard_map/ppermute | solution.py:24
  112.4 13.6 %collective-permute-start.29 = (bf16[16,64,128]{2,1,0:T(8,128)(2,1)S(1)}, bf16[16,64,128]{2,1,0:T(8,128)(2,1)S(1)}, u32[]{:S(2)}, u32[]{:S(2)}) collective-permute-start(bf16[16,64,128]{2,1,0:T(8,128)(2,1)S(1)} %shard_map.58), channel_id=1, source_target_pairs={{0,4},{4,0},{8,12},{12,8},{16,20},{20,16},{24,28},{28,24},{1,5},{5... | collective-permute-start | bytes 786440 | tf_op jit(solution)/shard_map/ppermute | solution.py:24
  (4 other events, 39.6 us)
